TPU v7x, 128 devices: a whole 4x4x4 slice. The times are simulated.
128 devices in a mesh: lat: 8 (over x, core), lon: 16 (over y, z).
Axes of the slice: x: 4, y: 4, z: 4, core: 2. Of those that a mesh axis runs over, the one named last changes fastest.
Arguments:
- fields: float32 [4, 90, 128, 2048], P(None, None, 'lat', 'lon'), may hold values from -6 to 6
- courant_lon: float32 [90, 128, 2048], P(None, 'lat', 'lon'), may hold values from -0.3 to 0.3
- courant_lat: float32 [90, 128, 2048], P(None, 'lat', 'lon'), may hold values from -0.3 to 0.3
- diffusion: float32 [90, 128, 2048], P(None, 'lat', 'lon'), may hold values from 0.1 to 0.24
- tend_cot: bfloat16 [4, 90, 128, 2048], P(None, None, 'lat', 'lon'), may hold values from -6 to 6
- col_list: int32 [8, 16, 2048], P('lat', 'lon'), may hold values from 0 to 2047, as said below
- block_count: int32 [8, 16, 16], P('lat', 'lon'), may hold values from 1 to 128, as said below
- block_dest: int32 [8, 16, 16], P('lat', 'lon'), may hold values from 0 to 15, each once within a row
- w_in: bfloat16 [16, 360, 512], P('lon', None, 'lat'), may hold values from -0.3125 to 0.3125
- w_mid: bfloat16 [16, 512, 512], P('lon', None, 'lat'), may hold values from -0.25 to 0.25
- w_out: bfloat16 [16, 360, 512], P('lon', None, 'lat'), may hold values from -0.25 to 0.25
Outputs:
- new_fields: float32 [4, 90, 128, 2048], P(None, None, 'lat', 'lon')
- adjoint: bfloat16 [4, 90, 128, 2048], P(None, None, 'lat', 'lon')
- grad_in: float32 [16, 360, 512], P('lon', None, 'lat')
- grad_mid: float32 [16, 512, 512], P('lon', None, 'lat')
- grad_out: float32 [16, 360, 512], P('lon', None, 'lat')
Inputs may be any that keep to these rules, and one draw needn't show every extreme that they name: `col_list`: within one tile's list no local column appears twice. `block_count`: in each tile one block has all 128 slots live. `block_dest`: each tile's row names every expert exactly once.
All inputs are finite; a program needn't handle non-finite values.
Results may differ from a plain program's by a relative error of at most 0.0074.
Values may be sent and summed in bfloat16 or wider, within the bound.
No kernel may reach another device: no remote copies, remote signals or barrier semaphores. Data moves between devices by JAX's collectives and lax.ppermute only.
A program may use at most 320 MiB of HBM per device.

v0:
```python
import jax
import jax.numpy as jnp
from jax import lax
from jax.sharding import PartitionSpec as P

STEPS = 4


def extended(array, sides, width):
    for axis, dim in sides:
        size, length = (lax.axis_size(axis), array.shape[dim])
        up = [(i, (i + 1) % size) for i in range(size)]
        down = [(j, i) for i, j in up]
        last = lax.slice_in_dim(array, length - width, length, axis=dim)
        first = lax.slice_in_dim(array, 0, width, axis=dim)
        before = lax.ppermute(last, axis, up)
        after = lax.ppermute(first, axis, down)
        array = jnp.concatenate([before, array, after], axis=dim)
    return array


def dsilu(value):
    sig = jax.nn.sigmoid(value)
    return sig * (1.0 + value * (1.0 - sig))


def physics(x, g, weights):
    w_first, w_second, w_third = weights
    lead = "e"
    xf = x.astype(jnp.float32)
    scale = lax.rsqrt(jnp.mean(xf * xf, axis=0, keepdims=True) + 1e-06)
    xn = (xf * scale).astype(jnp.bfloat16)
    a_one = jnp.einsum(lead + "fh,fbc->hbc", w_first, xn, preferred_element_type=jnp.float32)
    h_one = jax.nn.silu(a_one).astype(jnp.bfloat16)
    a_two = jnp.einsum(lead + "gh,gbc->hbc", w_second, h_one, preferred_element_type=jnp.float32)
    h_two = jax.nn.silu(a_two).astype(jnp.bfloat16)
    tend = jnp.einsum(
        lead + "fh,hbc->fbc", w_third, h_two, preferred_element_type=jnp.float32
    ).astype(jnp.bfloat16)
    back_two = jnp.einsum(lead + "fh,fbc->hbc", w_third, g, preferred_element_type=jnp.float32)
    d_two = (back_two * dsilu(a_two)).astype(jnp.bfloat16)
    back_one = jnp.einsum(lead + "gh,hbc->gbc", w_second, d_two, preferred_element_type=jnp.float32)
    d_one = (back_one * dsilu(a_one)).astype(jnp.bfloat16)
    d_norm = jnp.einsum(lead + "fh,hbc->fbc", w_first, d_one, preferred_element_type=jnp.float32)
    adj = (
        scale * d_norm - xf * (scale * scale * scale) * jnp.mean(xf * d_norm, axis=0, keepdims=True)
    ).astype(jnp.bfloat16)
    out_form = "fh"
    mid_form = "gh"
    grad_first = jnp.einsum("fbc,hbc->" + out_form, xn, d_one, preferred_element_type=jnp.float32)
    grad_second = jnp.einsum(
        "gbc,hbc->" + mid_form, h_one, d_two, preferred_element_type=jnp.float32
    )
    grad_third = jnp.einsum("fbc,hbc->" + out_form, g, h_two, preferred_element_type=jnp.float32)
    return (tend, adj, (grad_first[None], grad_second[None], grad_third[None]))


def update(state, c_lon, c_lat, c_dif, east, west, north, south):
    return (
        state
        - 0.5 * c_lon * (east - west)
        - 0.5 * c_lat * (north - south)
        + c_dif * (east + west + north + south - 4.0 * state)
    )


def shards(
    fields,
    courant_lon,
    courant_lat,
    diffusion,
    tend_cot,
    col_list,
    block_count,
    block_dest,
    w_in,
    w_mid,
    w_out,
):
    nfield, levels, rows, columns = fields.shape
    feat = nfield * levels
    ncol = rows * columns
    total_rows = rows * lax.axis_size("lat")
    first_row = lax.axis_index("lat") * rows
    nblock = block_dest.shape[-1]
    block_len = col_list.shape[-1] // nblock
    dest = block_dest.reshape(nblock)
    counts = block_count.reshape(nblock)
    order = jnp.zeros((nblock,), jnp.int32).at[dest].set(jnp.arange(nblock, dtype=jnp.int32))
    slots = col_list.reshape(nblock, block_len)[order]
    live = jnp.arange(block_len, dtype=jnp.int32)[None, :] < counts[order][:, None]
    col_data = fields.astype(jnp.bfloat16).reshape(feat, ncol)
    cot_data = tend_cot.reshape(feat, ncol)
    picked_x = col_data[:, slots]
    picked_g = cot_data[:, slots]
    send_x = jnp.where(live[None], picked_x, jnp.zeros_like(picked_x))
    send_g = jnp.where(live[None], picked_g, jnp.zeros_like(picked_g))
    weights = (
        lax.all_gather(w_in, "lat", axis=2, tiled=True),
        lax.all_gather(w_mid, "lat", axis=2, tiled=True),
        lax.all_gather(w_out, "lat", axis=2, tiled=True),
    )
    recv_x, recv_g = (
        lax.all_to_all(send_x, "lon", split_axis=1, concat_axis=1, tiled=True),
        lax.all_to_all(send_g, "lon", split_axis=1, concat_axis=1, tiled=True),
    )
    tend, adj, grads = physics(recv_x, recv_g, weights)
    back_tend, back_adj = (
        lax.all_to_all(tend, "lon", split_axis=1, concat_axis=1, tiled=True),
        lax.all_to_all(adj, "lon", split_axis=1, concat_axis=1, tiled=True),
    )
    state = fields
    lane = jnp.arange(columns, dtype=jnp.int32)[None, :]
    row_index = jnp.arange(rows, dtype=jnp.int32)[:, None]
    top_inside = (first_row + rows < total_rows).astype(jnp.float32)
    bottom_inside = (first_row > 0).astype(jnp.float32)
    for step in range(STEPS):
        padded = extended(state.astype(jnp.bfloat16), (("lat", 2), ("lon", 3)), 1).astype(
            state.dtype
        )
        east_rim = padded[:, :, 1:-1, -1:]
        west_rim = padded[:, :, 1:-1, :1]
        north_rim = padded[:, :, -1:, 1:-1] * top_inside
        south_rim = padded[:, :, :1, 1:-1] * bottom_inside
        east = jnp.where(lane == columns - 1, east_rim, jnp.roll(state, -1, axis=3))
        west = jnp.where(lane == 0, west_rim, jnp.roll(state, 1, axis=3))
        north = jnp.where(row_index == rows - 1, north_rim, jnp.roll(state, -1, axis=2))
        south = jnp.where(row_index == 0, south_rim, jnp.roll(state, 1, axis=2))
        state = update(state, courant_lon, courant_lat, diffusion, east, west, north, south)
    grad_in, grad_mid, grad_out = (
        lax.psum_scatter(grads[0], "lat", scatter_dimension=2, tiled=True),
        lax.psum_scatter(grads[1], "lat", scatter_dimension=2, tiled=True),
        lax.psum_scatter(grads[2], "lat", scatter_dimension=2, tiled=True),
    )
    flat = slots.reshape(-1)
    tend_cols = jnp.zeros((feat, ncol), jnp.bfloat16).at[:, flat].set(back_tend.reshape(feat, -1))
    adj_cols = jnp.zeros((feat, ncol), jnp.bfloat16).at[:, flat].set(back_adj.reshape(feat, -1))
    new_fields = state + tend_cols.astype(jnp.float32).reshape(fields.shape)
    adjoint = adj_cols.reshape(fields.shape)
    return (new_fields, adjoint, grad_in, grad_mid, grad_out)


def solution(mesh):
    return jax.shard_map(
        shards,
        mesh=mesh,
        in_specs=(
            P(None, None, "lat", "lon"),
            P(None, "lat", "lon"),
            P(None, "lat", "lon"),
            P(None, "lat", "lon"),
            P(None, None, "lat", "lon"),
            P("lat", "lon", None),
            P("lat", "lon", None),
            P("lat", "lon", None),
            P("lon", None, "lat"),
            P("lon", None, "lat"),
            P("lon", None, "lat"),
        ),
        out_specs=(
            P(None, None, "lat", "lon"),
            P(None, None, "lat", "lon"),
            P("lon", None, "lat"),
            P("lon", None, "lat"),
            P("lon", None, "lat"),
        ),
        check_vma=False,
    )
```

profile of v0, /device:TPU:8, one launch (start us, length us, event | category | flops | bytes accessed | tf_op | source)
XLA Modules:
  0.0 622.2 jit_solution(11210584672356937061)
XLA Ops:
  20.7 7.5 %gather_fusion.2 = bf16[2048,360]{1,0:T(8,128)(2,1)S(1)} fusion(bf16[360,2048]{0,1:T(8,128)(2,1)S(1)} %reshape.252, s32[2048]{0:T(1024)S(1)} %fusion.49), kind=kCustom, calls=%fused_computation.2 | custom fusion | bytes 2957312 | tf_op jit(solution)/shard_map/gather | solution.py:94
  31.0 7.5 %gather_fusion.3 = bf16[2048,360]{1,0:T(8,128)(2,1)S(1)} fusion(bf16[360,2048]{0,1:T(8,128)(2,1)S(1)} %copy.261, s32[2048]{0:T(1024)S(1)} %fusion.49), kind=kCustom, calls=%fused_computation.3 | custom fusion | bytes 2957312 | tf_op jit(solution)/shard_map/gather | solution.py:95
  44.2 8.7 %all-to-all-start = ((bf16[360,16,128]{2,0,1:T(8,128)(2,1)}), bf16[360,16,128]{2,0,1:T(8,128)(2,1)}, u32[]{:S(2)}, u32[]{:S(2)}) async-start(bf16[360,16,128]{2,0,1:T(8,128)(2,1)} %get-tuple-element.106), calls=%async_computation | async-start | bytes 2949120 | tf_op jit(solution)/shard_map/all_to_all | solution.py:104
  68.1 13.0 %all_gather.9 = bf16[1,360,512]{1,2,0:T(8,128)(2,1)S(1)} all-gather(bf16[1,360,64]{1,2,0:T(8,128)(2,1)S(1)} %copy-done.60), channel_id=1, replica_groups=mesh['lat'=8,'lon'=16] {'lat'}, dimensions={2}, use_global_device_ids=true | all-gather | bytes 414720 | tf_op jit(solution)/shard_map/all_gather | solution.py:99
  81.0 14.2 %all_gather.10 = bf16[1,512,512]{1,2,0:T(8,128)(2,1)} all-gather(bf16[1,512,64]{1,2,0:T(8,128)(2,1)S(1)} %copy-done.59), channel_id=1, replica_groups=mesh['lat'=8,'lon'=16] {'lat'}, dimensions={2}, use_global_device_ids=true | all-gather | bytes 589824 | tf_op jit(solution)/shard_map/all_gather | solution.py:100
  95.2 14.5 %all_gather.11 = bf16[1,360,512]{1,2,0:T(8,128)(2,1)} all-gather(bf16[1,360,64]{1,2,0:T(8,128)(2,1)S(1)} %copy-done.61), channel_id=1, replica_groups=mesh['lat'=8,'lon'=16] {'lat'}, dimensions={2}, use_global_device_ids=true | all-gather | bytes 414720 | tf_op jit(solution)/shard_map/all_gather | solution.py:101
  126.0 5.6 copy.314
  156.7 7.1 %maximum_convert_fusion = f32[4,90,18,130]{3,0,2,1:T(4,128)S(1)} fusion(bf16[4,90,18,1]{3,0,2,1:T(4,128)(2,1)} %copy.210, bf16[4,90,1,128]{3,0,2,1:T(4,128)(2,1)} %copy-done.41, bf16[4,90,16,128]{3,0,2,1:T(4,128)(2,1)} %copy-done.8, bf16[4,90,1,128]{3,0,2,1:T(4,128)(2,1)S(1)} %collective-permute-done, bf16[4,90,18,1]{3,0,2,1:T(4,128)(2,1)} %copy.209), kind=kLoop, calls=%fused_computation.33 | loop fusion | flops 8424000 | bytes 5054400 | tf_op jit(solution)/shard_map/convert_element_type | solution.py:118
  168.7 10.6 %copy.285 = f32[4,90,16,1]{0,2,1,3:T(8,128)} copy(f32[4,90,16,1]{3,0,2,1:T(4,128)} %get-tuple-element.45) | data formatting | bytes 46080 | tf_op jit(solution)/shard_map/jit(_where)/broadcast_in_dim | solution.py:125
  179.2 10.6 %copy.286 = f32[4,90,16,1]{0,2,1,3:T(8,128)} copy(f32[4,90,16,1]{3,0,2,1:T(4,128)} %get-tuple-element.46) | data formatting | bytes 46080 | tf_op jit(solution)/shard_map/jit(_where)/broadcast_in_dim | solution.py:126
  192.4 12.2 %fusion.57 = (bf16[4,90,16,128]{3,0,2,1:T(4,128)(2,1)S(1)}, f32[4,90,16,128]{3,0,2,1:T(4,128)S(1)}) fusion(f32[90,16,128]{2,1,0:T(8,128)S(1)} %copy-done.32, f32[4,90,15,128]{3,0,2,1:T(4,128)} %copy.310, f32[4,90,1,128]{3,0,2,1:T(4,128)S(1)} %copy-done.54, f32[4,90,128]{2,0,1:T(4,128)S(1)} %get-tuple-element.54, pred[16]{0:T(512)(128)(4,1)S(1)} %get-tuple-element.113, ...), kind=kLoop, calls=%fused_computation.135 | loop fusion | flops 16220160 | bytes 21796128 | tf_op jit(solution)/shard_map/convert_element_type | solution.py:118
  240.1 6.8 %maximum_convert_fusion.1 = f32[4,90,18,130]{3,0,2,1:T(4,128)S(1)} fusion(bf16[4,90,18,1]{3,0,2,1:T(4,128)(2,1)} %copy.228, bf16[4,90,1,128]{3,0,2,1:T(4,128)(2,1)} %copy-done.45, bf16[4,90,16,128]{3,0,2,1:T(4,128)(2,1)S(1)} %copy-done.14, bf16[4,90,1,128]{3,0,2,1:T(4,128)(2,1)} %copy-done.43, bf16[4,90,18,1]{3,0,2,1:T(4,128)(2,1)S(1)} %copy.227), kind=kLoop, calls=%fused_computation.34 | loop fusion | flops 8424000 | bytes 5054400 | tf_op jit(solution)/shard_map/convert_element_type | solution.py:118
  251.7 10.6 %copy.287 = f32[4,90,16,1]{0,2,1,3:T(8,128)} copy(f32[4,90,16,1]{3,0,2,1:T(4,128)} %get-tuple-element.43) | data formatting | bytes 46080 | tf_op jit(solution)/shard_map/jit(_where)/broadcast_in_dim | solution.py:125
  262.3 10.6 %copy.288 = f32[4,90,16,1]{0,2,1,3:T(8,128)} copy(f32[4,90,16,1]{3,0,2,1:T(4,128)} %get-tuple-element.44) | data formatting | bytes 46080 | tf_op jit(solution)/shard_map/jit(_where)/broadcast_in_dim | solution.py:126
  275.4 12.8 %fusion.56 = (bf16[4,90,16,128]{3,0,2,1:T(4,128)(2,1)S(1)}, f32[4,90,16,128]{3,0,2,1:T(4,128)S(1)}) fusion(f32[4,90,16,128]{3,0,2,1:T(4,128)S(1)} %copy-done.7, f32[90,16,128]{2,1,0:T(8,128)S(1)} %copy-done.33, f32[4,90,15,128]{3,0,2,1:T(4,128)} %get-tuple-element.76, f32[4,90,1,128]{3,0,2,1:T(4,128)} %get-tuple-element.78, ...), kind=kLoop, calls=%fused_computation.134 | loop fusion | flops 16220160 | bytes 21796128 | tf_op jit(solution)/shard_map/convert_element_type | solution.py:118
  323.3 6.8 %maximum_convert_fusion.2 = f32[4,90,18,130]{3,0,2,1:T(4,128)S(1)} fusion(bf16[4,90,18,1]{3,0,2,1:T(4,128)(2,1)} %copy.236, bf16[4,90,1,128]{3,0,2,1:T(4,128)(2,1)} %copy-done.46, bf16[4,90,16,128]{3,0,2,1:T(4,128)(2,1)S(1)} %copy-done.12, bf16[4,90,1,128]{3,0,2,1:T(4,128)(2,1)} %copy-done.44, bf16[4,90,18,1]{3,0,2,1:T(4,128)(2,1)S(1)} %copy.235), kind=kLoop, calls=%fused_computation.35 | loop fusion | flops 8424000 | bytes 5054400 | tf_op jit(solution)/shard_map/convert_element_type | solution.py:118
  334.9 10.6 %copy.289 = f32[4,90,16,1]{0,2,1,3:T(8,128)} copy(f32[4,90,16,1]{3,0,2,1:T(4,128)} %get-tuple-element.41) | data formatting | bytes 46080 | tf_op jit(solution)/shard_map/jit(_where)/broadcast_in_dim | solution.py:125
  345.5 10.6 %copy.290 = f32[4,90,16,1]{0,2,1,3:T(8,128)} copy(f32[4,90,16,1]{3,0,2,1:T(4,128)} %get-tuple-element.42) | data formatting | bytes 46080 | tf_op jit(solution)/shard_map/jit(_where)/broadcast_in_dim | solution.py:126
  358.6 12.6 %fusion.55 = (bf16[4,90,16,128]{3,0,2,1:T(4,128)(2,1)S(1)}, f32[4,90,16,128]{3,0,2,1:T(4,128)S(1)}) fusion(f32[4,90,16,128]{3,0,2,1:T(4,128)S(1)} %copy-done.5, f32[90,16,128]{2,1,0:T(8,128)S(1)} %copy-done.34, f32[4,90,15,128]{3,0,2,1:T(4,128)} %get-tuple-element.68, f32[4,90,1,128]{3,0,2,1:T(4,128)} %get-tuple-element.70, ...), kind=kLoop, calls=%fused_computation.133 | loop fusion | flops 16220160 | bytes 21796128 | tf_op jit(solution)/shard_map/convert_element_type | solution.py:118
  406.1 8.7 %maximum_convert_fusion.3 = f32[4,90,18,130]{3,0,2,1:T(4,128)} fusion(bf16[4,90,18,1]{3,0,2,1:T(4,128)(2,1)} %copy.244, bf16[4,90,1,128]{3,0,2,1:T(4,128)(2,1)} %copy-done.42, bf16[4,90,16,128]{3,0,2,1:T(4,128)(2,1)} %copy-done.10, bf16[4,90,1,128]{3,0,2,1:T(4,128)(2,1)S(1)} %collective-permute-done.12, bf16[4,90,18,1]{3,0,2,1:T(4,128)(2,1)} %copy.243), kind=kLoop, calls=%fused_computation.36 | loop fusion | flops 8424000 | bytes 5054400 | tf_op jit(solution)/shard_map/convert_element_type | solution.py:118
  414.9 10.7 %all-to-all-start.2 = ((bf16[360,16,128]{2,0,1:T(8,128)(2,1)}), bf16[360,16,128]{2,0,1:T(8,128)(2,1)}, u32[]{:S(2)}, u32[]{:S(2)}) async-start(bf16[360,16,128]{2,0,1:T(8,128)(2,1)} %get-tuple-element.105), calls=%async_computation.2 | async-start | bytes 2949120 | tf_op jit(solution)/shard_map/all_to_all | solution.py:105
  436.0 6.5 %all-to-all-done.2 = bf16[360,16,128]{2,0,1:T(8,128)(2,1)} async-done(((bf16[360,16,128]{2,0,1:T(8,128)(2,1)}), bf16[360,16,128]{2,0,1:T(8,128)(2,1)}, u32[]{:S(2)}, u32[]{:S(2)}) %all-to-all-start.2) | async-done | bytes 1474592 | tf_op jit(solution)/shard_map/all_to_all | solution.py:105
  442.5 5.2 fusion.1
  472.3 6.5 %all-to-all-start.1 = ((bf16[360,16,128]{2,0,1:T(8,128)(2,1)}), bf16[360,16,128]{2,0,1:T(8,128)(2,1)}, u32[]{:S(2)}, u32[]{:S(2)}) async-start(bf16[360,16,128]{2,0,1:T(8,128)(2,1)} %fusion.20), calls=%async_computation.1 | async-start | bytes 2949120 | tf_op jit(solution)/shard_map/all_to_all | solution.py:109
  479.5 7.0 %fusion.58 = (f32[4,90,16,1]{3,0,2,1:T(4,128)}, f32[4,90,16,1]{3,0,2,1:T(4,128)}) fusion(f32[4,90,18,130]{3,0,2,1:T(4,128)} %maximum_convert_fusion.3), kind=kLoop, calls=%fused_computation.136 | loop fusion | bytes 92160 | tf_op jit(solution)/shard_map/slice | solution.py:121
  486.5 10.6 %copy.291 = f32[4,90,16,1]{0,2,1,3:T(8,128)} copy(f32[4,90,16,1]{3,0,2,1:T(4,128)} %get-tuple-element.39) | data formatting | bytes 46080 | tf_op jit(solution)/shard_map/jit(_where)/broadcast_in_dim | solution.py:125
  497.1 10.6 %copy.292 = f32[4,90,16,1]{0,2,1,3:T(8,128)} copy(f32[4,90,16,1]{3,0,2,1:T(4,128)} %get-tuple-element.40) | data formatting | bytes 46080 | tf_op jit(solution)/shard_map/jit(_where)/broadcast_in_dim | solution.py:126
  515.5 35.7 %all-reduce.6.cloned.1.call-done = (f32[1,360,512]{1,0,2:T(1,128)}, f32[1,512,512]{1,0,2:T(1,128)}, f32[1,360,512]{1,0,2:T(1,128)}) async-done(((f32[1,360,512]{1,0,2:T(1,128)}, f32[1,512,512]{1,0,2:T(1,128)}, f32[1,360,512]{1,0,2:T(1,128)}), (f32[1,360,512]{1,0,2:T(1,128)}, f32[1,512,512]{1,0,2:T(1,128)}, f32[1,360,512]{1,0,2:T(1,128)})) %all-reduce.6.cloned.1.call-update) | async-done | bytes 2523152
  555.1 7.4 %all-to-all-start.3 = ((bf16[360,16,128]{2,0,1:T(8,128)(2,1)}), bf16[360,16,128]{2,0,1:T(8,128)(2,1)}, u32[]{:S(2)}, u32[]{:S(2)}) async-start(bf16[360,16,128]{2,0,1:T(8,128)(2,1)} %fusion.18), calls=%async_computation.3 | async-start | bytes 2949120 | tf_op jit(solution)/shard_map/all_to_all | solution.py:110
  567.7 11.3 %scatter_custom_fusion.1 = bf16[360,2048]{0,1:T(8,128)(2,1)} fusion(s32[2048]{0:T(1024)} %bitcast.207, bf16[2048,360]{1,0:T(8,128)(2,1)} %copy.258, bf16[]{:T(256)} %constant.6.clone.1), kind=kCustom, calls=%fused_computation.83 | custom fusion | bytes 1475072 | tf_op jit(solution)/shard_map/scatter | solution.py:136
  586.3 12.2 %copy_add_fusion = f32[4,90,16,128]{3,0,2,1:T(4,128)S(1)} fusion(f32[4,90,16,128]{3,2,1,0:T(8,128)S(1)} %bitcast.191, f32[4,90,16,128]{3,0,2,1:T(4,128)S(1)} %get-tuple-element.34, f32[4,90,15,128]{3,0,2,1:T(4,128)} %get-tuple-element.60, f32[4,90,1,128]{3,0,2,1:T(4,128)} %get-tuple-element.62, f32[4,90,1,128]{3,0,2,1:T(4,128)S(1)} %copy-done.49, ...), kind=kLoop, calls=%fused_computation.60 | loop fusion | flops 16220160 | bytes 23270688 | tf_op jit(solution)/shard_map/add | solution.py:138
  602.9 10.0 %scatter_custom_fusion.2 = bf16[360,2048]{0,1:T(8,128)(2,1)S(1)} fusion(s32[2048]{0:T(1024)} %bitcast.208, bf16[2048,360]{1,0:T(8,128)(2,1)S(1)} %copy.266, bf16[]{:T(256)} %constant.6.clone.1), kind=kCustom, calls=%fused_computation.81 | custom fusion | bytes 1475072 | tf_op jit(solution)/shard_map/scatter | solution.py:137
  (297 shorter events, 271.5 us)
Async XLA Ops:
  44.2 370.7 %all-to-all-start = ((bf16[360,16,128]{2,0,1:T(8,128)(2,1)}), bf16[360,16,128]{2,0,1:T(8,128)(2,1)}, u32[]{:S(2)}, u32[]{:S(2)}) async-start(bf16[360,16,128]{2,0,1:T(8,128)(2,1)} %get-tuple-element.106), calls=%async_computation | async-start | bytes 2949120 | tf_op jit(solution)/shard_map/all_to_all | solution.py:104
  53.9 57.7 %collective-permute-start = (bf16[4,90,1,128]{3,0,2,1:T(4,128)(2,1)S(1)}, bf16[4,90,1,128]{3,0,2,1:T(4,128)(2,1)S(1)}, u32[]{:S(2)}, u32[]{:S(2)}) collective-permute-start(bf16[4,90,1,128]{3,0,2,1:T(4,128)(2,1)S(1)} %get-tuple-element.101), channel_id=1, source_target_pairs={{0,16},{16,32},{32,48},{48,64},{64,80},{80,96},{96,112},{112,0},{1... | collective-permute-start | bytes 276488 | tf_op jit(solution)/shard_map/ppermute | solution.py:16
  53.9 57.7 %collective-permute-start.1 = (bf16[4,90,1,128]{3,0,2,1:T(4,128)(2,1)S(1)}, bf16[4,90,1,128]{3,0,2,1:T(4,128)(2,1)S(1)}, u32[]{:S(2)}, u32[]{:S(2)}) collective-permute-start(bf16[4,90,1,128]{3,0,2,1:T(4,128)(2,1)S(1)} %get-tuple-element.102), channel_id=1, source_target_pairs={{16,0},{32,16},{48,32},{64,48},{80,64},{96,80},{112,96},{0,112},{1... | collective-permute-start | bytes 276488 | tf_op jit(solution)/shard_map/ppermute | solution.py:17
  63.9 17.1 %copy-start.59 = (bf16[1,512,64]{1,2,0:T(8,128)(2,1)S(1)}, bf16[1,512,64]{1,2,0:T(8,128)(2,1)}, u32[]{:S(2)}) copy-start(bf16[1,512,64]{1,2,0:T(8,128)(2,1)} %param.20) | copy-start | bytes 196612
  63.9 31.3 %copy-start.61 = (bf16[1,360,64]{1,2,0:T(8,128)(2,1)S(1)}, bf16[1,360,64]{1,2,0:T(8,128)(2,1)}, u32[]{:S(2)}) copy-start(bf16[1,360,64]{1,2,0:T(8,128)(2,1)} %param.21) | copy-start | bytes 138244
  63.9 46.4 %copy-start.50 = (f32[90,16,128]{2,1,0:T(8,128)S(1)}, f32[90,16,128]{2,1,0:T(8,128)}, u32[]{:S(2)}) copy-start(f32[90,16,128]{2,1,0:T(8,128)} %param.13) | copy-start | bytes 2211844
  63.9 46.4 %copy-start.51 = (f32[90,16,128]{2,1,0:T(8,128)S(1)}, f32[90,16,128]{2,1,0:T(8,128)}, u32[]{:S(2)}) copy-start(f32[90,16,128]{2,1,0:T(8,128)} %param.12) | copy-start | bytes 2211844
  67.0 44.6 %copy-start.9 = (bf16[4,90,16,128]{3,0,2,1:T(4,128)(2,1)S(1)}, bf16[4,90,16,128]{3,0,2,1:T(4,128)(2,1)}, u32[]{:S(2)}) copy-start(bf16[4,90,16,128]{3,0,2,1:T(4,128)(2,1)} %copy-done.8) | copy-start | bytes 4423684
  111.6 245.8 %copy-start.62 = (pred[16]{0:T(512)(128)(4,1)}, pred[16]{0:T(512)(128)(4,1)S(1)}, u32[]{:S(2)}) copy-start(pred[16]{0:T(512)(128)(4,1)S(1)} %get-tuple-element.113) | copy-start | bytes 52
  111.6 245.8 %copy-start.64 = (pred[16]{0:T(512)(128)(4,1)}, pred[16]{0:T(512)(128)(4,1)S(1)}, u32[]{:S(2)}) copy-start(pred[16]{0:T(512)(128)(4,1)S(1)} %get-tuple-element.114) | copy-start | bytes 52
  118.9 32.8 %collective-permute-start.2 = (bf16[4,90,18,1]{1,0,3,2:T(4,128)(2,1)S(1)}, bf16[4,90,18,1]{1,0,3,2:T(4,128)(2,1)S(1)}, u32[]{:S(2)}, u32[]{:S(2)}) collective-permute-start(bf16[4,90,18,1]{1,0,3,2:T(4,128)(2,1)S(1)} %copy.207), channel_id=1, source_target_pairs={{0,1},{1,2},{2,3},{3,4},{4,5},{5,6},{6,7},{7,8},{8,9},{9,10},{10,1... | collective-permute-start | bytes 38888 | tf_op jit(solution)/shard_map/ppermute | solution.py:16
  123.2 31.0 %collective-permute-start.3 = (bf16[4,90,18,1]{1,0,3,2:T(4,128)(2,1)S(1)}, bf16[4,90,18,1]{1,0,3,2:T(4,128)(2,1)S(1)}, u32[]{:S(2)}, u32[]{:S(2)}) collective-permute-start(bf16[4,90,18,1]{1,0,3,2:T(4,128)(2,1)S(1)} %copy.208), channel_id=1, source_target_pairs={{1,0},{2,1},{3,2},{4,3},{5,4},{6,5},{7,6},{8,7},{9,8},{10,9},{11,1... | collective-permute-start | bytes 38888 | tf_op jit(solution)/shard_map/ppermute | solution.py:17
  126.0 65.2 %copy-start.66 = (pred[128]{0:T(512)(128)(4,1)}, pred[128]{0:T(512)(128)(4,1)S(1)}, u32[]{:S(2)}) copy-start(pred[128]{0:T(512)(128)(4,1)S(1)} %get-tuple-element.115) | copy-start | bytes 388
  126.0 65.2 %copy-start.69 = (pred[128]{0:T(512)(128)(4,1)}, pred[128]{0:T(512)(128)(4,1)S(1)}, u32[]{:S(2)}) copy-start(pred[128]{0:T(512)(128)(4,1)S(1)} %get-tuple-element.116) | copy-start | bytes 388
  204.7 15.2 %copy-start.13 = (bf16[4,90,16,128]{3,0,2,1:T(4,128)(2,1)}, bf16[4,90,16,128]{3,0,2,1:T(4,128)(2,1)S(1)}, u32[]{:S(2)}) copy-start(bf16[4,90,16,128]{3,0,2,1:T(4,128)(2,1)S(1)} %get-tuple-element.37) | copy-start | bytes 4423684
  213.7 6.1 collective-permute-start.4
  213.7 6.1 collective-permute-start.5
  226.5 8.0 %collective-permute-start.6 = (bf16[4,90,18,1]{1,0,3,2:T(4,128)(2,1)S(1)}, bf16[4,90,18,1]{1,0,3,2:T(4,128)(2,1)}, u32[]{:S(2)}, u32[]{:S(2)}) collective-permute-start(bf16[4,90,18,1]{1,0,3,2:T(4,128)(2,1)S(1)} %copy.225), channel_id=1, source_target_pairs={{0,1},{1,2},{2,3},{3,4},{4,5},{5,6},{6,7},{7,8},{8,9},{9,10},{10,1... | collective-permute-start | bytes 38888 | tf_op jit(solution)/shard_map/ppermute | solution.py:16
  228.5 8.4 %collective-permute-start.7 = (bf16[4,90,18,1]{1,0,3,2:T(4,128)(2,1)}, bf16[4,90,18,1]{1,0,3,2:T(4,128)(2,1)}, u32[]{:S(2)}, u32[]{:S(2)}) collective-permute-start(bf16[4,90,18,1]{1,0,3,2:T(4,128)(2,1)} %copy.226), channel_id=1, source_target_pairs={{1,0},{2,1},{3,2},{4,3},{5,4},{6,5},{7,6},{8,7},{9,8},{10,9},{11,1... | collective-permute-start | bytes 38888 | tf_op jit(solution)/shard_map/ppermute | solution.py:17
  288.2 29.6 %copy-start.4 = (f32[4,90,16,128]{3,0,2,1:T(4,128)}, f32[4,90,16,128]{3,0,2,1:T(4,128)S(1)}, u32[]{:S(2)}) copy-start(f32[4,90,16,128]{3,0,2,1:T(4,128)S(1)} %get-tuple-element.36) | copy-start | bytes 8847364
  297.0 6.1 collective-permute-start.8
  297.0 6.1 collective-permute-start.9
  310.2 8.4 %collective-permute-start.10 = (bf16[4,90,18,1]{1,0,3,2:T(4,128)(2,1)S(1)}, bf16[4,90,18,1]{1,0,3,2:T(4,128)(2,1)S(1)}, u32[]{:S(2)}, u32[]{:S(2)}) collective-permute-start(bf16[4,90,18,1]{1,0,3,2:T(4,128)(2,1)S(1)} %copy.233), channel_id=1, source_target_pairs={{0,1},{1,2},{2,3},{3,4},{4,5},{5,6},{6,7},{7,8},{8,9},{9,10},{10,1... | collective-permute-start | bytes 38888 | tf_op jit(solution)/shard_map/ppermute | solution.py:16
  313.7 6.4 %collective-permute-start.11 = (bf16[4,90,18,1]{1,0,3,2:T(4,128)(2,1)}, bf16[4,90,18,1]{1,0,3,2:T(4,128)(2,1)}, u32[]{:S(2)}, u32[]{:S(2)}) collective-permute-start(bf16[4,90,18,1]{1,0,3,2:T(4,128)(2,1)} %copy.234), channel_id=1, source_target_pairs={{1,0},{2,1},{3,2},{4,3},{5,4},{6,5},{7,6},{8,7},{9,8},{10,9},{11,1... | collective-permute-start | bytes 38888 | tf_op jit(solution)/shard_map/ppermute | solution.py:17
  380.0 6.2 %collective-permute-start.12 = (bf16[4,90,1,128]{3,0,2,1:T(4,128)(2,1)S(1)}, bf16[4,90,1,128]{3,0,2,1:T(4,128)(2,1)S(1)}, u32[]{:S(2)}, u32[]{:S(2)}) collective-permute-start(bf16[4,90,1,128]{3,0,2,1:T(4,128)(2,1)S(1)} %get-tuple-element.95), channel_id=1, source_target_pairs={{0,16},{16,32},{32,48},{48,64},{64,80},{80,96},{96,112},{112,0},{1... | collective-permute-start | bytes 276488 | tf_op jit(solution)/shard_map/ppermute | solution.py:16
  380.0 6.2 collective-permute-start.13
  393.4 7.9 %collective-permute-start.14 = (bf16[4,90,18,1]{1,0,3,2:T(4,128)(2,1)S(1)}, bf16[4,90,18,1]{1,0,3,2:T(4,128)(2,1)S(1)}, u32[]{:S(2)}, u32[]{:S(2)}) collective-permute-start(bf16[4,90,18,1]{1,0,3,2:T(4,128)(2,1)S(1)} %copy.241), channel_id=1, source_target_pairs={{0,1},{1,2},{2,3},{3,4},{4,5},{5,6},{6,7},{7,8},{8,9},{9,10},{10,1... | collective-permute-start | bytes 38888 | tf_op jit(solution)/shard_map/ppermute | solution.py:16
  396.3 7.4 %collective-permute-start.15 = (bf16[4,90,18,1]{1,0,3,2:T(4,128)(2,1)S(1)}, bf16[4,90,18,1]{1,0,3,2:T(4,128)(2,1)S(1)}, u32[]{:S(2)}, u32[]{:S(2)}) collective-permute-start(bf16[4,90,18,1]{1,0,3,2:T(4,128)(2,1)S(1)} %copy.242), channel_id=1, source_target_pairs={{1,0},{2,1},{3,2},{4,3},{5,4},{6,5},{7,6},{8,7},{9,8},{10,9},{11,1... | collective-permute-start | bytes 38888 | tf_op jit(solution)/shard_map/ppermute | solution.py:17
  414.9 27.6 %all-to-all-start.2 = ((bf16[360,16,128]{2,0,1:T(8,128)(2,1)}), bf16[360,16,128]{2,0,1:T(8,128)(2,1)}, u32[]{:S(2)}, u32[]{:S(2)}) async-start(bf16[360,16,128]{2,0,1:T(8,128)(2,1)} %get-tuple-element.105), calls=%async_computation.2 | async-start | bytes 2949120 | tf_op jit(solution)/shard_map/all_to_all | solution.py:105
  472.3 82.8 %all-to-all-start.1 = ((bf16[360,16,128]{2,0,1:T(8,128)(2,1)}), bf16[360,16,128]{2,0,1:T(8,128)(2,1)}, u32[]{:S(2)}, u32[]{:S(2)}) async-start(bf16[360,16,128]{2,0,1:T(8,128)(2,1)} %fusion.20), calls=%async_computation.1 | async-start | bytes 2949120 | tf_op jit(solution)/shard_map/all_to_all | solution.py:109
  478.8 72.4 %all-reduce.6.cloned.1.call-start = ((), (), s32[]{:S(2)}) async-start(), calls=%async_computation.4 | async-start | bytes 5242880
  555.1 45.4 %all-to-all-start.3 = ((bf16[360,16,128]{2,0,1:T(8,128)(2,1)}), bf16[360,16,128]{2,0,1:T(8,128)(2,1)}, u32[]{:S(2)}, u32[]{:S(2)}) async-start(bf16[360,16,128]{2,0,1:T(8,128)(2,1)} %fusion.18), calls=%async_computation.3 | async-start | bytes 2949120 | tf_op jit(solution)/shard_map/all_to_all | solution.py:110
  (64 other events, 275.2 us)
Sparse Core Ops, SparseCore 0:
  482.1 68.9 all-reduce.5
where the time goes:
time: 632 us; the launch traced here: 622 us
  local copies, waits for them, and re-layouts  328 us (52%)
  other arithmetic  102 us (16%)
  starting transfers between devices  62.2 us (10%)
  waiting for transfers between devices  42.7 us (7%)
  blocking collectives  41.6 us (7%)
  matrix products  29.2 us (5%)
  between operations  15.9 us (3%)
    unnamed x169, local copies, waits for them, and re-layouts  46 us
    broadcast_in_dim x4, local copies, waits for them, and re-layouts, shards(): east = jnp.where(lane == columns - 1, east_rim, jnp.roll(state, -1, axis=3))  42.3 us
    broadcast_in_dim x4, local copies, waits for them, and re-layouts, shards(): west = jnp.where(lane == 0, west_rim, jnp.roll(state, 1, axis=3))  42.2 us
    convert_element_type x3, other arithmetic, shards(): state.astype(jnp.bfloat16)  37.7 us
    unnamed x2, waiting for transfers between devices  36.2 us
    slice x8, local copies, waits for them, and re-layouts, shards(): east = jnp.where(lane == columns - 1, east_rim, jnp.roll(state, -1, axis=3))  33.4 us
    convert_element_type x4, other arithmetic, shards(): extended(state.astype(jnp.bfloat16), (('lat', 2), ('lon', 3)), 1)  29.3 us
    ppermute x8, starting transfers between devices, extended(): after = lax.ppermute(first, axis, down)  26.9 us
  transfers between devices with their start and end apart: 21, of which 2 were waited for; matrix products, arithmetic and copies ran while one was open for 60% of the time, Pallas kernels for 0%

commit v1 on v0

v1 whole, which is shorter than its diff:
```python
import jax
import jax.numpy as jnp
from jax import lax
from jax.experimental import pallas as pl
from jax.experimental.pallas import tpu as pltpu
from jax.sharding import PartitionSpec as P


STEPS = 4
LANE = 128
WIDE = 4
GROUP = 32
LEVELS = 16
F32 = jnp.float32
BF16 = jnp.bfloat16


def iota(shape, dim):
    return lax.broadcasted_iota(jnp.int32, shape, dim)


def rows_of_source(src_ref, mat_ref, rows):
    for r in range(rows):
        mat_ref[:, r * LANE : (r + 1) * LANE] = src_ref[pl.ds(r, mat_ref.shape[0], stride=rows), :].astype(BF16)


def gather_blocks(table_ref, mat_ref, out_ref):
    ncol = mat_ref.shape[1]
    first = pl.program_id(0) * WIDE
    column = iota((ncol, LANE), 0)
    hot = [jnp.where(column == table_ref[pl.ds(first + b, 1), :], 1.0, 0.0).astype(BF16) for b in range(WIDE)]
    got = jnp.dot(mat_ref[...], jnp.concatenate(hot, axis=1), preferred_element_type=F32).astype(BF16)
    for b in range(WIDE):
        out_ref[b] = got[:, b * LANE : (b + 1) * LANE]


def gather_first_kernel(dest_ref, count_ref, cols_ref, src_ref, out_ref, table_ref, mat_ref, *, rows):
    @pl.when(pl.program_id(0) == 0)
    def _():
        slot = iota((1, LANE), 1)
        for b in range(cols_ref.shape[0]):
            row = jnp.where(slot < count_ref[0, 0, b], cols_ref[b], -1)
            table_ref[pl.ds(dest_ref[0, 0, b], 1), :] = row
        rows_of_source(src_ref, mat_ref, rows)

    gather_blocks(table_ref, mat_ref, out_ref)


def gather_kernel(table_ref, src_ref, out_ref, mat_ref, wide_ref, *, rows):
    @pl.when(pl.program_id(0) == 0)
    def _():
        wide_ref[...] = src_ref[...].astype(F32)
        rows_of_source(wide_ref, mat_ref, rows)

    gather_blocks(table_ref, mat_ref, out_ref)


def gather_parts(source, nblock, feat, rows):
    once = pl.BlockSpec(source.shape, lambda i: (0, 0), pipeline_mode=pl.Buffered(1))
    out = pl.BlockSpec((WIDE, feat, LANE), lambda i: (i, 0, 0))
    shape = jax.ShapeDtypeStruct((nblock, feat, LANE), BF16)
    cost = pl.CostEstimate(
        flops=2 * feat * rows * LANE * nblock * LANE,
        transcendentals=0,
        bytes_accessed=source.size * source.dtype.itemsize + feat * nblock * LANE * 2,
    )
    return once, out, shape, cost


def gather_first(dest, count, cols, source, feat, rows):
    nblock = cols.shape[0]
    once, out, shape, cost = gather_parts(source, nblock, feat, rows)
    table = jax.ShapeDtypeStruct((nblock, LANE), jnp.int32)

    def kernel(*refs):
        gather_first_kernel(*refs, rows=rows)

    scalars = pl.BlockSpec(memory_space=pltpu.SMEM)
    return pl.pallas_call(
        kernel,
        grid=(nblock // WIDE,),
        in_specs=[scalars, scalars, pl.BlockSpec(cols.shape, lambda i: (0, 0, 0)), once],
        out_specs=[out, pl.BlockSpec(table.shape, lambda i: (0, 0))],
        out_shape=[shape, table],
        scratch_shapes=[pltpu.VMEM((feat, rows * LANE), BF16)],
        cost_estimate=cost,
        name="gather_first",
    )(dest, count, cols, source)


def gather_columns(table, source, feat, rows):
    nblock = table.shape[0]
    once, out, shape, cost = gather_parts(source, nblock, feat, rows)

    def kernel(*refs):
        gather_kernel(*refs, rows=rows)

    return pl.pallas_call(
        kernel,
        grid=(nblock // WIDE,),
        in_specs=[pl.BlockSpec(table.shape, lambda i: (0, 0)), once],
        out_specs=out,
        out_shape=shape,
        scratch_shapes=[pltpu.VMEM((feat, rows * LANE), BF16), pltpu.VMEM(source.shape, F32)],
        cost_estimate=cost,
        name="gather_columns",
    )(table, source)


def scatter_rows(table_ref, blocks_ref, mat_ref, where_ref):
    nblock = blocks_ref.shape[0]

    @pl.when(pl.program_id(0) == 0)
    def _():
        table = table_ref[...].astype(F32)
        by_slot = jnp.concatenate([table, jnp.zeros((LANE - nblock, LANE), F32)], axis=0).T
        for b in range(nblock):
            mat_ref[:, b * LANE : (b + 1) * LANE] = blocks_ref[b]
            column = jnp.broadcast_to(by_slot[:, b : b + 1], (LANE, LANE))
            where_ref[b * LANE : (b + 1) * LANE, :] = column.astype(jnp.int32)

    where = where_ref[...]
    lane = iota(where.shape, 1) + pl.program_id(0) * (WIDE * LANE)
    hot = [jnp.where(where == lane + r * LANE, 1.0, 0.0).astype(BF16) for r in range(WIDE)]
    return jnp.dot(mat_ref[...], jnp.concatenate(hot, axis=1), preferred_element_type=F32)


def scatter_add_kernel(table_ref, blocks_ref, base_ref, out_ref, mat_ref, where_ref, *, rows):
    got = scatter_rows(table_ref, blocks_ref, mat_ref, where_ref)
    for r in range(WIDE):
        at = pl.ds(pl.program_id(0) * WIDE + r, mat_ref.shape[0], stride=rows)
        out_ref[at, :] = base_ref[at, :] + got[:, r * LANE : (r + 1) * LANE]


def scatter_kernel(table_ref, blocks_ref, out_ref, mat_ref, where_ref, full_ref, *, rows):
    got = scatter_rows(table_ref, blocks_ref, mat_ref, where_ref)
    for r in range(WIDE):
        at = pl.ds(pl.program_id(0) * WIDE + r, mat_ref.shape[0], stride=rows)
        full_ref[at, :] = got[:, r * LANE : (r + 1) * LANE]

    @pl.when(pl.program_id(0) == pl.num_programs(0) - 1)
    def _():
        out_ref[...] = full_ref[...].astype(BF16)


def scatter_columns(table, blocks, rows, base=None):
    nblock, feat, length = blocks.shape
    nslot = nblock * length
    shape = (feat * rows, LANE)
    whole = pl.BlockSpec(shape, lambda i: (0, 0), pipeline_mode=pl.Buffered(1))
    specs = [
        pl.BlockSpec(table.shape, lambda i: (0, 0)),
        pl.BlockSpec(blocks.shape, lambda i: (0, 0, 0), pipeline_mode=pl.Buffered(1)),
    ]
    scratch = [pltpu.VMEM((feat, nslot), BF16), pltpu.VMEM((nslot, LANE), jnp.int32)]
    if base is None:
        body, operands, dtype = scatter_kernel, (table, blocks), BF16
        scratch.append(pltpu.VMEM(shape, F32))
    else:
        body, operands, dtype = scatter_add_kernel, (table, blocks, base), F32
        specs.append(whole)

    def kernel(*refs):
        body(*refs, rows=rows)

    return pl.pallas_call(
        kernel,
        grid=(rows // WIDE,),
        in_specs=specs,
        out_specs=pl.BlockSpec(shape, lambda i: (0, 0)),
        out_shape=jax.ShapeDtypeStruct(shape, dtype),
        scratch_shapes=scratch,
        cost_estimate=pl.CostEstimate(
            flops=2 * feat * nslot * rows * LANE, transcendentals=0, bytes_accessed=feat * nslot * 8
        ),
        name="scatter_columns",
    )(*operands)


def wide(ref):
    return jnp.concatenate([ref[b] for b in range(ref.shape[0])], axis=1)


def normalised(x):
    xf = x.astype(F32)
    scale = lax.rsqrt(jnp.mean(xf * xf, axis=0, keepdims=True) + 1e-06)
    return xf, scale, (xf * scale).astype(BF16)


def mul(a, b):
    return jnp.dot(a, b, preferred_element_type=F32)


def mul_slots(a, b):
    return lax.dot_general(a, b, (((1,), (1,)), ((), ())), preferred_element_type=F32)


def forward_kernel(x_ref, wt_ref, w_ref, tend_ref, a1_ref, a2_ref, *, cuts):
    (in0, in1), (mid0, mid1), (out0, out1) = cuts
    _, _, xn = normalised(wide(x_ref))
    a_one = mul(wt_ref[:, in0:in1], xn)
    a1_ref[...] = a_one
    h_one = (a_one * jax.nn.sigmoid(a_one)).astype(BF16)
    a_two = mul(wt_ref[:, mid0:mid1], h_one)
    a2_ref[...] = a_two
    h_two = (a_two * jax.nn.sigmoid(a_two)).astype(BF16)
    tend = mul(w_ref[out0:out1, :], h_two).astype(BF16)
    for b in range(x_ref.shape[0]):
        tend_ref[b] = tend[:, b * LANE : (b + 1) * LANE]


def backward_kernel(x_ref, g_ref, a1_ref, a2_ref, wt_ref, w_ref, adj_ref, grad_ref, sum_ref, *, cuts):
    (in0, in1), (mid0, mid1), (out0, out1) = cuts

    @pl.when(pl.program_id(0) == 0)
    def _():
        sum_ref[...] = jnp.zeros_like(sum_ref)

    xf, scale, xn = normalised(wide(x_ref))
    g = wide(g_ref)
    a_two = a2_ref[...]
    sig = jax.nn.sigmoid(a_two)
    h_two = (a_two * sig).astype(BF16)
    d_two = (mul(wt_ref[:, out0:out1], g) * (sig * (1.0 + a_two * (1.0 - sig)))).astype(BF16)
    sum_ref[:, out0:out1] += mul_slots(h_two, g)
    a_one = a1_ref[...]
    sig = jax.nn.sigmoid(a_one)
    h_one = (a_one * sig).astype(BF16)
    d_one = (mul(w_ref[mid0:mid1, :], d_two) * (sig * (1.0 + a_one * (1.0 - sig)))).astype(BF16)
    sum_ref[:, mid0:mid1] += mul_slots(d_two, h_one)
    d_norm = mul(w_ref[in0:in1, :], d_one)
    adj = (
        scale * d_norm - xf * (scale * scale * scale) * jnp.mean(xf * d_norm, axis=0, keepdims=True)
    ).astype(BF16)
    for b in range(x_ref.shape[0]):
        adj_ref[b] = adj[:, b * LANE : (b + 1) * LANE]
    sum_ref[:, in0:in1] += mul_slots(d_one, xn)

    @pl.when(pl.program_id(0) == pl.num_programs(0) - 1)
    def _():
        grad_ref[...] = sum_ref[...].astype(BF16)


def column_specs(shape, pair, hid, span):
    _, feat, length = shape
    block = pl.BlockSpec((pair, feat, length), lambda i: (i, 0, 0))
    hidden = pl.BlockSpec((hid, pair * length), lambda i: (0, i))
    w_t = pl.BlockSpec((hid, span), lambda i: (0, 0), pipeline_mode=pl.Buffered(1))
    w = pl.BlockSpec((span, hid), lambda i: (0, 0), pipeline_mode=pl.Buffered(1))
    return block, hidden, w_t, w


def physics_forward(x, w_t, w, cuts):
    nblock, feat, length = x.shape
    hid, span = w_t.shape
    pair = WIDE
    block, hidden, spec_t, spec = column_specs(x.shape, pair, hid, span)

    def kernel(*refs):
        forward_kernel(*refs, cuts=cuts)

    kept = jax.ShapeDtypeStruct((hid, nblock * length), F32)
    return pl.pallas_call(
        kernel,
        grid=(nblock // pair,),
        in_specs=[block, spec_t, spec],
        out_specs=[block, hidden, hidden],
        out_shape=[jax.ShapeDtypeStruct(x.shape, BF16), kept, kept],
        cost_estimate=pl.CostEstimate(
            flops=2 * hid * (2 * feat + hid) * nblock * length,
            transcendentals=4 * hid * nblock * length,
            bytes_accessed=x.size * 4 + hid * nblock * length * 8,
        ),
        name="physics_forward",
    )(x, w_t, w)


def physics_backward(x, g, a_one, a_two, w_t, w, cuts):
    nblock, feat, length = x.shape
    hid, span = w_t.shape
    pair = WIDE
    block, hidden, spec_t, spec = column_specs(x.shape, pair, hid, span)

    def kernel(*refs):
        backward_kernel(*refs, cuts=cuts)

    return pl.pallas_call(
        kernel,
        grid=(nblock // pair,),
        in_specs=[block, block, hidden, hidden, spec_t, spec],
        out_specs=[block, pl.BlockSpec((hid, span), lambda i: (0, 0))],
        out_shape=[jax.ShapeDtypeStruct(x.shape, BF16), jax.ShapeDtypeStruct((hid, span), BF16)],
        scratch_shapes=[pltpu.VMEM((hid, span), F32)],
        cost_estimate=pl.CostEstimate(
            flops=4 * hid * (2 * feat + hid) * nblock * length,
            transcendentals=4 * hid * nblock * length,
            bytes_accessed=x.size * 6 + hid * nblock * length * 8,
        ),
        name="physics_backward",
    )(x, g, a_one, a_two, w_t, w)


def plane(fields_ref, coef_refs, a, at):
    nfield = fields_ref.shape[0]
    return fields_ref[a, at, :] if a < nfield else coef_refs[a - nfield][at, :]


def inside(levels):
    return iota((GROUP, LANE), 0) + pl.program_id(0) * GROUP < levels


def rim_kernel(fields_ref, lon_ref, lat_ref, dif_ref, low_ref, high_ref, *, rows, levels):
    coefs = (lon_ref, lat_ref, dif_ref)
    keep = inside(levels)
    for r in range(STEPS):
        for a in range(low_ref.shape[1]):
            for first, out in ((r, low_ref), (rows - STEPS + r, high_ref)):
                value = plane(fields_ref, coefs, a, pl.ds(first, GROUP, stride=rows))
                out[r, a] = jnp.where(keep, value, 0.0).astype(BF16)


def strip_kernel(
    fields_ref, lon_ref, lat_ref, dif_ref, south_ref, north_ref, west_ref, east_ref, all_ref, sum_ref, *, rows, levels
):
    coefs = (lon_ref, lat_ref, dif_ref)
    planes = south_ref.shape[1]
    keep = inside(levels)
    for t in range(rows + 2 * STEPS):
        for a in range(planes):
            if t < STEPS:
                value = south_ref[t, a]
            elif t >= rows + STEPS:
                value = north_ref[t - rows - STEPS, a]
            else:
                own = plane(fields_ref, coefs, a, pl.ds(t - STEPS, GROUP, stride=rows))
                value = jnp.where(keep, own, 0.0).astype(BF16)
            all_ref[t * GROUP : (t + 1) * GROUP, a * LANE : (a + 1) * LANE] = value
    shape = (planes * LANE, 2 * LANE)
    k, n = iota(shape, 0), iota(shape, 1)
    a, q = k // LANE, k % LANE
    west = jnp.where(q < STEPS, STEPS * a + q, -1)
    east = jnp.where(q >= LANE - STEPS, STEPS * a + q - (LANE - STEPS) + LANE, -1)
    pick = jnp.where((n == west) | (n == east), 1.0, 0.0).astype(BF16)
    got = jnp.dot(all_ref[...], pick, preferred_element_type=F32)
    group = pl.program_id(0)

    @pl.when(group == 0)
    def _():
        sum_ref[...] = got

    @pl.when(group > 0)
    def _():
        for half in range(2):
            part = got[:, half * LANE : (half + 1) * LANE]
            sum_ref[:, half * LANE : (half + 1) * LANE] += pltpu.roll(part, group * GROUP, 1)

    @pl.when(group == pl.num_programs(0) - 1)
    def _():
        west_ref[...] = sum_ref[:, :LANE].astype(BF16)
        east_ref[...] = sum_ref[:, LANE:].astype(BF16)


def weights_of(c_lon, c_lat, c_dif):
    return (
        1.0 - 4.0 * c_dif,
        c_dif - 0.5 * c_lon,
        c_dif + 0.5 * c_lon,
        c_dif - 0.5 * c_lat,
        c_dif + 0.5 * c_lat,
    )


def stepped(coef, centre, east, west, north, south):
    return coef[0] * centre + (coef[1] * east + coef[2] * west) + (coef[3] * north + coef[4] * south)


def dynamics_kernel(
    fields_ref,
    lon_ref,
    lat_ref,
    dif_ref,
    south_ref,
    north_ref,
    own_w_ref,
    own_e_ref,
    from_e_ref,
    from_w_ref,
    out_ref,
    rim_ref,
    strip_ref,
    coef_ref,
    join_ref,
    state_ref,
    shift_ref,
    *,
    rows,
):
    coefs = (lon_ref, lat_ref, dif_ref)
    nfield = fields_ref.shape[0]
    total = rows + 2 * STEPS
    rim_ref[0] = south_ref[...].astype(F32)
    rim_ref[1] = north_ref[...].astype(F32)

    sources = jnp.concatenate([own_e_ref[...], from_e_ref[...], from_w_ref[...], own_w_ref[...]], axis=1)
    shape = (4 * LANE, 4 * LANE)
    k, n = iota(shape, 0), iota(shape, 1)
    lane, kind, m = k % LANE, n // LANE, n % LANE
    row_code = (k // LANE) * STEPS + lane % STEPS + 16 * ((lane // STEPS) % 8)
    row_code = jnp.where(lane // GROUP == pl.program_id(0), row_code, -1)
    col_code = jnp.where(kind == 0, m, m % 16 + 16 * (nfield - 1 + kind))
    col_code = jnp.where(m < 16 * nfield, col_code, -2)
    pick = jnp.where(row_code == col_code, 1.0, 0.0).astype(BF16)
    strip_ref[...] = jnp.dot(sources, pick, preferred_element_type=F32)

    @pl.when(pl.program_id(0) == 0)
    def _():
        shape = (2 * LANE, 2 * LANE)
        k, n = iota(shape, 0), iota(shape, 1)
        east = jnp.where(k < LANE, k - 1, jnp.where(k % 16 == 4, LANE - 1, -1))
        west = jnp.where(k < LANE - 1, k + 1 + LANE, jnp.where((k >= LANE) & (k % 16 == 11), LANE, -1))
        shift_ref[...] = jnp.where(((n == east) & (k > 0)) | (n == west), 1.0, 0.0).astype(BF16)

    part = LEVELS
    field_of_lane = iota((part, LANE), 1) // 16

    def levels(sub, carry):
        def cell(a, t):
            if STEPS <= t < rows + STEPS:
                return plane(fields_ref, coefs, a, pl.ds(sub * (part * rows) + t - STEPS, part, stride=rows))
            side, at = (0, t) if t < STEPS else (1, t - rows - STEPS)
            return rim_ref[side, at, a, pl.ds(sub * part, part), :]

        def strip(kind, t):
            return strip_ref[pl.ds(t * GROUP + sub * part, part), kind * LANE : (kind + 1) * LANE]

        for t in range(1, total - 1):
            at = slice(t * part, (t + 1) * part)
            for c, value in enumerate(weights_of(cell(nfield, t), cell(nfield + 1, t), cell(nfield + 2, t))):
                coef_ref[0, c, at] = value
            for c, value in enumerate(weights_of(strip(1, t), strip(2, t), strip(3, t))):
                coef_ref[1, c, at] = value
        for f in range(nfield):
            for t in range(total):
                state_ref[0, f, t * part : (t + 1) * part] = cell(f, t)

        state = {t: strip(0, t) for t in range(total)}
        for step in range(STEPS):
            inner = range(step + 1, total - 1 - step)
            for t in inner:
                for f in range(nfield):
                    join_ref[step, f, t * part : (t + 1) * part] = jnp.where(field_of_lane == f, state[t], 0.0).astype(BF16)
            if step < STEPS - 1:
                state = {
                    t: stepped(
                        [coef_ref[1, c, t * part : (t + 1) * part] for c in range(5)],
                        state[t],
                        pltpu.roll(state[t], LANE - 1, 1),
                        pltpu.roll(state[t], 1, 1),
                        state[t + 1],
                        state[t - 1],
                    )
                    for t in inner
                }

        def rows_of(step, by=0):
            return slice((step + 1 + by) * part, (total - 1 - step + by) * part)

        def neighbours(step, pair):
            at = rows_of(step)
            cells = [
                jnp.concatenate([state_ref[step % 2, f, at].astype(BF16), join_ref[step, f, at]], axis=1) for f in pair
            ]
            return mul(jnp.concatenate(cells, axis=0), shift_ref[...])

        turns = [(step, pair) for step in range(STEPS) for pair in ((0, 1), (2, 3))]
        ready = neighbours(*turns[0])
        for turn, (step, pair) in enumerate(turns):
            sides = ready
            if turn + 1 < len(turns):
                ready = neighbours(*turns[turn + 1])
            size = (total - 2 - 2 * step) * part
            coef = [coef_ref[0, c, rows_of(step)] for c in range(5)]
            for n, f in enumerate(pair):
                cur = step % 2
                value = stepped(
                    coef,
                    state_ref[cur, f, rows_of(step)],
                    sides[n * size : (n + 1) * size, :LANE],
                    sides[n * size : (n + 1) * size, LANE:],
                    state_ref[cur, f, rows_of(step, 1)],
                    state_ref[cur, f, rows_of(step, -1)],
                )
                if step < STEPS - 1:
                    state_ref[1 - cur, f, rows_of(step)] = value
                    continue
                for r in range(rows):
                    out_ref[f, pl.ds(sub * (part * rows) + r, part, stride=rows), :] = value[r * part : (r + 1) * part]
        return carry

    lax.fori_loop(0, GROUP // part, levels, 0)


class Dynamics:
    def __init__(self, fields, coefs, rows, levels):
        self.args = (fields, *coefs)
        self.rows, self.levels = rows, levels
        nfield = fields.shape[0]
        planes = nfield + len(coefs)
        groups = pl.cdiv(levels, GROUP)
        self.grid = (groups,)
        self.planes = planes
        self.strip_rows = (rows + 2 * STEPS) * GROUP
        self.fields_spec = pl.BlockSpec((nfield, GROUP * rows, LANE), lambda i: (0, i, 0))
        self.arg_specs = [self.fields_spec] + [pl.BlockSpec((GROUP * rows, LANE), lambda i: (i, 0))] * 3
        self.rim_spec = pl.BlockSpec((STEPS, planes, GROUP, LANE), lambda i: (0, 0, i, 0))
        self.rim_shape = jax.ShapeDtypeStruct((STEPS, planes, groups * GROUP, LANE), BF16)
        self.strip_spec = pl.BlockSpec((self.strip_rows, LANE), lambda i: (0, 0))
        self.strip_shape = jax.ShapeDtypeStruct((self.strip_rows, LANE), BF16)

    def rims(self):
        def kernel(*refs):
            rim_kernel(*refs, rows=self.rows, levels=self.levels)

        return pl.pallas_call(
            kernel,
            grid=self.grid,
            in_specs=self.arg_specs,
            out_specs=[self.rim_spec, self.rim_spec],
            out_shape=[self.rim_shape, self.rim_shape],
            name="rims",
        )(*self.args)

    def send_rims(self, low, high):
        size = lax.axis_size("lat")
        up = [(i, i + 1) for i in range(size - 1)]
        south = lax.ppermute(high, "lat", up)
        north = lax.ppermute(low, "lat", [(j, i) for i, j in up])
        return south, north

    def strips(self, south, north, start):
        def kernel(*refs):
            strip_kernel(*refs, rows=self.rows, levels=self.levels)

        south, north = after((south, north), start)
        return pl.pallas_call(
            kernel,
            grid=self.grid,
            in_specs=self.arg_specs + [self.rim_spec, self.rim_spec],
            out_specs=[self.strip_spec, self.strip_spec],
            out_shape=[self.strip_shape, self.strip_shape],
            scratch_shapes=[
                pltpu.VMEM((self.strip_rows, self.planes * LANE), BF16),
                pltpu.VMEM((self.strip_rows, 2 * LANE), F32),
            ],
            name="strips",
        )(*self.args, south, north)

    def send_strips(self, own_w, own_e):
        size = lax.axis_size("lon")
        around = [(i, (i + 1) % size) for i in range(size)]
        from_w = lax.ppermute(own_e, "lon", around)
        from_e = lax.ppermute(own_w, "lon", [(j, i) for i, j in around])
        return from_w, from_e

    def steps(self, south, north, own_w, own_e, from_w, from_e, start):
        def kernel(*refs):
            dynamics_kernel(*refs, rows=self.rows)

        fields = self.args[0]
        from_w, from_e = after((from_w, from_e), start)
        return pl.pallas_call(
            kernel,
            grid=self.grid,
            in_specs=self.arg_specs + [self.rim_spec, self.rim_spec] + [self.strip_spec] * 4,
            out_specs=self.fields_spec,
            out_shape=jax.ShapeDtypeStruct(fields.shape, F32),
            scratch_shapes=[
                pltpu.VMEM((2, STEPS, self.planes, GROUP, LANE), F32),
                pltpu.VMEM((self.strip_rows, 4 * LANE), F32),
                pltpu.VMEM((2, 5, (self.rows + 2 * STEPS) * LEVELS, LANE), F32),
                pltpu.VMEM((STEPS, fields.shape[0], (self.rows + 2 * STEPS) * LEVELS, LANE), BF16),
                pltpu.VMEM((2, fields.shape[0], (self.rows + 2 * STEPS) * LEVELS, LANE), F32),
                pltpu.VMEM((2 * LANE, 2 * LANE), BF16),
            ],
            cost_estimate=pl.CostEstimate(flops=fields.size * 60, transcendentals=0, bytes_accessed=fields.size * 11),
            name="dynamics",
        )(*self.args, south, north, own_w, own_e, from_e, from_w)


def after(values, start):
    return lax.optimization_barrier((values, start))[0]


def exchange(array, axis):
    return lax.all_to_all(array, axis, split_axis=0, concat_axis=0, tiled=True)


def scattered(parts):
    size = parts.shape[0]
    core = lax.axis_index("lat") % 2
    pairs = parts.reshape((size // 2, 2) + parts.shape[1:])
    mine = lax.dynamic_index_in_dim(pairs, core, 1, keepdims=False)
    other = lax.dynamic_index_in_dim(pairs, 1 - core, 1, keepdims=False)
    other = lax.ppermute(other, "lat", [(i, i ^ 1) for i in range(size)])
    both = mine.astype(F32) + other.astype(F32)
    chips = size // 2
    chip = lax.axis_index("lat") // 2
    total = lax.dynamic_index_in_dim(both, chip, 0, keepdims=False)
    both = both.astype(BF16)
    for shift in range(1, chips):
        part = lax.dynamic_index_in_dim(both, (chip + shift) % chips, 0, keepdims=False)
        to = [(i, (i + 2 * shift) % size) for i in range(size)]
        total = total + lax.ppermute(part, "lat", to).astype(F32)
    return total


def shards(
    fields,
    courant_lon,
    courant_lat,
    diffusion,
    tend_cot,
    col_list,
    block_count,
    block_dest,
    w_in,
    w_mid,
    w_out,
):
    nfield, levels, rows, columns = fields.shape
    feat = nfield * levels
    hid_mid, hid_own = w_mid.shape[1:]
    nlat = lax.axis_size("lat")
    pad = -feat % LANE
    cuts = (
        (0, feat),
        (feat + pad, feat + pad + hid_mid),
        (feat + pad + hid_mid, 2 * feat + pad + hid_mid),
    )
    span = cuts[2][1] + pad

    rest = jnp.zeros((pad, hid_own), BF16)
    own = jnp.concatenate([w_in[0], rest, w_mid[0], w_out[0], rest], axis=0).T
    w_t = exchange(jnp.broadcast_to(own[None], (nlat,) + own.shape), "lat").reshape(nlat * hid_own, span)
    w = w_t.T
    coefs = [c.reshape(levels * rows, columns) for c in (courant_lon, courant_lat, diffusion)]
    window = Dynamics(fields.reshape(nfield, levels * rows, columns), coefs, rows, levels)

    nblock = block_dest.shape[-1]
    low, high = window.rims()
    south, north = window.send_rims(low, high)
    cols = after(col_list.reshape(nblock, 1, LANE), low)
    send_x, table = gather_first(block_dest, block_count, cols, fields.reshape(feat * rows, columns), feat, rows)
    recv_x = exchange(send_x, "lon")
    own_w, own_e = window.strips(south, north, send_x)
    send_g = gather_columns(after(table, own_w), tend_cot.reshape(feat * rows, columns), feat, rows)
    recv_g = exchange(send_g, "lon")
    from_w, from_e = window.send_strips(own_w, own_e)
    tend, a_one, a_two = physics_forward(after(recv_x, send_g), w_t, w, cuts)
    back_tend = exchange(tend, "lon")
    state = window.steps(south, north, own_w, own_e, from_w, from_e, tend)
    adj, grads = physics_backward(recv_x, after(recv_g, state), a_one, a_two, w_t, w, cuts)
    back_adj = exchange(after(adj, back_tend), "lon")
    summed = scattered(grads.reshape(nlat, hid_own, span)).T
    grad_in, grad_mid, grad_out = (summed[a:b][None] for a, b in cuts)

    new_fields = scatter_columns(table, back_tend, rows, state.reshape(feat * rows, columns))
    adjoint = scatter_columns(table, back_adj, rows)
    return (new_fields.reshape(fields.shape), adjoint.reshape(fields.shape), grad_in, grad_mid, grad_out)


def solution(mesh):
    return jax.shard_map(
        shards,
        mesh=mesh,
        in_specs=(
            P(None, None, "lat", "lon"),
            P(None, "lat", "lon"),
            P(None, "lat", "lon"),
            P(None, "lat", "lon"),
            P(None, None, "lat", "lon"),
            P("lat", "lon", None),
            P("lat", "lon", None),
            P("lat", "lon", None),
            P("lon", None, "lat"),
            P("lon", None, "lat"),
            P("lon", None, "lat"),
        ),
        out_specs=(
            P(None, None, "lat", "lon"),
            P(None, None, "lat", "lon"),
            P("lon", None, "lat"),
            P("lon", None, "lat"),
            P("lon", None, "lat"),
        ),
        check_vma=False,
    )
```

time: 632 us -> 175 us (0.28)
  the two profiles are of different devices: /device:TPU:8 before, /device:TPU:2 now
where the time goes in v1:
time: 175 us; the launch traced here: 174 us
  Pallas kernels  80.6 us (46%)
  starting transfers between devices  44.3 us (25%)
  waiting for transfers between devices  37.2 us (21%)
  local copies, waits for them, and re-layouts  9.21 us (5%)
    all_to_all x5, starting transfers between devices, exchange(): return lax.all_to_all(array, axis, split_axis=0, concat_axis=0, tiled=True)  29.9 us
    pallas_call x2, Pallas kernels, scatter_columns(): pl.pallas_call(kernel, grid=(rows // WIDE,), in_specs=specs, out_specs=pl...  17.6 us
    pallas_call x1, Pallas kernels, steps(): pl.pallas_call(kernel, grid=self.grid, in_specs=self.arg_specs + [self.ri...  16 us
    all_to_all x5, waiting for transfers between devices, exchange(): return lax.all_to_all(array, axis, split_axis=0, concat_axis=0, tiled=True)  14.7 us
    pallas_call x1, Pallas kernels, physics_backward(): pl.pallas_call(kernel, grid=(nblock // pair,), in_specs=[block, block, hi...  12.8 us
    pallas_call x1, Pallas kernels, gather_first(): pl.pallas_call(kernel, grid=(nblock // WIDE,), in_specs=[scalars, scalars...  7.88 us
    pallas_call x1, Pallas kernels, gather_columns(): pl.pallas_call(kernel, grid=(nblock // WIDE,), in_specs=[pl.BlockSpec(tab...  7.52 us
    pallas_call x1, Pallas kernels, physics_forward(): pl.pallas_call(kernel, grid=(nblock // pair,), in_specs=[block, spec_t, s...  7.33 us
  transfers between devices with their start and end apart: 13, of which 8 were waited for; matrix products, arithmetic and copies ran while one was open for 3% of the time, Pallas kernels for 42%

profile of v1, /device:TPU:2, one launch (start us, length us, event | category | flops | bytes accessed | tf_op | source)
XLA Modules:
  0.0 173.8 jit_solution(10380021250480263827)
XLA Ops:
  1.6 1.1 broadcast_in_dim.19
  2.7 4.8 %all-to-all-start.1 = ((bf16[8,64,1280]{2,1,0:T(8,128)(2,1)}), bf16[8,64,1280]{2,1,0:T(8,128)(2,1)S(1)}, u32[]{:S(2)}, u32[]{:S(2)}) async-start(bf16[8,64,1280]{2,1,0:T(8,128)(2,1)} %broadcast_in_dim.19), calls=%async_computation.1 | async-start | bytes 2621440 | tf_op jit(solution)/shard_map/all_to_all | solution.py:595
  7.6 4.5 %rims.1 = (bf16[4,7,96,128]{3,2,1,0:T(8,128)(2,1)}, bf16[4,7,96,128]{3,2,1,0:T(8,128)(2,1)}) custom-call(f32[4,1440,128]{2,1,0:T(8,128)} %bitcast.45, f32[1440,128]{1,0:T(8,128)} %bitcast.49, f32[1440,128]{1,0:T(8,128)} %bitcast.52, f32[1440,128]{1,0:T(8,128)} %bitcast.55), custom_call_target="tpu_custom_call" | custom-call | tf_op jit(solution)/shard_map/rims/pallas_call | solution.py:524
  12.1 7.9 %gather_first.1 = (bf16[16,360,128]{2,1,0:T(8,128)(2,1)}, s32[16,128]{1,0:T(8,128)}) custom-call(s32[1,1,16]{2,1,0:T(1,128)} %refs_0_.1, s32[1,1,16]{2,1,0:T(1,128)} %refs_1_.1, s32[16,1,128]{2,1,0:T(1,128)} %bitcast.71, f32[5760,128]{1,0:T(8,128)} %bitcast.46), custom_call_target="tpu_custom_call" | custom-call | flops 3019898880 | bytes 4423680 | tf_op jit(solution)/shard_map/gather_first/pallas_call | solution.py:79
  20.0 4.9 %all-to-all-done.1 = bf16[8,64,1280]{2,1,0:T(8,128)(2,1)S(1)} async-done(((bf16[8,64,1280]{2,1,0:T(8,128)(2,1)}), bf16[8,64,1280]{2,1,0:T(8,128)(2,1)S(1)}, u32[]{:S(2)}, u32[]{:S(2)}) %all-to-all-start.1) | async-done | bytes 1310752 | tf_op jit(solution)/shard_map/all_to_all | solution.py:595
  24.9 8.2 %all-to-all-start = ((bf16[16,360,128]{2,1,0:T(8,128)(2,1)}), bf16[16,360,128]{2,1,0:T(8,128)(2,1)}, u32[]{:S(2)}, u32[]{:S(2)}) async-start(bf16[16,360,128]{2,1,0:T(8,128)(2,1)} %get-tuple-element.28), calls=%async_computation | async-start | bytes 2949120 | tf_op jit(solution)/shard_map/all_to_all | solution.py:595
  33.1 2.2 %collective-permute-start.1 = (bf16[4,7,96,128]{3,2,1,0:T(8,128)(2,1)}, bf16[4,7,96,128]{3,2,1,0:T(8,128)(2,1)S(1)}, u32[]{:S(2)}, u32[]{:S(2)}) collective-permute-start(bf16[4,7,96,128]{3,2,1,0:T(8,128)(2,1)} %get-tuple-element.25), channel_id=1, source_target_pairs={{16,0},{32,16},{48,32},{64,48},{80,64},{96,80},{112,96},{17,1},{33... | collective-permute-start | bytes 2064392 | tf_op jit(solution)/shard_map/ppermute | solution.py:537
  35.3 2.1 %collective-permute-start = (bf16[4,7,96,128]{3,2,1,0:T(8,128)(2,1)S(1)}, bf16[4,7,96,128]{3,2,1,0:T(8,128)(2,1)S(1)}, u32[]{:S(2)}, u32[]{:S(2)}) collective-permute-start(bf16[4,7,96,128]{3,2,1,0:T(8,128)(2,1)S(1)} %copy-done.8), channel_id=1, source_target_pairs={{0,16},{16,32},{32,48},{48,64},{64,80},{80,96},{96,112},{1,17},{17... | collective-permute-start | bytes 2064392 | tf_op jit(solution)/shard_map/ppermute | solution.py:536
  37.4 6.6 %collective-permute-done.1.refs_5_ = bf16[4,7,96,128]{3,2,1,0:T(8,128)(2,1)S(1)} collective-permute-done((bf16[4,7,96,128]{3,2,1,0:T(8,128)(2,1)}, bf16[4,7,96,128]{3,2,1,0:T(8,128)(2,1)S(1)}, u32[]{:S(2)}, u32[]{:S(2)}) %collective-permute-start.1) | collective-permute-done | bytes 688160 | tf_op jit(solution)/shard_map/ppermute | solution.py:537
  44.1 3.5 %collective-permute-done.refs_4_ = bf16[4,7,96,128]{3,2,1,0:T(8,128)(2,1)S(1)} collective-permute-done((bf16[4,7,96,128]{3,2,1,0:T(8,128)(2,1)S(1)}, bf16[4,7,96,128]{3,2,1,0:T(8,128)(2,1)S(1)}, u32[]{:S(2)}, u32[]{:S(2)}) %collective-permute-start) | collective-permute-done | bytes 688160 | tf_op jit(solution)/shard_map/ppermute | solution.py:536
  48.5 6.9 %strips.1 = (bf16[768,128]{1,0:T(8,128)(2,1)}, bf16[768,128]{1,0:T(8,128)(2,1)}) custom-call(f32[4,1440,128]{2,1,0:T(8,128)} %bitcast.47, f32[1440,128]{1,0:T(8,128)} %bitcast.50, f32[1440,128]{1,0:T(8,128)} %bitcast.53, f32[1440,128]{1,0:T(8,128)} %bitcast.56, bf16[4,7,96,128]{3,2,1,0:T(8,128)(2,1)} %copy-done.2, bf16[4,7,96,128]{3,2,1,0:T(8,128)(2,1)} %copy-done.1), custom_call_target="tpu_custom_call" | custom-call | tf_op jit(solution)/shard_map/strips/pallas_call | solution.py:545
  55.4 7.5 %gather_columns.1 = bf16[16,360,128]{2,1,0:T(8,128)(2,1)} custom-call(s32[16,128]{1,0:T(8,128)} %get-tuple-element.33.refs_0_, bf16[5760,128]{1,0:T(8,128)(2,1)} %bitcast.70), custom_call_target="tpu_custom_call" | custom-call | flops 3019898880 | bytes 2949120 | tf_op jit(solution)/shard_map/gather_columns/pallas_call | solution.py:98
  62.9 7.0 %all-to-all-start.3 = ((bf16[16,360,128]{2,1,0:T(8,128)(2,1)}), bf16[16,360,128]{2,1,0:T(8,128)(2,1)S(1)}, u32[]{:S(2)}, u32[]{:S(2)}) async-start(bf16[16,360,128]{2,1,0:T(8,128)(2,1)} %gather_columns.1), calls=%async_computation.3 | async-start | bytes 2949120 | tf_op jit(solution)/shard_map/all_to_all | solution.py:595
  70.0 5.3 %collective-permute-start.3 = (bf16[768,128]{1,0:T(8,128)(2,1)S(1)}, bf16[768,128]{1,0:T(8,128)(2,1)S(1)}, u32[]{:S(2)}, u32[]{:S(2)}) collective-permute-start(bf16[768,128]{1,0:T(8,128)(2,1)S(1)} %copy-done.5), channel_id=1, source_target_pairs={{1,0},{2,1},{3,2},{4,3},{5,4},{6,5},{7,6},{8,7},{9,8},{10,9},{11,1... | collective-permute-start | bytes 589832 | tf_op jit(solution)/shard_map/ppermute | solution.py:562
  75.3 1.5 copy.19
  76.8 7.3 %physics_forward.1 = (bf16[16,360,128]{2,1,0:T(8,128)(2,1)}, f32[512,2048]{1,0:T(8,128)}, f32[512,2048]{1,0:T(8,128)}) custom-call(bf16[16,360,128]{2,1,0:T(8,128)(2,1)} %all-to-all-done.refs_0_, bf16[512,1280]{1,0:T(8,128)(2,1)} %bitcast.59, bf16[1280,512]{1,0:T(8,128)(2,1)} %bitcast.62), custom_call_target="tpu_custom_call" | custom-call | flops 2583691264 | bytes 11337728 | tf_op jit(solution)/shard_map/physics_forward/pallas_call | solution.py:263
  84.1 6.7 %collective-permute-done.3.refs_8_ = bf16[768,128]{1,0:T(8,128)(2,1)S(1)} collective-permute-done((bf16[768,128]{1,0:T(8,128)(2,1)S(1)}, bf16[768,128]{1,0:T(8,128)(2,1)S(1)}, u32[]{:S(2)}, u32[]{:S(2)}) %collective-permute-start.3) | collective-permute-done | bytes 196640 | tf_op jit(solution)/shard_map/ppermute | solution.py:562
  90.8 3.5 %collective-permute-done.2.refs_9_ = bf16[768,128]{1,0:T(8,128)(2,1)} collective-permute-done((bf16[768,128]{1,0:T(8,128)(2,1)S(1)}, bf16[768,128]{1,0:T(8,128)(2,1)}, u32[]{:S(2)}, u32[]{:S(2)}) %collective-permute-start.2) | collective-permute-done | bytes 196640 | tf_op jit(solution)/shard_map/ppermute | solution.py:561
  94.3 16.0 %dynamics.1 = f32[4,1440,128]{2,1,0:T(8,128)} custom-call(f32[4,1440,128]{2,1,0:T(8,128)} %bitcast.48, f32[1440,128]{1,0:T(8,128)} %bitcast.51, f32[1440,128]{1,0:T(8,128)} %bitcast.54, f32[1440,128]{1,0:T(8,128)} %bitcast.57, bf16[4,7,96,128]{3,2,1,0:T(8,128)(2,1)} %copy-done.2, bf16[4,7,96,128]{3,2,1,0:T(8,128)(2,1)} %copy-done.1, ...), custom_call_target="tpu_custom_call" | custom-call | flops 44236800 | bytes 8110080 | tf_op jit(solution)/shard_map/dynamics/pallas_call | solution.py:571
  111.5 5.2 %all-to-all-start.2 = ((bf16[16,360,128]{2,1,0:T(8,128)(2,1)}), bf16[16,360,128]{2,1,0:T(8,128)(2,1)S(1)}, u32[]{:S(2)}, u32[]{:S(2)}) async-start(bf16[16,360,128]{2,1,0:T(8,128)(2,1)} %get-tuple-element.35), calls=%async_computation.2 | async-start | bytes 2949120 | tf_op jit(solution)/shard_map/all_to_all | solution.py:595
  116.7 12.8 %physics_backward.1 = (bf16[16,360,128]{2,1,0:T(8,128)(2,1)}, bf16[512,1280]{1,0:T(8,128)(2,1)}) custom-call(bf16[16,360,128]{2,1,0:T(8,128)(2,1)} %all-to-all-done.refs_0_, bf16[16,360,128]{2,1,0:T(8,128)(2,1)} %copy-done.4, f32[512,2048]{1,0:T(8,128)} %get-tuple-element.40.refs_2_, f32[512,2048]{1,0:T(8,128)} %get-tuple-element.41.refs_3_, ...), custom_call_target="tpu_custom_call" | custom-call | flops 5167382528 | bytes 12812288 | tf_op jit(solution)/shard_map/physics_backward/pallas_call | solution.py:287
  129.5 1.1 dynamic-slice_bitcast_fusion
  130.8 2.1 %collective-permute-done.4 = bf16[4,64,1280]{2,1,0:T(8,128)(2,1)} collective-permute-done((bf16[4,64,1280]{2,1,0:T(8,128)(2,1)S(1)}, bf16[4,64,1280]{2,1,0:T(8,128)(2,1)}, u32[]{:S(2)}, u32[]{:S(2)}) %collective-permute-start.4) | collective-permute-done | bytes 655392 | tf_op jit(solution)/shard_map/ppermute | solution.py:604
  132.9 1.5 fusion.3
  134.4 2.7 %all-to-all-done.2.refs_1_ = bf16[16,360,128]{2,1,0:T(8,128)(2,1)S(1)} async-done(((bf16[16,360,128]{2,1,0:T(8,128)(2,1)}), bf16[16,360,128]{2,1,0:T(8,128)(2,1)S(1)}, u32[]{:S(2)}, u32[]{:S(2)}) %all-to-all-start.2) | async-done | bytes 1474592 | tf_op jit(solution)/shard_map/all_to_all | solution.py:595
  137.2 1.1 copy-done.3
  138.3 4.5 %all-to-all-start.4 = ((bf16[16,360,128]{2,1,0:T(8,128)(2,1)}), bf16[16,360,128]{2,1,0:T(8,128)(2,1)}, u32[]{:S(2)}, u32[]{:S(2)}) async-start(bf16[16,360,128]{2,1,0:T(8,128)(2,1)} %get-tuple-element.43), calls=%async_computation.4 | async-start | bytes 2949120 | tf_op jit(solution)/shard_map/all_to_all | solution.py:595
  142.9 2.6 %collective-permute-start.5 = (bf16[64,1280]{1,0:T(8,128)(2,1)S(1)}, bf16[64,1280]{1,0:T(8,128)(2,1)S(1)}, u32[]{:S(2)}, u32[]{:S(2)}) collective-permute-start(bf16[64,1280]{1,0:T(8,128)(2,1)S(1)} %get-tuple-element.47), channel_id=1, source_target_pairs={{0,32},{16,48},{32,64},{48,80},{64,96},{80,112},{96,0},{112,16},{1... | collective-permute-start | bytes 491528 | tf_op jit(solution)/shard_map/ppermute | solution.py:613
  145.4 2.2 %collective-permute-start.7 = (bf16[64,1280]{1,0:T(8,128)(2,1)S(1)}, bf16[64,1280]{1,0:T(8,128)(2,1)S(1)}, u32[]{:S(2)}, u32[]{:S(2)}) collective-permute-start(bf16[64,1280]{1,0:T(8,128)(2,1)S(1)} %get-tuple-element.48), channel_id=1, source_target_pairs={{0,96},{16,112},{32,0},{48,16},{64,32},{80,48},{96,64},{112,80},{1... | collective-permute-start | bytes 491528 | tf_op jit(solution)/shard_map/ppermute | solution.py:613
  147.6 9.8 %scatter_columns.2 = f32[5760,128]{1,0:T(8,128)} custom-call(s32[16,128]{1,0:T(8,128)} %get-tuple-element.33.refs_0_, bf16[16,360,128]{2,1,0:T(8,128)(2,1)} %copy-done.3, f32[5760,128]{1,0:T(8,128)} %bitcast.61), custom_call_target="tpu_custom_call" | custom-call | flops 3019898880 | bytes 5898240 | tf_op jit(solution)/shard_map/scatter_columns/pallas_call | solution.py:166
  158.8 7.1 %all-to-all-done.4.refs_1_ = bf16[16,360,128]{2,1,0:T(8,128)(2,1)} async-done(((bf16[16,360,128]{2,1,0:T(8,128)(2,1)}), bf16[16,360,128]{2,1,0:T(8,128)(2,1)}, u32[]{:S(2)}, u32[]{:S(2)}) %all-to-all-start.4) | async-done | bytes 1474592 | tf_op jit(solution)/shard_map/all_to_all | solution.py:595
  166.0 7.8 %scatter_columns.3 = bf16[5760,128]{1,0:T(8,128)(2,1)} custom-call(s32[16,128]{1,0:T(8,128)} %get-tuple-element.33.refs_0_, bf16[16,360,128]{2,1,0:T(8,128)(2,1)} %all-to-all-done.4.refs_1_), custom_call_target="tpu_custom_call" | custom-call | flops 3019898880 | bytes 5898240 | tf_op jit(solution)/shard_map/scatter_columns/pallas_call | solution.py:166
  (31 shorter events, 4.5 us)
Async XLA Ops:
  2.7 22.1 %all-to-all-start.1 = ((bf16[8,64,1280]{2,1,0:T(8,128)(2,1)}), bf16[8,64,1280]{2,1,0:T(8,128)(2,1)S(1)}, u32[]{:S(2)}, u32[]{:S(2)}) async-start(bf16[8,64,1280]{2,1,0:T(8,128)(2,1)} %broadcast_in_dim.19), calls=%async_computation.1 | async-start | bytes 2621440 | tf_op jit(solution)/shard_map/all_to_all | solution.py:595
  24.8 50.4 %copy-start = (bf16[8,64,1280]{2,1,0:T(8,128)(2,1)}, bf16[8,64,1280]{2,1,0:T(8,128)(2,1)S(1)}, u32[]{:S(2)}) copy-start(bf16[8,64,1280]{2,1,0:T(8,128)(2,1)S(1)} %all-to-all-done.1) | copy-start | bytes 3932164
  24.9 10.5 %copy-start.8 = (bf16[4,7,96,128]{3,2,1,0:T(8,128)(2,1)S(1)}, bf16[4,7,96,128]{3,2,1,0:T(8,128)(2,1)}, u32[]{:S(2)}) copy-start(bf16[4,7,96,128]{3,2,1,0:T(8,128)(2,1)} %get-tuple-element.29) | copy-start | bytes 2064388
  24.9 38.0 %all-to-all-start = ((bf16[16,360,128]{2,1,0:T(8,128)(2,1)}), bf16[16,360,128]{2,1,0:T(8,128)(2,1)}, u32[]{:S(2)}, u32[]{:S(2)}) async-start(bf16[16,360,128]{2,1,0:T(8,128)(2,1)} %get-tuple-element.28), calls=%async_computation | async-start | bytes 2949120 | tf_op jit(solution)/shard_map/all_to_all | solution.py:595
  33.1 11.0 %collective-permute-start.1 = (bf16[4,7,96,128]{3,2,1,0:T(8,128)(2,1)}, bf16[4,7,96,128]{3,2,1,0:T(8,128)(2,1)S(1)}, u32[]{:S(2)}, u32[]{:S(2)}) collective-permute-start(bf16[4,7,96,128]{3,2,1,0:T(8,128)(2,1)} %get-tuple-element.25), channel_id=1, source_target_pairs={{16,0},{32,16},{48,32},{64,48},{80,64},{96,80},{112,96},{17,1},{33... | collective-permute-start | bytes 2064392 | tf_op jit(solution)/shard_map/ppermute | solution.py:537
  35.3 12.3 %collective-permute-start = (bf16[4,7,96,128]{3,2,1,0:T(8,128)(2,1)S(1)}, bf16[4,7,96,128]{3,2,1,0:T(8,128)(2,1)S(1)}, u32[]{:S(2)}, u32[]{:S(2)}) collective-permute-start(bf16[4,7,96,128]{3,2,1,0:T(8,128)(2,1)S(1)} %copy-done.8), channel_id=1, source_target_pairs={{0,16},{16,32},{32,48},{48,64},{64,80},{80,96},{96,112},{1,17},{17... | collective-permute-start | bytes 2064392 | tf_op jit(solution)/shard_map/ppermute | solution.py:536
  44.1 3.5 %copy-start.1 = (bf16[4,7,96,128]{3,2,1,0:T(8,128)(2,1)}, bf16[4,7,96,128]{3,2,1,0:T(8,128)(2,1)S(1)}, u32[]{:S(2)}) copy-start(bf16[4,7,96,128]{3,2,1,0:T(8,128)(2,1)S(1)} %collective-permute-done.1.refs_5_) | copy-start | bytes 2064388
  47.6 0.9 copy-start.2
  62.9 7.1 %copy-start.5 = (bf16[768,128]{1,0:T(8,128)(2,1)S(1)}, bf16[768,128]{1,0:T(8,128)(2,1)}, u32[]{:S(2)}) copy-start(bf16[768,128]{1,0:T(8,128)(2,1)} %get-tuple-element.32.refs_6_) | copy-start | bytes 589828
  62.9 12.4 %copy-start.6 = (bf16[768,128]{1,0:T(8,128)(2,1)S(1)}, bf16[768,128]{1,0:T(8,128)(2,1)}, u32[]{:S(2)}) copy-start(bf16[768,128]{1,0:T(8,128)(2,1)} %get-tuple-element.36.refs_7_) | copy-start | bytes 589828
  62.9 47.5 %all-to-all-start.3 = ((bf16[16,360,128]{2,1,0:T(8,128)(2,1)}), bf16[16,360,128]{2,1,0:T(8,128)(2,1)S(1)}, u32[]{:S(2)}, u32[]{:S(2)}) async-start(bf16[16,360,128]{2,1,0:T(8,128)(2,1)} %gather_columns.1), calls=%async_computation.3 | async-start | bytes 2949120 | tf_op jit(solution)/shard_map/all_to_all | solution.py:595
  70.0 20.9 %collective-permute-start.3 = (bf16[768,128]{1,0:T(8,128)(2,1)S(1)}, bf16[768,128]{1,0:T(8,128)(2,1)S(1)}, u32[]{:S(2)}, u32[]{:S(2)}) collective-permute-start(bf16[768,128]{1,0:T(8,128)(2,1)S(1)} %copy-done.5), channel_id=1, source_target_pairs={{1,0},{2,1},{3,2},{4,3},{5,4},{6,5},{7,6},{8,7},{9,8},{10,9},{11,1... | collective-permute-start | bytes 589832 | tf_op jit(solution)/shard_map/ppermute | solution.py:562
  75.3 19.1 %collective-permute-start.2 = (bf16[768,128]{1,0:T(8,128)(2,1)S(1)}, bf16[768,128]{1,0:T(8,128)(2,1)}, u32[]{:S(2)}, u32[]{:S(2)}) collective-permute-start(bf16[768,128]{1,0:T(8,128)(2,1)S(1)} %copy-done.6), channel_id=1, source_target_pairs={{0,1},{1,2},{2,3},{3,4},{4,5},{5,6},{6,7},{7,8},{8,9},{9,10},{10,1... | collective-permute-start | bytes 589832 | tf_op jit(solution)/shard_map/ppermute | solution.py:561
  90.8 3.5 %copy-start.7 = (bf16[768,128]{1,0:T(8,128)(2,1)}, bf16[768,128]{1,0:T(8,128)(2,1)S(1)}, u32[]{:S(2)}) copy-start(bf16[768,128]{1,0:T(8,128)(2,1)S(1)} %collective-permute-done.3.refs_8_) | copy-start | bytes 589828
  110.4 1.1 copy-start.4
  111.5 25.7 %all-to-all-start.2 = ((bf16[16,360,128]{2,1,0:T(8,128)(2,1)}), bf16[16,360,128]{2,1,0:T(8,128)(2,1)S(1)}, u32[]{:S(2)}, u32[]{:S(2)}) async-start(bf16[16,360,128]{2,1,0:T(8,128)(2,1)} %get-tuple-element.35), calls=%async_computation.2 | async-start | bytes 2949120 | tf_op jit(solution)/shard_map/all_to_all | solution.py:595
  130.6 2.3 %collective-permute-start.4 = (bf16[4,64,1280]{2,1,0:T(8,128)(2,1)S(1)}, bf16[4,64,1280]{2,1,0:T(8,128)(2,1)}, u32[]{:S(2)}, u32[]{:S(2)}) collective-permute-start(bf16[4,64,1280]{2,1,0:T(8,128)(2,1)S(1)} %dynamic-slice_bitcast_fusion), channel_id=1, source_target_pairs={{0,16},{16,0},{32,48},{48,32},{64,80},{80,64},{96,112},{112,96},{1... | collective-permute-start | bytes 1966088 | tf_op jit(solution)/shard_map/ppermute | solution.py:604
  137.2 1.1 copy-start.3
  138.3 27.7 %all-to-all-start.4 = ((bf16[16,360,128]{2,1,0:T(8,128)(2,1)}), bf16[16,360,128]{2,1,0:T(8,128)(2,1)}, u32[]{:S(2)}, u32[]{:S(2)}) async-start(bf16[16,360,128]{2,1,0:T(8,128)(2,1)} %get-tuple-element.43), calls=%async_computation.4 | async-start | bytes 2949120 | tf_op jit(solution)/shard_map/all_to_all | solution.py:595
  142.9 14.5 %collective-permute-start.5 = (bf16[64,1280]{1,0:T(8,128)(2,1)S(1)}, bf16[64,1280]{1,0:T(8,128)(2,1)S(1)}, u32[]{:S(2)}, u32[]{:S(2)}) collective-permute-start(bf16[64,1280]{1,0:T(8,128)(2,1)S(1)} %get-tuple-element.47), channel_id=1, source_target_pairs={{0,32},{16,48},{32,64},{48,80},{64,96},{80,112},{96,0},{112,16},{1... | collective-permute-start | bytes 491528 | tf_op jit(solution)/shard_map/ppermute | solution.py:613
  145.4 12.0 %collective-permute-start.6 = (bf16[64,1280]{1,0:T(8,128)(2,1)S(1)}, bf16[64,1280]{1,0:T(8,128)(2,1)S(1)}, u32[]{:S(2)}, u32[]{:S(2)}) collective-permute-start(bf16[64,1280]{1,0:T(8,128)(2,1)S(1)} %get-tuple-element.49), channel_id=1, source_target_pairs={{0,64},{16,80},{32,96},{48,112},{64,0},{80,16},{96,32},{112,48},{1... | collective-permute-start | bytes 491528 | tf_op jit(solution)/shard_map/ppermute | solution.py:613
  145.4 12.0 %collective-permute-start.7 = (bf16[64,1280]{1,0:T(8,128)(2,1)S(1)}, bf16[64,1280]{1,0:T(8,128)(2,1)S(1)}, u32[]{:S(2)}, u32[]{:S(2)}) collective-permute-start(bf16[64,1280]{1,0:T(8,128)(2,1)S(1)} %get-tuple-element.48), channel_id=1, source_target_pairs={{0,96},{16,112},{32,0},{48,16},{64,32},{80,48},{96,64},{112,80},{1... | collective-permute-start | bytes 491528 | tf_op jit(solution)/shard_map/ppermute | solution.py:613

commit v2 on v1

--- a/solution.py
+++ b/solution.py
@@ -34,14 +34,26 @@
         out_ref[b] = got[:, b * LANE : (b + 1) * LANE]
 
 
-def gather_first_kernel(dest_ref, count_ref, cols_ref, src_ref, out_ref, table_ref, mat_ref, *, rows):
+def gather_first_kernel(dest_ref, count_ref, cols_ref, src_ref, out_ref, table_ref, mat_ref, full_ref, sems, *, rows):
+    feat = mat_ref.shape[0]
+
     @pl.when(pl.program_id(0) == 0)
     def _():
+        cuts = [(start, min(start + LANE, feat)) for start in range(0, feat, LANE)]
+        loads = []
+        for n, (start, stop) in enumerate(cuts):
+            at = pl.ds(start * rows, (stop - start) * rows)
+            loads.append(pltpu.make_async_copy(src_ref.at[at], full_ref.at[at], sems.at[n]))
+            loads[-1].start()
         slot = iota((1, LANE), 1)
         for b in range(cols_ref.shape[0]):
             row = jnp.where(slot < count_ref[0, 0, b], cols_ref[b], -1)
             table_ref[pl.ds(dest_ref[0, 0, b], 1), :] = row
-        rows_of_source(src_ref, mat_ref, rows)
+        for load, (start, stop) in zip(loads, cuts):
+            load.wait()
+            for r in range(rows):
+                part = full_ref[pl.ds(start * rows + r, stop - start, stride=rows), :]
+                mat_ref[start:stop, r * LANE : (r + 1) * LANE] = part.astype(BF16)
 
     gather_blocks(table_ref, mat_ref, out_ref)
 
@@ -69,7 +81,7 @@
 
 def gather_first(dest, count, cols, source, feat, rows):
     nblock = cols.shape[0]
-    once, out, shape, cost = gather_parts(source, nblock, feat, rows)
+    _, out, shape, cost = gather_parts(source, nblock, feat, rows)
     table = jax.ShapeDtypeStruct((nblock, LANE), jnp.int32)
 
     def kernel(*refs):
@@ -79,10 +91,14 @@
     return pl.pallas_call(
         kernel,
         grid=(nblock // WIDE,),
-        in_specs=[scalars, scalars, pl.BlockSpec(cols.shape, lambda i: (0, 0, 0)), once],
+        in_specs=[scalars, scalars, pl.BlockSpec(cols.shape, lambda i: (0, 0, 0)), pl.BlockSpec(memory_space=pl.ANY)],
         out_specs=[out, pl.BlockSpec(table.shape, lambda i: (0, 0))],
         out_shape=[shape, table],
-        scratch_shapes=[pltpu.VMEM((feat, rows * LANE), BF16)],
+        scratch_shapes=[
+            pltpu.VMEM((feat, rows * LANE), BF16),
+            pltpu.VMEM(source.shape, F32),
+            pltpu.SemaphoreType.DMA((pl.cdiv(feat, LANE),)),
+        ],
         cost_estimate=cost,
         name="gather_first",
     )(dest, count, cols, source)
@@ -107,17 +123,23 @@
     )(table, source)
 
 
-def scatter_rows(table_ref, blocks_ref, mat_ref, where_ref):
+def scatter_rows(table_ref, blocks_ref, mat_ref, where_ref, sems):
     nblock = blocks_ref.shape[0]
 
     @pl.when(pl.program_id(0) == 0)
     def _():
+        loads = []
+        for b in range(nblock):
+            to = mat_ref.at[:, pl.ds(b * LANE, LANE)]
+            loads.append(pltpu.make_async_copy(blocks_ref.at[b], to, sems.at[b]))
+            loads[-1].start()
         table = table_ref[...].astype(F32)
         by_slot = jnp.concatenate([table, jnp.zeros((LANE - nblock, LANE), F32)], axis=0).T
         for b in range(nblock):
-            mat_ref[:, b * LANE : (b + 1) * LANE] = blocks_ref[b]
             column = jnp.broadcast_to(by_slot[:, b : b + 1], (LANE, LANE))
             where_ref[b * LANE : (b + 1) * LANE, :] = column.astype(jnp.int32)
+        for load in loads:
+            load.wait()
 
     where = where_ref[...]
     lane = iota(where.shape, 1) + pl.program_id(0) * (WIDE * LANE)
@@ -125,15 +147,26 @@
     return jnp.dot(mat_ref[...], jnp.concatenate(hot, axis=1), preferred_element_type=F32)
 
 
-def scatter_add_kernel(table_ref, blocks_ref, base_ref, out_ref, mat_ref, where_ref, *, rows):
-    got = scatter_rows(table_ref, blocks_ref, mat_ref, where_ref)
+def scatter_add_kernel(table_ref, blocks_ref, base_ref, out_ref, mat_ref, where_ref, sems, full_ref, base_sem, *, rows):
+    load = pltpu.make_async_copy(base_ref, full_ref, base_sem)
+
+    @pl.when(pl.program_id(0) == 0)
+    def _():
+        load.start()
+
+    got = scatter_rows(table_ref, blocks_ref, mat_ref, where_ref, sems)
+
+    @pl.when(pl.program_id(0) == 0)
+    def _():
+        load.wait()
+
     for r in range(WIDE):
         at = pl.ds(pl.program_id(0) * WIDE + r, mat_ref.shape[0], stride=rows)
-        out_ref[at, :] = base_ref[at, :] + got[:, r * LANE : (r + 1) * LANE]
-
-
-def scatter_kernel(table_ref, blocks_ref, out_ref, mat_ref, where_ref, full_ref, *, rows):
-    got = scatter_rows(table_ref, blocks_ref, mat_ref, where_ref)
+        out_ref[at, :] = full_ref[at, :] + got[:, r * LANE : (r + 1) * LANE]
+
+
+def scatter_kernel(table_ref, blocks_ref, out_ref, mat_ref, where_ref, sems, full_ref, *, rows):
+    got = scatter_rows(table_ref, blocks_ref, mat_ref, where_ref, sems)
     for r in range(WIDE):
         at = pl.ds(pl.program_id(0) * WIDE + r, mat_ref.shape[0], stride=rows)
         full_ref[at, :] = got[:, r * LANE : (r + 1) * LANE]
@@ -147,18 +180,20 @@
     nblock, feat, length = blocks.shape
     nslot = nblock * length
     shape = (feat * rows, LANE)
-    whole = pl.BlockSpec(shape, lambda i: (0, 0), pipeline_mode=pl.Buffered(1))
-    specs = [
-        pl.BlockSpec(table.shape, lambda i: (0, 0)),
-        pl.BlockSpec(blocks.shape, lambda i: (0, 0, 0), pipeline_mode=pl.Buffered(1)),
+    in_place = pl.BlockSpec(memory_space=pl.ANY)
+    specs = [pl.BlockSpec(table.shape, lambda i: (0, 0)), in_place]
+    scratch = [
+        pltpu.VMEM((feat, nslot), BF16),
+        pltpu.VMEM((nslot, LANE), jnp.int32),
+        pltpu.SemaphoreType.DMA((nblock,)),
+        pltpu.VMEM(shape, F32),
     ]
-    scratch = [pltpu.VMEM((feat, nslot), BF16), pltpu.VMEM((nslot, LANE), jnp.int32)]
     if base is None:
         body, operands, dtype = scatter_kernel, (table, blocks), BF16
-        scratch.append(pltpu.VMEM(shape, F32))
     else:
         body, operands, dtype = scatter_add_kernel, (table, blocks, base), F32
-        specs.append(whole)
+        specs.append(in_place)
+        scratch.append(pltpu.SemaphoreType.DMA)
 
     def kernel(*refs):
         body(*refs, rows=rows)
@@ -195,25 +230,48 @@
     return lax.dot_general(a, b, (((1,), (1,)), ((), ())), preferred_element_type=F32)
 
 
-def forward_kernel(x_ref, wt_ref, w_ref, tend_ref, a1_ref, a2_ref, *, cuts):
+def place_weights(at_ref, piece_refs, w_t_ref, w_ref, parts):
+    chips = len(piece_refs)
+    size = piece_refs[0].shape[0] // 2
+    for n, piece in enumerate(piece_refs):
+        chip = (at_ref[0] + (chips - n)) % chips
+        for half in range(2):
+            core = at_ref[1] if half == 0 else 1 - at_ref[1]
+            at = pl.multiple_of((2 * chip + core) * size, size)
+            w_t_ref[pl.ds(at, size), :] = piece[half * size : (half + 1) * size, :]
+    row = 0
+    for start, stop in parts:
+        w_ref[row : row + stop - start, :] = w_t_ref[:, start:stop].T
+        row += stop - start
+
+
+def forward_kernel(at_ref, x_ref, *refs, cuts):
+    *piece_refs, tend_ref, a1_ref, a2_ref, w_t_ref, w_ref = refs
     (in0, in1), (mid0, mid1), (out0, out1) = cuts
+
+    @pl.when(pl.program_id(0) == 0)
+    def _():
+        place_weights(at_ref, piece_refs, w_t_ref, w_ref, [(out0, w_t_ref.shape[1])])
+
     _, _, xn = normalised(wide(x_ref))
-    a_one = mul(wt_ref[:, in0:in1], xn)
+    a_one = mul(w_t_ref[:, in0:in1], xn)
     a1_ref[...] = a_one
     h_one = (a_one * jax.nn.sigmoid(a_one)).astype(BF16)
-    a_two = mul(wt_ref[:, mid0:mid1], h_one)
+    a_two = mul(w_t_ref[:, mid0:mid1], h_one)
     a2_ref[...] = a_two
     h_two = (a_two * jax.nn.sigmoid(a_two)).astype(BF16)
-    tend = mul(w_ref[out0:out1, :], h_two).astype(BF16)
+    tend = mul(w_ref[: out1 - out0, :], h_two).astype(BF16)
     for b in range(x_ref.shape[0]):
         tend_ref[b] = tend[:, b * LANE : (b + 1) * LANE]
 
 
-def backward_kernel(x_ref, g_ref, a1_ref, a2_ref, wt_ref, w_ref, adj_ref, grad_ref, sum_ref, *, cuts):
+def backward_kernel(at_ref, x_ref, g_ref, a1_ref, a2_ref, *refs, cuts):
+    *piece_refs, adj_ref, grad_ref, w_t_ref, w_ref, sum_ref = refs
     (in0, in1), (mid0, mid1), (out0, out1) = cuts
 
     @pl.when(pl.program_id(0) == 0)
     def _():
+        place_weights(at_ref, piece_refs, w_t_ref, w_ref, [(0, out0)])
         sum_ref[...] = jnp.zeros_like(sum_ref)
 
     xf, scale, xn = normalised(wide(x_ref))
@@ -221,7 +279,7 @@
     a_two = a2_ref[...]
     sig = jax.nn.sigmoid(a_two)
     h_two = (a_two * sig).astype(BF16)
-    d_two = (mul(wt_ref[:, out0:out1], g) * (sig * (1.0 + a_two * (1.0 - sig)))).astype(BF16)
+    d_two = (mul(w_t_ref[:, out0:out1], g) * (sig * (1.0 + a_two * (1.0 - sig)))).astype(BF16)
     sum_ref[:, out0:out1] += mul_slots(h_two, g)
     a_one = a1_ref[...]
     sig = jax.nn.sigmoid(a_one)
@@ -241,20 +299,19 @@
         grad_ref[...] = sum_ref[...].astype(BF16)
 
 
-def column_specs(shape, pair, hid, span):
+def column_specs(shape, pieces):
     _, feat, length = shape
-    block = pl.BlockSpec((pair, feat, length), lambda i: (i, 0, 0))
-    hidden = pl.BlockSpec((hid, pair * length), lambda i: (0, i))
-    w_t = pl.BlockSpec((hid, span), lambda i: (0, 0), pipeline_mode=pl.Buffered(1))
-    w = pl.BlockSpec((span, hid), lambda i: (0, 0), pipeline_mode=pl.Buffered(1))
-    return block, hidden, w_t, w
-
-
-def physics_forward(x, w_t, w, cuts):
+    rows, span = pieces[0].shape
+    hid = rows * len(pieces)
+    block = pl.BlockSpec((WIDE, feat, length), lambda i: (i, 0, 0))
+    hidden = pl.BlockSpec((hid, WIDE * length), lambda i: (0, i))
+    piece = pl.BlockSpec((rows, span), lambda i: (0, 0), pipeline_mode=pl.Buffered(1))
+    return hid, span, block, hidden, [piece] * len(pieces)
+
+
+def physics_forward(at, x, pieces, cuts):
     nblock, feat, length = x.shape
-    hid, span = w_t.shape
-    pair = WIDE
-    block, hidden, spec_t, spec = column_specs(x.shape, pair, hid, span)
+    hid, span, block, hidden, piece_specs = column_specs(x.shape, pieces)
 
     def kernel(*refs):
         forward_kernel(*refs, cuts=cuts)
@@ -262,42 +319,45 @@
     kept = jax.ShapeDtypeStruct((hid, nblock * length), F32)
     return pl.pallas_call(
         kernel,
-        grid=(nblock // pair,),
-        in_specs=[block, spec_t, spec],
+        grid=(nblock // WIDE,),
+        in_specs=[pl.BlockSpec(memory_space=pltpu.SMEM), block] + piece_specs,
         out_specs=[block, hidden, hidden],
         out_shape=[jax.ShapeDtypeStruct(x.shape, BF16), kept, kept],
+        scratch_shapes=[pltpu.VMEM((hid, span), BF16), pltpu.VMEM((span - cuts[2][0], hid), BF16)],
         cost_estimate=pl.CostEstimate(
             flops=2 * hid * (2 * feat + hid) * nblock * length,
             transcendentals=4 * hid * nblock * length,
             bytes_accessed=x.size * 4 + hid * nblock * length * 8,
         ),
         name="physics_forward",
-    )(x, w_t, w)
-
-
-def physics_backward(x, g, a_one, a_two, w_t, w, cuts):
+    )(at, x, *pieces)
+
+
+def physics_backward(at, x, g, a_one, a_two, pieces, cuts):
     nblock, feat, length = x.shape
-    hid, span = w_t.shape
-    pair = WIDE
-    block, hidden, spec_t, spec = column_specs(x.shape, pair, hid, span)
+    hid, span, block, hidden, piece_specs = column_specs(x.shape, pieces)
 
     def kernel(*refs):
         backward_kernel(*refs, cuts=cuts)
 
     return pl.pallas_call(
         kernel,
-        grid=(nblock // pair,),
-        in_specs=[block, block, hidden, hidden, spec_t, spec],
+        grid=(nblock // WIDE,),
+        in_specs=[pl.BlockSpec(memory_space=pltpu.SMEM), block, block, hidden, hidden] + piece_specs,
         out_specs=[block, pl.BlockSpec((hid, span), lambda i: (0, 0))],
         out_shape=[jax.ShapeDtypeStruct(x.shape, BF16), jax.ShapeDtypeStruct((hid, span), BF16)],
-        scratch_shapes=[pltpu.VMEM((hid, span), F32)],
+        scratch_shapes=[
+            pltpu.VMEM((hid, span), BF16),
+            pltpu.VMEM((cuts[2][0], hid), BF16),
+            pltpu.VMEM((hid, span), F32),
+        ],
         cost_estimate=pl.CostEstimate(
             flops=4 * hid * (2 * feat + hid) * nblock * length,
             transcendentals=4 * hid * nblock * length,
             bytes_accessed=x.size * 6 + hid * nblock * length * 8,
         ),
         name="physics_backward",
-    )(x, g, a_one, a_two, w_t, w)
+    )(at, x, g, a_one, a_two, *pieces)
 
 
 def plane(fields_ref, coef_refs, a, at):
@@ -394,6 +454,7 @@
     shift_ref,
     *,
     rows,
+    first,
 ):
     coefs = (lon_ref, lat_ref, dif_ref)
     nfield = fields_ref.shape[0]
@@ -406,7 +467,7 @@
     k, n = iota(shape, 0), iota(shape, 1)
     lane, kind, m = k % LANE, n // LANE, n % LANE
     row_code = (k // LANE) * STEPS + lane % STEPS + 16 * ((lane // STEPS) % 8)
-    row_code = jnp.where(lane // GROUP == pl.program_id(0), row_code, -1)
+    row_code = jnp.where(lane // GROUP == pl.program_id(0) + first, row_code, -1)
     col_code = jnp.where(kind == 0, m, m % 16 + 16 * (nfield - 1 + kind))
     col_code = jnp.where(m < 16 * nfield, col_code, -2)
     pick = jnp.where(row_code == col_code, 1.0, 0.0).astype(BF16)
@@ -421,7 +482,8 @@
         shift_ref[...] = jnp.where(((n == east) & (k > 0)) | (n == west), 1.0, 0.0).astype(BF16)
 
     part = LEVELS
-    field_of_lane = iota((part, LANE), 1) // 16
+    lane = iota((part, LANE), 1)
+    of_field = [jnp.where(lane // 16 == f, 1.0, 0.0).astype(BF16) for f in range(nfield)]
 
     def levels(sub, carry):
         def cell(a, t):
@@ -447,8 +509,9 @@
         for step in range(STEPS):
             inner = range(step + 1, total - 1 - step)
             for t in inner:
+                narrow = state[t].astype(BF16)
                 for f in range(nfield):
-                    join_ref[step, f, t * part : (t + 1) * part] = jnp.where(field_of_lane == f, state[t], 0.0).astype(BF16)
+                    join_ref[step, f, t * part : (t + 1) * part] = narrow * of_field[f]
             if step < STEPS - 1:
                 state = {
                     t: stepped(
@@ -479,22 +542,23 @@
             if turn + 1 < len(turns):
                 ready = neighbours(*turns[turn + 1])
             size = (total - 2 - 2 * step) * part
-            coef = [coef_ref[0, c, rows_of(step)] for c in range(5)]
-            for n, f in enumerate(pair):
-                cur = step % 2
-                value = stepped(
-                    coef,
-                    state_ref[cur, f, rows_of(step)],
-                    sides[n * size : (n + 1) * size, :LANE],
-                    sides[n * size : (n + 1) * size, LANE:],
-                    state_ref[cur, f, rows_of(step, 1)],
-                    state_ref[cur, f, rows_of(step, -1)],
-                )
-                if step < STEPS - 1:
-                    state_ref[1 - cur, f, rows_of(step)] = value
-                    continue
-                for r in range(rows):
-                    out_ref[f, pl.ds(sub * (part * rows) + r, part, stride=rows), :] = value[r * part : (r + 1) * part]
+            cur = step % 2
+            for u in range(step + 1, total - 1 - step):
+                at, side = slice(u * part, (u + 1) * part), (u - step - 1) * part
+                coef = [coef_ref[0, c, at] for c in range(5)]
+                for n, f in enumerate(pair):
+                    value = stepped(
+                        coef,
+                        state_ref[cur, f, at],
+                        sides[n * size + side : n * size + side + part, :LANE],
+                        sides[n * size + side : n * size + side + part, LANE:],
+                        state_ref[cur, f, (u + 1) * part : (u + 2) * part],
+                        state_ref[cur, f, (u - 1) * part : u * part],
+                    )
+                    if step < STEPS - 1:
+                        state_ref[1 - cur, f, at] = value
+                    else:
+                        out_ref[f, pl.ds(sub * (part * rows) + u - STEPS, part, stride=rows), :] = value
         return carry
 
     lax.fori_loop(0, GROUP // part, levels, 0)
@@ -517,7 +581,7 @@
         self.strip_spec = pl.BlockSpec((self.strip_rows, LANE), lambda i: (0, 0))
         self.strip_shape = jax.ShapeDtypeStruct((self.strip_rows, LANE), BF16)
 
-    def rims(self):
+    def rims(self, start):
         def kernel(*refs):
             rim_kernel(*refs, rows=self.rows, levels=self.levels)
 
@@ -528,7 +592,7 @@
             out_specs=[self.rim_spec, self.rim_spec],
             out_shape=[self.rim_shape, self.rim_shape],
             name="rims",
-        )(*self.args)
+        )(self.args[0], *after(self.args[1:], start))
 
     def send_rims(self, low, high):
         size = lax.axis_size("lat")
@@ -562,29 +626,47 @@
         from_e = lax.ppermute(own_w, "lon", [(j, i) for i, j in around])
         return from_w, from_e
 
-    def steps(self, south, north, own_w, own_e, from_w, from_e, start):
+    def steps(self, first, count, rims, strips, start, state=None):
         def kernel(*refs):
-            dynamics_kernel(*refs, rows=self.rows)
+            inputs = refs[:10]
+            dynamics_kernel(*inputs, *refs[10 + (state is not None) :], rows=self.rows, first=first)
 
         fields = self.args[0]
-        from_w, from_e = after((from_w, from_e), start)
+        nfield = fields.shape[0]
+        chunk = GROUP * self.rows
+        fields_spec = pl.BlockSpec((nfield, chunk, LANE), lambda i: (0, i + first, 0))
+        coef_spec = pl.BlockSpec((chunk, LANE), lambda i: (i + first, 0))
+        rim_spec = pl.BlockSpec((STEPS, self.planes, GROUP, LANE), lambda i: (0, 0, i + first, 0))
+        specs = [fields_spec] + [coef_spec] * 3 + [rim_spec] * 2 + [self.strip_spec] * 4
+        operands = self.args + rims + after(strips, start)
+        aliases = {}
+        if state is not None:
+            specs.append(pl.BlockSpec(memory_space=pl.ANY))
+            aliases = {len(operands): 0}
+            operands += (state,)
+        cells = (self.rows + 2 * STEPS) * LEVELS
         return pl.pallas_call(
             kernel,
-            grid=self.grid,
-            in_specs=self.arg_specs + [self.rim_spec, self.rim_spec] + [self.strip_spec] * 4,
-            out_specs=self.fields_spec,
+            grid=(count,),
+            in_specs=specs,
+            out_specs=fields_spec,
             out_shape=jax.ShapeDtypeStruct(fields.shape, F32),
+            input_output_aliases=aliases,
             scratch_shapes=[
                 pltpu.VMEM((2, STEPS, self.planes, GROUP, LANE), F32),
                 pltpu.VMEM((self.strip_rows, 4 * LANE), F32),
-                pltpu.VMEM((2, 5, (self.rows + 2 * STEPS) * LEVELS, LANE), F32),
-                pltpu.VMEM((STEPS, fields.shape[0], (self.rows + 2 * STEPS) * LEVELS, LANE), BF16),
-                pltpu.VMEM((2, fields.shape[0], (self.rows + 2 * STEPS) * LEVELS, LANE), F32),
+                pltpu.VMEM((2, 5, cells, LANE), F32),
+                pltpu.VMEM((STEPS, nfield, cells, LANE), BF16),
+                pltpu.VMEM((2, nfield, cells, LANE), F32),
                 pltpu.VMEM((2 * LANE, 2 * LANE), BF16),
             ],
-            cost_estimate=pl.CostEstimate(flops=fields.size * 60, transcendentals=0, bytes_accessed=fields.size * 11),
+            cost_estimate=pl.CostEstimate(
+                flops=fields.size * 60 * count // self.grid[0],
+                transcendentals=0,
+                bytes_accessed=fields.size * 11 * count // self.grid[0],
+            ),
             name="dynamics",
-        )(*self.args, south, north, own_w, own_e, from_e, from_w)
+        )(*operands)
 
 
 def after(values, start):
@@ -595,7 +677,17 @@
     return lax.all_to_all(array, axis, split_axis=0, concat_axis=0, tiled=True)
 
 
-def scattered(parts):
+def spread(piece):
+    size = lax.axis_size("lat")
+    other = lax.ppermute(piece, "lat", [(i, i ^ 1) for i in range(size)])
+    both = jnp.concatenate([piece, other], axis=0)
+    pieces = [both]
+    for shift in range(1, size // 2):
+        pieces.append(lax.ppermute(both, "lat", [(i, (i + 2 * shift) % size) for i in range(size)]))
+    return pieces
+
+
+def scattered(parts, start):
     size = parts.shape[0]
     core = lax.axis_index("lat") % 2
     pairs = parts.reshape((size // 2, 2) + parts.shape[1:])
@@ -606,7 +698,7 @@
     chips = size // 2
     chip = lax.axis_index("lat") // 2
     total = lax.dynamic_index_in_dim(both, chip, 0, keepdims=False)
-    both = both.astype(BF16)
+    both = after(both.astype(BF16), start)
     for shift in range(1, chips):
         part = lax.dynamic_index_in_dim(both, (chip + shift) % chips, 0, keepdims=False)
         to = [(i, (i + 2 * shift) % size) for i in range(size)]
@@ -639,29 +731,33 @@
     )
     span = cuts[2][1] + pad
 
+    coefs = [c.reshape(levels * rows, columns) for c in (courant_lon, courant_lat, diffusion)]
+    window = Dynamics(fields.reshape(nfield, levels * rows, columns), coefs, rows, levels)
+
+    nblock = block_dest.shape[-1]
+    cols = col_list.reshape(nblock, 1, LANE)
+    send_x, table = gather_first(block_dest, block_count, cols, fields.reshape(feat * rows, columns), feat, rows)
+    recv_x = exchange(send_x, "lon")
     rest = jnp.zeros((pad, hid_own), BF16)
     own = jnp.concatenate([w_in[0], rest, w_mid[0], w_out[0], rest], axis=0).T
-    w_t = exchange(jnp.broadcast_to(own[None], (nlat,) + own.shape), "lat").reshape(nlat * hid_own, span)
-    w = w_t.T
-    coefs = [c.reshape(levels * rows, columns) for c in (courant_lon, courant_lat, diffusion)]
-    window = Dynamics(fields.reshape(nfield, levels * rows, columns), coefs, rows, levels)
-
-    nblock = block_dest.shape[-1]
-    low, high = window.rims()
+    pieces = spread(after(own, send_x))
+    lat = lax.axis_index("lat")
+    at = jnp.stack([lat // 2, lat % 2]).astype(jnp.int32)
+    low, high = window.rims(send_x)
     south, north = window.send_rims(low, high)
-    cols = after(col_list.reshape(nblock, 1, LANE), low)
-    send_x, table = gather_first(block_dest, block_count, cols, fields.reshape(feat * rows, columns), feat, rows)
-    recv_x = exchange(send_x, "lon")
-    own_w, own_e = window.strips(south, north, send_x)
-    send_g = gather_columns(after(table, own_w), tend_cot.reshape(feat * rows, columns), feat, rows)
+    send_g = gather_columns(after(table, low), tend_cot.reshape(feat * rows, columns), feat, rows)
     recv_g = exchange(send_g, "lon")
+    own_w, own_e = window.strips(south, north, send_g)
     from_w, from_e = window.send_strips(own_w, own_e)
-    tend, a_one, a_two = physics_forward(after(recv_x, send_g), w_t, w, cuts)
+    tend, a_one, a_two = physics_forward(at, after(recv_x, own_w), pieces, cuts)
     back_tend = exchange(tend, "lon")
-    state = window.steps(south, north, own_w, own_e, from_w, from_e, tend)
-    adj, grads = physics_backward(recv_x, after(recv_g, state), a_one, a_two, w_t, w, cuts)
+    adj, grads = physics_backward(at, recv_x, recv_g, a_one, a_two, pieces, cuts)
+    rims, strips = (south, north), (own_w, own_e, from_e, from_w)
+    last = window.grid[0] - 1
+    state = window.steps(last, 1, rims, strips, adj)
     back_adj = exchange(after(adj, back_tend), "lon")
-    summed = scattered(grads.reshape(nlat, hid_own, span)).T
+    state = window.steps(0, last, rims, strips, back_tend, state)
+    summed = scattered(grads.reshape(nlat, hid_own, span), back_tend).T
     grad_in, grad_mid, grad_out = (summed[a:b][None] for a, b in cuts)
 
     new_fields = scatter_columns(table, back_tend, rows, state.reshape(feat * rows, columns))

time: 175 us -> 169 us (0.966)
  the two profiles are of different devices: /device:TPU:2 before, /device:TPU:8 now
where the time goes in v2:
time: 169 us; the launch traced here: 168 us
  Pallas kernels  83 us (49%)
  starting transfers between devices  50.5 us (30%)
  waiting for transfers between devices  23.1 us (14%)
  local copies, waits for them, and re-layouts  8.38 us (5%)
  other arithmetic  2.13 us (1%)
    all_to_all x4, starting transfers between devices, exchange(): return lax.all_to_all(array, axis, split_axis=0, concat_axis=0, tiled=True)  30.4 us
    pallas_call x2, Pallas kernels, scatter_columns(): pl.pallas_call(kernel, grid=(rows // WIDE,), in_specs=specs, out_specs=pl...  18.4 us
    pallas_call x2, Pallas kernels, steps(): pl.pallas_call(kernel, grid=(count,), in_specs=specs, out_specs=fields_sp...  17.7 us
    pallas_call x1, Pallas kernels, physics_backward(): pl.pallas_call(kernel, grid=(nblock // WIDE,), in_specs=[pl.BlockSpec(mem...  12.9 us
    all_to_all x4, waiting for transfers between devices, exchange(): return lax.all_to_all(array, axis, split_axis=0, concat_axis=0, tiled=True)  8.2 us
    pallas_call x1, Pallas kernels, gather_first(): pl.pallas_call(kernel, grid=(nblock // WIDE,), in_specs=[scalars, scalars...  7.77 us
    pallas_call x1, Pallas kernels, gather_columns(): pl.pallas_call(kernel, grid=(nblock // WIDE,), in_specs=[pl.BlockSpec(tab...  7.51 us
    pallas_call x1, Pallas kernels, physics_forward(): pl.pallas_call(kernel, grid=(nblock // WIDE,), in_specs=[pl.BlockSpec(mem...  7.22 us
  transfers between devices with their start and end apart: 16, of which 6 were waited for; matrix products, arithmetic and copies ran while one was open for 3% of the time, Pallas kernels for 40%

profile of v2, /device:TPU:8, one launch (start us, length us, event | category | flops | bytes accessed | tf_op | source)
XLA Modules:
  0.0 168.1 jit_solution(513161184499334094)
XLA Ops:
  0.6 7.8 %gather_first.1 = (bf16[16,360,128]{2,1,0:T(8,128)(2,1)}, s32[16,128]{1,0:T(8,128)}) custom-call(s32[1,1,16]{2,1,0:T(1,128)} %refs_0_.1, s32[1,1,16]{2,1,0:T(1,128)} %refs_1_.1, s32[16,1,128]{2,1,0:T(1,128)} %bitcast.71, f32[5760,128]{1,0:T(8,128)} %bitcast.45), custom_call_target="tpu_custom_call" | custom-call | flops 3019898880 | bytes 4423680 | tf_op jit(solution)/shard_map/gather_first/pallas_call | solution.py:91
  8.4 8.4 %all-to-all-start = ((bf16[16,360,128]{2,1,0:T(8,128)(2,1)}), bf16[16,360,128]{2,1,0:T(8,128)(2,1)S(1)}, u32[]{:S(2)}, u32[]{:S(2)}) async-start(bf16[16,360,128]{2,1,0:T(8,128)(2,1)} %get-tuple-element.35), calls=%async_computation | async-start | bytes 2949120 | tf_op jit(solution)/shard_map/all_to_all | solution.py:677
  16.8 4.5 %rims.1 = (bf16[4,7,96,128]{3,2,1,0:T(8,128)(2,1)}, bf16[4,7,96,128]{3,2,1,0:T(8,128)(2,1)}) custom-call(f32[4,1440,128]{2,1,0:T(8,128)} %bitcast.46, f32[1440,128]{1,0:T(8,128)} %bitcast.50, f32[1440,128]{1,0:T(8,128)} %bitcast.54, f32[1440,128]{1,0:T(8,128)} %bitcast.58), custom_call_target="tpu_custom_call" | custom-call | tf_op jit(solution)/shard_map/rims/pallas_call | solution.py:588
  21.3 7.5 %gather_columns.1 = bf16[16,360,128]{2,1,0:T(8,128)(2,1)} custom-call(s32[16,128]{1,0:T(8,128)} %get-tuple-element.41.refs_0_, bf16[5760,128]{1,0:T(8,128)(2,1)} %bitcast.70), custom_call_target="tpu_custom_call" | custom-call | flops 3019898880 | bytes 2949120 | tf_op jit(solution)/shard_map/gather_columns/pallas_call | solution.py:114
  28.9 8.2 %all-to-all-done.refs_1_ = bf16[16,360,128]{2,1,0:T(8,128)(2,1)S(1)} async-done(((bf16[16,360,128]{2,1,0:T(8,128)(2,1)}), bf16[16,360,128]{2,1,0:T(8,128)(2,1)S(1)}, u32[]{:S(2)}, u32[]{:S(2)}) %all-to-all-start) | async-done | bytes 1474592 | tf_op jit(solution)/shard_map/all_to_all | solution.py:677
  37.1 1.1 copy-done.3
  38.2 6.7 %all-to-all-start.2 = ((bf16[16,360,128]{2,1,0:T(8,128)(2,1)}), bf16[16,360,128]{2,1,0:T(8,128)(2,1)}, u32[]{:S(2)}, u32[]{:S(2)}) async-start(bf16[16,360,128]{2,1,0:T(8,128)(2,1)} %gather_columns.1), calls=%async_computation.2 | async-start | bytes 2949120 | tf_op jit(solution)/shard_map/all_to_all | solution.py:677
  44.9 1.3 collective-permute-start.1
  46.1 3.1 %collective-permute-start = (bf16[4,7,96,128]{3,2,1,0:T(8,128)(2,1)S(1)}, bf16[4,7,96,128]{3,2,1,0:T(8,128)(2,1)S(1)}, u32[]{:S(2)}, u32[]{:S(2)}) collective-permute-start(bf16[4,7,96,128]{3,2,1,0:T(8,128)(2,1)S(1)} %copy-done.12), channel_id=1, source_target_pairs={{0,16},{16,32},{32,48},{48,64},{64,80},{80,96},{96,112},{1,17},{17... | collective-permute-start | bytes 2064392 | tf_op jit(solution)/shard_map/ppermute | solution.py:600
  49.4 1.1 collective-permute-start.2
  50.5 1.0 collective-permute-done.2
  51.6 1.6 collective-permute-start.3
  53.1 2.4 %collective-permute-start.4 = (bf16[128,1280]{1,0:T(8,128)(2,1)S(1)}, bf16[128,1280]{1,0:T(8,128)(2,1)S(1)}, u32[]{:S(2)}, u32[]{:S(2)}) collective-permute-start(bf16[128,1280]{1,0:T(8,128)(2,1)S(1)} %constant_dynamic-update-slice_fusion.refs_2_.refs_5_), channel_id=1, source_target_pairs={{0,64},{16,80},{32,96},{48,112},{64,0},{80,16},{96,32},{112,48},{1... | collective-permute-start | bytes 983048 | tf_op jit(solution)/shard_map/ppermute | solution.py:686
  55.5 1.5 collective-permute-start.5
  59.3 6.9 %strips.1 = (bf16[768,128]{1,0:T(8,128)(2,1)}, bf16[768,128]{1,0:T(8,128)(2,1)}) custom-call(f32[4,1440,128]{2,1,0:T(8,128)} %bitcast.47, f32[1440,128]{1,0:T(8,128)} %bitcast.51, f32[1440,128]{1,0:T(8,128)} %bitcast.55, f32[1440,128]{1,0:T(8,128)} %bitcast.59, bf16[4,7,96,128]{3,2,1,0:T(8,128)(2,1)} %copy-done.1, bf16[4,7,96,128]{3,2,1,0:T(8,128)(2,1)} %copy-done), custom_call_target="tpu_custom_call" | custom-call | tf_op jit(solution)/shard_map/strips/pallas_call | solution.py:609
  66.3 4.9 %collective-permute-done.4.refs_4_.refs_7_ = bf16[128,1280]{1,0:T(8,128)(2,1)S(1)} collective-permute-done((bf16[128,1280]{1,0:T(8,128)(2,1)S(1)}, bf16[128,1280]{1,0:T(8,128)(2,1)S(1)}, u32[]{:S(2)}, u32[]{:S(2)}) %collective-permute-start.4) | collective-permute-done | bytes 327712 | tf_op jit(solution)/shard_map/ppermute | solution.py:686
  72.6 7.2 %physics_forward.1 = (bf16[16,360,128]{2,1,0:T(8,128)(2,1)}, f32[512,2048]{1,0:T(8,128)}, f32[512,2048]{1,0:T(8,128)}) custom-call(s32[2]{0:T(128)} %pad_add_fusion.refs_0_, bf16[16,360,128]{2,1,0:T(8,128)(2,1)} %copy-done.3, bf16[128,1280]{1,0:T(8,128)(2,1)} %copy-done.8, bf16[128,1280]{1,0:T(8,128)(2,1)} %copy-done.13, bf16[128,1280]{1,0:T(8,128)(2,1)} %copy-done.14, ...), custom_call_target="tpu_custom_call" | custom-call | flops 2583691264 | bytes 11337728 | tf_op jit(solution)/shard_map/physics_forward/pallas_call | solution.py:320
  79.8 7.3 %all-to-all-start.1 = ((bf16[16,360,128]{2,1,0:T(8,128)(2,1)}), bf16[16,360,128]{2,1,0:T(8,128)(2,1)S(1)}, u32[]{:S(2)}, u32[]{:S(2)}) async-start(bf16[16,360,128]{2,1,0:T(8,128)(2,1)} %get-tuple-element.47), calls=%async_computation.1 | async-start | bytes 2949120 | tf_op jit(solution)/shard_map/all_to_all | solution.py:677
  87.1 12.9 %physics_backward.1 = (bf16[16,360,128]{2,1,0:T(8,128)(2,1)}, bf16[512,1280]{1,0:T(8,128)(2,1)}) custom-call(s32[2]{0:T(128)} %pad_add_fusion.refs_0_, bf16[16,360,128]{2,1,0:T(8,128)(2,1)} %copy-done.3, bf16[16,360,128]{2,1,0:T(8,128)(2,1)} %all-to-all-done.2.refs_2_, f32[512,2048]{1,0:T(8,128)} %get-tuple-element.53.refs_3_, ...), custom_call_target="tpu_custom_call" | custom-call | flops 5167382528 | bytes 12812288 | tf_op jit(solution)/shard_map/physics_backward/pallas_call | solution.py:343
  100.0 1.1 dynamic-slice_bitcast_fusion
  101.1 3.5 %collective-permute-start.8 = (bf16[4,64,1280]{2,1,0:T(8,128)(2,1)S(1)}, bf16[4,64,1280]{2,1,0:T(8,128)(2,1)}, u32[]{:S(2)}, u32[]{:S(2)}) collective-permute-start(bf16[4,64,1280]{2,1,0:T(8,128)(2,1)S(1)} %dynamic-slice_bitcast_fusion), channel_id=1, source_target_pairs={{0,16},{16,0},{32,48},{48,32},{64,80},{80,64},{96,112},{112,96},{1... | collective-permute-start | bytes 1966088 | tf_op jit(solution)/shard_map/ppermute | solution.py:696
  104.6 2.7 %collective-permute-start.6 = (bf16[768,128]{1,0:T(8,128)(2,1)S(1)}, bf16[768,128]{1,0:T(8,128)(2,1)S(1)}, u32[]{:S(2)}, u32[]{:S(2)}) collective-permute-start(bf16[768,128]{1,0:T(8,128)(2,1)S(1)} %copy-done.4), channel_id=1, source_target_pairs={{1,0},{2,1},{3,2},{4,3},{5,4},{6,5},{7,6},{8,7},{9,8},{10,9},{11,1... | collective-permute-start | bytes 589832 | tf_op jit(solution)/shard_map/ppermute | solution.py:626
  107.3 4.4 %collective-permute-done.6.refs_8_ = bf16[768,128]{1,0:T(8,128)(2,1)S(1)} collective-permute-done((bf16[768,128]{1,0:T(8,128)(2,1)S(1)}, bf16[768,128]{1,0:T(8,128)(2,1)S(1)}, u32[]{:S(2)}, u32[]{:S(2)}) %collective-permute-start.6) | collective-permute-done | bytes 196640 | tf_op jit(solution)/shard_map/ppermute | solution.py:626
  111.7 4.3 %collective-permute-done.7.refs_9_ = bf16[768,128]{1,0:T(8,128)(2,1)S(1)} collective-permute-done((bf16[768,128]{1,0:T(8,128)(2,1)S(1)}, bf16[768,128]{1,0:T(8,128)(2,1)S(1)}, u32[]{:S(2)}, u32[]{:S(2)}) %collective-permute-start.7) | collective-permute-done | bytes 196640 | tf_op jit(solution)/shard_map/ppermute | solution.py:625
  116.7 6.7 %dynamics.2.refs_10_ = f32[4,1440,128]{2,1,0:T(8,128)} custom-call(f32[4,1440,128]{2,1,0:T(8,128)} %bitcast.48, f32[1440,128]{1,0:T(8,128)} %bitcast.52, f32[1440,128]{1,0:T(8,128)} %bitcast.56, f32[1440,128]{1,0:T(8,128)} %bitcast.60, bf16[4,7,96,128]{3,2,1,0:T(8,128)(2,1)} %copy-done.1, bf16[4,7,96,128]{3,2,1,0:T(8,128)(2,1)} %copy-done, ...), custom_call_target="tpu_custom_call" | custom-call | flops 14745600 | bytes 2703360 | tf_op jit(solution)/shard_map/dynamics/pallas_call | solution.py:648
  123.4 1.5 fusion.3
  124.9 1.1 copy-done.2
  126.0 8.0 %all-to-all-start.3 = ((bf16[16,360,128]{2,1,0:T(8,128)(2,1)}), bf16[16,360,128]{2,1,0:T(8,128)(2,1)}, u32[]{:S(2)}, u32[]{:S(2)}) async-start(bf16[16,360,128]{2,1,0:T(8,128)(2,1)} %get-tuple-element.60), calls=%async_computation.3 | async-start | bytes 2949120 | tf_op jit(solution)/shard_map/all_to_all | solution.py:677
  135.0 2.0 %collective-permute-start.9 = (bf16[64,1280]{1,0:T(8,128)(2,1)S(1)}, bf16[64,1280]{1,0:T(8,128)(2,1)S(1)}, u32[]{:S(2)}, u32[]{:S(2)}) collective-permute-start(bf16[64,1280]{1,0:T(8,128)(2,1)S(1)} %get-tuple-element.65), channel_id=1, source_target_pairs={{0,32},{16,48},{32,64},{48,80},{64,96},{80,112},{96,0},{112,16},{1... | collective-permute-start | bytes 491528 | tf_op jit(solution)/shard_map/ppermute | solution.py:705
  137.0 11.0 %dynamics.3 = f32[4,1440,128]{2,1,0:T(8,128)} custom-call(f32[4,1440,128]{2,1,0:T(8,128)} %bitcast.49, f32[1440,128]{1,0:T(8,128)} %bitcast.53, f32[1440,128]{1,0:T(8,128)} %bitcast.57, f32[1440,128]{1,0:T(8,128)} %bitcast.61, bf16[4,7,96,128]{3,2,1,0:T(8,128)(2,1)} %copy-done.1, bf16[4,7,96,128]{3,2,1,0:T(8,128)(2,1)} %copy-done, ...), custom_call_target="tpu_custom_call", output_to_operand_aliasing={{}: (10, {})} | custom-call | flops 29491200 | bytes 5406720 | tf_op jit(solution)/shard_map/dynamics/pallas_call | solution.py:648
  148.0 10.5 %scatter_columns.2 = f32[5760,128]{1,0:T(8,128)} custom-call(s32[16,128]{1,0:T(8,128)} %get-tuple-element.41.refs_0_, bf16[16,360,128]{2,1,0:T(8,128)(2,1)} %copy-done.2, f32[5760,128]{1,0:T(8,128)} %bitcast.62), custom_call_target="tpu_custom_call" | custom-call | flops 3019898880 | bytes 5898240 | tf_op jit(solution)/shard_map/scatter_columns/pallas_call | solution.py:201
  160.0 7.9 %scatter_columns.3 = bf16[5760,128]{1,0:T(8,128)(2,1)} custom-call(s32[16,128]{1,0:T(8,128)} %get-tuple-element.41.refs_0_, bf16[16,360,128]{2,1,0:T(8,128)(2,1)} %all-to-all-done.3.refs_1_), custom_call_target="tpu_custom_call" | custom-call | flops 3019898880 | bytes 5898240 | tf_op jit(solution)/shard_map/scatter_columns/pallas_call | solution.py:201
  (53 shorter events, 7.0 us)
Async XLA Ops:
  8.4 28.6 %all-to-all-start = ((bf16[16,360,128]{2,1,0:T(8,128)(2,1)}), bf16[16,360,128]{2,1,0:T(8,128)(2,1)S(1)}, u32[]{:S(2)}, u32[]{:S(2)}) async-start(bf16[16,360,128]{2,1,0:T(8,128)(2,1)} %get-tuple-element.35), calls=%async_computation | async-start | bytes 2949120 | tf_op jit(solution)/shard_map/all_to_all | solution.py:677
  28.9 17.3 %copy-start.12 = (bf16[4,7,96,128]{3,2,1,0:T(8,128)(2,1)S(1)}, bf16[4,7,96,128]{3,2,1,0:T(8,128)(2,1)}, u32[]{:S(2)}) copy-start(bf16[4,7,96,128]{3,2,1,0:T(8,128)(2,1)} %get-tuple-element.39) | copy-start | bytes 2064388
  28.9 20.4 %copy-start.9 = (bf16[1,512,64]{1,2,0:T(8,128)(2,1)S(1)}, bf16[1,512,64]{1,2,0:T(8,128)(2,1)}, u32[]{:S(2)}) copy-start(bf16[1,512,64]{1,2,0:T(8,128)(2,1)} %param.20) | copy-start | bytes 196612
  28.9 20.4 %copy-start.10 = (bf16[1,360,64]{1,2,0:T(8,128)(2,1)S(1)}, bf16[1,360,64]{1,2,0:T(8,128)(2,1)}, u32[]{:S(2)}) copy-start(bf16[1,360,64]{1,2,0:T(8,128)(2,1)} %param.19) | copy-start | bytes 138244
  28.9 20.4 %copy-start.11 = (bf16[1,360,64]{1,2,0:T(8,128)(2,1)S(1)}, bf16[1,360,64]{1,2,0:T(8,128)(2,1)}, u32[]{:S(2)}) copy-start(bf16[1,360,64]{1,2,0:T(8,128)(2,1)} %param.21) | copy-start | bytes 138244
  37.1 1.1 copy-start.3
  38.2 41.6 %all-to-all-start.2 = ((bf16[16,360,128]{2,1,0:T(8,128)(2,1)}), bf16[16,360,128]{2,1,0:T(8,128)(2,1)}, u32[]{:S(2)}, u32[]{:S(2)}) async-start(bf16[16,360,128]{2,1,0:T(8,128)(2,1)} %gather_columns.1), calls=%async_computation.2 | async-start | bytes 2949120 | tf_op jit(solution)/shard_map/all_to_all | solution.py:677
  44.9 12.7 %collective-permute-start.1 = (bf16[4,7,96,128]{3,2,1,0:T(8,128)(2,1)}, bf16[4,7,96,128]{3,2,1,0:T(8,128)(2,1)S(1)}, u32[]{:S(2)}, u32[]{:S(2)}) collective-permute-start(bf16[4,7,96,128]{3,2,1,0:T(8,128)(2,1)} %get-tuple-element.40), channel_id=1, source_target_pairs={{16,0},{32,16},{48,32},{64,48},{80,64},{96,80},{112,96},{17,1},{33... | collective-permute-start | bytes 2064392 | tf_op jit(solution)/shard_map/ppermute | solution.py:601
  46.1 11.4 %collective-permute-start = (bf16[4,7,96,128]{3,2,1,0:T(8,128)(2,1)S(1)}, bf16[4,7,96,128]{3,2,1,0:T(8,128)(2,1)S(1)}, u32[]{:S(2)}, u32[]{:S(2)}) collective-permute-start(bf16[4,7,96,128]{3,2,1,0:T(8,128)(2,1)S(1)} %copy-done.12), channel_id=1, source_target_pairs={{0,16},{16,32},{32,48},{48,64},{64,80},{80,96},{96,112},{1,17},{17... | collective-permute-start | bytes 2064392 | tf_op jit(solution)/shard_map/ppermute | solution.py:600
  49.4 2.2 %collective-permute-start.2 = (bf16[64,1280]{1,0:T(8,128)(2,1)S(1)}, bf16[64,1280]{1,0:T(8,128)(2,1)S(1)}, u32[]{:S(2)}, u32[]{:S(2)}) collective-permute-start(bf16[64,1280]{1,0:T(8,128)(2,1)S(1)} %bitcast.65), channel_id=1, source_target_pairs={{0,16},{16,0},{32,48},{48,32},{64,80},{80,64},{96,112},{112,96},{1... | collective-permute-start | bytes 491528 | tf_op jit(solution)/shard_map/ppermute | solution.py:682
  51.6 19.9 %copy-start.8 = (bf16[128,1280]{1,0:T(8,128)(2,1)}, bf16[128,1280]{1,0:T(8,128)(2,1)S(1)}, u32[]{:S(2)}) copy-start(bf16[128,1280]{1,0:T(8,128)(2,1)S(1)} %constant_dynamic-update-slice_fusion.refs_2_.refs_5_) | copy-start | bytes 983044
  51.6 14.7 %collective-permute-start.3 = (bf16[128,1280]{1,0:T(8,128)(2,1)S(1)}, bf16[128,1280]{1,0:T(8,128)(2,1)S(1)}, u32[]{:S(2)}, u32[]{:S(2)}) collective-permute-start(bf16[128,1280]{1,0:T(8,128)(2,1)S(1)} %constant_dynamic-update-slice_fusion.refs_2_.refs_5_), channel_id=1, source_target_pairs={{0,32},{16,48},{32,64},{48,80},{64,96},{80,112},{96,0},{112,16},{1... | collective-permute-start | bytes 983048 | tf_op jit(solution)/shard_map/ppermute | solution.py:686
  53.1 18.0 %collective-permute-start.4 = (bf16[128,1280]{1,0:T(8,128)(2,1)S(1)}, bf16[128,1280]{1,0:T(8,128)(2,1)S(1)}, u32[]{:S(2)}, u32[]{:S(2)}) collective-permute-start(bf16[128,1280]{1,0:T(8,128)(2,1)S(1)} %constant_dynamic-update-slice_fusion.refs_2_.refs_5_), channel_id=1, source_target_pairs={{0,64},{16,80},{32,96},{48,112},{64,0},{80,16},{96,32},{112,48},{1... | collective-permute-start | bytes 983048 | tf_op jit(solution)/shard_map/ppermute | solution.py:686
  55.5 15.9 %collective-permute-start.5 = (bf16[128,1280]{1,0:T(8,128)(2,1)S(1)}, bf16[128,1280]{1,0:T(8,128)(2,1)S(1)}, u32[]{:S(2)}, u32[]{:S(2)}) collective-permute-start(bf16[128,1280]{1,0:T(8,128)(2,1)S(1)} %constant_dynamic-update-slice_fusion.refs_2_.refs_5_), channel_id=1, source_target_pairs={{0,96},{16,112},{32,0},{48,16},{64,32},{80,48},{96,64},{112,80},{1... | collective-permute-start | bytes 983048 | tf_op jit(solution)/shard_map/ppermute | solution.py:686
  57.6 0.9 copy-start
  58.5 0.9 copy-start.1
  66.2 5.2 %copy-start.13 = (bf16[128,1280]{1,0:T(8,128)(2,1)}, bf16[128,1280]{1,0:T(8,128)(2,1)S(1)}, u32[]{:S(2)}) copy-start(bf16[128,1280]{1,0:T(8,128)(2,1)S(1)} %collective-permute-done.3.refs_3_.refs_6_) | copy-start | bytes 983044
  71.1 0.7 copy-start.14
  71.8 0.7 copy-start.15
  79.8 45.1 %all-to-all-start.1 = ((bf16[16,360,128]{2,1,0:T(8,128)(2,1)}), bf16[16,360,128]{2,1,0:T(8,128)(2,1)S(1)}, u32[]{:S(2)}, u32[]{:S(2)}) async-start(bf16[16,360,128]{2,1,0:T(8,128)(2,1)} %get-tuple-element.47), calls=%async_computation.1 | async-start | bytes 2949120 | tf_op jit(solution)/shard_map/all_to_all | solution.py:677
  87.0 17.6 %copy-start.4 = (bf16[768,128]{1,0:T(8,128)(2,1)S(1)}, bf16[768,128]{1,0:T(8,128)(2,1)}, u32[]{:S(2)}) copy-start(bf16[768,128]{1,0:T(8,128)(2,1)} %get-tuple-element.56.refs_6_) | copy-start | bytes 589828
  87.1 20.2 %copy-start.5 = (bf16[768,128]{1,0:T(8,128)(2,1)S(1)}, bf16[768,128]{1,0:T(8,128)(2,1)}, u32[]{:S(2)}) copy-start(bf16[768,128]{1,0:T(8,128)(2,1)} %get-tuple-element.57.refs_7_) | copy-start | bytes 589828
  101.1 22.3 %collective-permute-start.8 = (bf16[4,64,1280]{2,1,0:T(8,128)(2,1)S(1)}, bf16[4,64,1280]{2,1,0:T(8,128)(2,1)}, u32[]{:S(2)}, u32[]{:S(2)}) collective-permute-start(bf16[4,64,1280]{2,1,0:T(8,128)(2,1)S(1)} %dynamic-slice_bitcast_fusion), channel_id=1, source_target_pairs={{0,16},{16,0},{32,48},{48,32},{64,80},{80,64},{96,112},{112,96},{1... | collective-permute-start | bytes 1966088 | tf_op jit(solution)/shard_map/ppermute | solution.py:696
  104.6 7.1 %collective-permute-start.6 = (bf16[768,128]{1,0:T(8,128)(2,1)S(1)}, bf16[768,128]{1,0:T(8,128)(2,1)S(1)}, u32[]{:S(2)}, u32[]{:S(2)}) collective-permute-start(bf16[768,128]{1,0:T(8,128)(2,1)S(1)} %copy-done.4), channel_id=1, source_target_pairs={{1,0},{2,1},{3,2},{4,3},{5,4},{6,5},{7,6},{8,7},{9,8},{10,9},{11,1... | collective-permute-start | bytes 589832 | tf_op jit(solution)/shard_map/ppermute | solution.py:626
  107.3 8.7 %collective-permute-start.7 = (bf16[768,128]{1,0:T(8,128)(2,1)S(1)}, bf16[768,128]{1,0:T(8,128)(2,1)S(1)}, u32[]{:S(2)}, u32[]{:S(2)}) collective-permute-start(bf16[768,128]{1,0:T(8,128)(2,1)S(1)} %copy-done.5), channel_id=1, source_target_pairs={{0,1},{1,2},{2,3},{3,4},{4,5},{5,6},{6,7},{7,8},{8,9},{9,10},{10,1... | collective-permute-start | bytes 589832 | tf_op jit(solution)/shard_map/ppermute | solution.py:625
  111.7 4.3 %copy-start.6 = (bf16[768,128]{1,0:T(8,128)(2,1)}, bf16[768,128]{1,0:T(8,128)(2,1)S(1)}, u32[]{:S(2)}) copy-start(bf16[768,128]{1,0:T(8,128)(2,1)S(1)} %collective-permute-done.6.refs_8_) | copy-start | bytes 589828
  116.0 0.7 copy-start.7
  124.9 1.1 copy-start.2
  126.0 34.0 %all-to-all-start.3 = ((bf16[16,360,128]{2,1,0:T(8,128)(2,1)}), bf16[16,360,128]{2,1,0:T(8,128)(2,1)}, u32[]{:S(2)}, u32[]{:S(2)}) async-start(bf16[16,360,128]{2,1,0:T(8,128)(2,1)} %get-tuple-element.60), calls=%async_computation.3 | async-start | bytes 2949120 | tf_op jit(solution)/shard_map/all_to_all | solution.py:677
  134.1 24.5 %collective-permute-start.10 = (bf16[64,1280]{1,0:T(8,128)(2,1)S(1)}, bf16[64,1280]{1,0:T(8,128)(2,1)S(1)}, u32[]{:S(2)}, u32[]{:S(2)}) collective-permute-start(bf16[64,1280]{1,0:T(8,128)(2,1)S(1)} %get-tuple-element.67), channel_id=1, source_target_pairs={{0,64},{16,80},{32,96},{48,112},{64,0},{80,16},{96,32},{112,48},{1... | collective-permute-start | bytes 491528 | tf_op jit(solution)/shard_map/ppermute | solution.py:705
  135.0 23.6 %collective-permute-start.11 = (bf16[64,1280]{1,0:T(8,128)(2,1)S(1)}, bf16[64,1280]{1,0:T(8,128)(2,1)S(1)}, u32[]{:S(2)}, u32[]{:S(2)}) collective-permute-start(bf16[64,1280]{1,0:T(8,128)(2,1)S(1)} %get-tuple-element.66), channel_id=1, source_target_pairs={{0,96},{16,112},{32,0},{48,16},{64,32},{80,48},{96,64},{112,80},{1... | collective-permute-start | bytes 491528 | tf_op jit(solution)/shard_map/ppermute | solution.py:705
  135.0 23.6 %collective-permute-start.9 = (bf16[64,1280]{1,0:T(8,128)(2,1)S(1)}, bf16[64,1280]{1,0:T(8,128)(2,1)S(1)}, u32[]{:S(2)}, u32[]{:S(2)}) collective-permute-start(bf16[64,1280]{1,0:T(8,128)(2,1)S(1)} %get-tuple-element.65), channel_id=1, source_target_pairs={{0,32},{16,48},{32,64},{48,80},{64,96},{80,112},{96,0},{112,16},{1... | collective-permute-start | bytes 491528 | tf_op jit(solution)/shard_map/ppermute | solution.py:705

commit v3 on v2

--- a/solution.py
+++ b/solution.py
@@ -123,23 +123,17 @@
     )(table, source)
 
 
-def scatter_rows(table_ref, blocks_ref, mat_ref, where_ref, sems):
+def scatter_rows(table_ref, blocks_ref, mat_ref, where_ref):
     nblock = blocks_ref.shape[0]
 
     @pl.when(pl.program_id(0) == 0)
     def _():
-        loads = []
-        for b in range(nblock):
-            to = mat_ref.at[:, pl.ds(b * LANE, LANE)]
-            loads.append(pltpu.make_async_copy(blocks_ref.at[b], to, sems.at[b]))
-            loads[-1].start()
         table = table_ref[...].astype(F32)
         by_slot = jnp.concatenate([table, jnp.zeros((LANE - nblock, LANE), F32)], axis=0).T
         for b in range(nblock):
+            mat_ref[:, b * LANE : (b + 1) * LANE] = blocks_ref[b]
             column = jnp.broadcast_to(by_slot[:, b : b + 1], (LANE, LANE))
             where_ref[b * LANE : (b + 1) * LANE, :] = column.astype(jnp.int32)
-        for load in loads:
-            load.wait()
 
     where = where_ref[...]
     lane = iota(where.shape, 1) + pl.program_id(0) * (WIDE * LANE)
@@ -147,26 +141,15 @@
     return jnp.dot(mat_ref[...], jnp.concatenate(hot, axis=1), preferred_element_type=F32)
 
 
-def scatter_add_kernel(table_ref, blocks_ref, base_ref, out_ref, mat_ref, where_ref, sems, full_ref, base_sem, *, rows):
-    load = pltpu.make_async_copy(base_ref, full_ref, base_sem)
-
-    @pl.when(pl.program_id(0) == 0)
-    def _():
-        load.start()
-
-    got = scatter_rows(table_ref, blocks_ref, mat_ref, where_ref, sems)
-
-    @pl.when(pl.program_id(0) == 0)
-    def _():
-        load.wait()
-
+def scatter_add_kernel(table_ref, blocks_ref, base_ref, out_ref, mat_ref, where_ref, *, rows):
+    got = scatter_rows(table_ref, blocks_ref, mat_ref, where_ref)
     for r in range(WIDE):
         at = pl.ds(pl.program_id(0) * WIDE + r, mat_ref.shape[0], stride=rows)
-        out_ref[at, :] = full_ref[at, :] + got[:, r * LANE : (r + 1) * LANE]
-
-
-def scatter_kernel(table_ref, blocks_ref, out_ref, mat_ref, where_ref, sems, full_ref, *, rows):
-    got = scatter_rows(table_ref, blocks_ref, mat_ref, where_ref, sems)
+        out_ref[at, :] = base_ref[at, :] + got[:, r * LANE : (r + 1) * LANE]
+
+
+def scatter_kernel(table_ref, blocks_ref, out_ref, mat_ref, where_ref, full_ref, *, rows):
+    got = scatter_rows(table_ref, blocks_ref, mat_ref, where_ref)
     for r in range(WIDE):
         at = pl.ds(pl.program_id(0) * WIDE + r, mat_ref.shape[0], stride=rows)
         full_ref[at, :] = got[:, r * LANE : (r + 1) * LANE]
@@ -180,20 +163,18 @@
     nblock, feat, length = blocks.shape
     nslot = nblock * length
     shape = (feat * rows, LANE)
-    in_place = pl.BlockSpec(memory_space=pl.ANY)
-    specs = [pl.BlockSpec(table.shape, lambda i: (0, 0)), in_place]
-    scratch = [
-        pltpu.VMEM((feat, nslot), BF16),
-        pltpu.VMEM((nslot, LANE), jnp.int32),
-        pltpu.SemaphoreType.DMA((nblock,)),
-        pltpu.VMEM(shape, F32),
+    whole = pl.BlockSpec(shape, lambda i: (0, 0), pipeline_mode=pl.Buffered(1))
+    specs = [
+        pl.BlockSpec(table.shape, lambda i: (0, 0)),
+        pl.BlockSpec(blocks.shape, lambda i: (0, 0, 0), pipeline_mode=pl.Buffered(1)),
     ]
+    scratch = [pltpu.VMEM((feat, nslot), BF16), pltpu.VMEM((nslot, LANE), jnp.int32)]
     if base is None:
         body, operands, dtype = scatter_kernel, (table, blocks), BF16
+        scratch.append(pltpu.VMEM(shape, F32))
     else:
         body, operands, dtype = scatter_add_kernel, (table, blocks, base), F32
-        specs.append(in_place)
-        scratch.append(pltpu.SemaphoreType.DMA)
+        specs.append(whole)
 
     def kernel(*refs):
         body(*refs, rows=rows)
@@ -231,14 +212,11 @@
 
 
 def place_weights(at_ref, piece_refs, w_t_ref, w_ref, parts):
-    chips = len(piece_refs)
     size = piece_refs[0].shape[0] // 2
-    for n, piece in enumerate(piece_refs):
-        chip = (at_ref[0] + (chips - n)) % chips
-        for half in range(2):
-            core = at_ref[1] if half == 0 else 1 - at_ref[1]
-            at = pl.multiple_of((2 * chip + core) * size, size)
-            w_t_ref[pl.ds(at, size), :] = piece[half * size : (half + 1) * size, :]
+    pieces = [ref.at[k : k + size] for ref in piece_refs for k in range(0, ref.shape[0], size)]
+    for n, piece in enumerate(pieces):
+        place = 2 * (at_ref[0] ^ (n // 2)) + (at_ref[1] ^ (n % 2))
+        w_t_ref[pl.ds(pl.multiple_of(place * size, size), size), :] = piece[...]
     row = 0
     for start, stop in parts:
         w_ref[row : row + stop - start, :] = w_t_ref[:, start:stop].T
@@ -301,12 +279,12 @@
 
 def column_specs(shape, pieces):
     _, feat, length = shape
-    rows, span = pieces[0].shape
-    hid = rows * len(pieces)
+    span = pieces[0].shape[1]
+    hid = sum(piece.shape[0] for piece in pieces)
     block = pl.BlockSpec((WIDE, feat, length), lambda i: (i, 0, 0))
     hidden = pl.BlockSpec((hid, WIDE * length), lambda i: (0, i))
-    piece = pl.BlockSpec((rows, span), lambda i: (0, 0), pipeline_mode=pl.Buffered(1))
-    return hid, span, block, hidden, [piece] * len(pieces)
+    specs = [pl.BlockSpec(piece.shape, lambda i: (0, 0), pipeline_mode=pl.Buffered(1)) for piece in pieces]
+    return hid, span, block, hidden, specs
 
 
 def physics_forward(at, x, pieces, cuts):
@@ -463,14 +441,17 @@
     rim_ref[1] = north_ref[...].astype(F32)
 
     sources = jnp.concatenate([own_e_ref[...], from_e_ref[...], from_w_ref[...], own_w_ref[...]], axis=1)
-    shape = (4 * LANE, 4 * LANE)
-    k, n = iota(shape, 0), iota(shape, 1)
-    lane, kind, m = k % LANE, n // LANE, n % LANE
+    k = iota((4 * LANE, LANE), 0)
+    lane = k % LANE
     row_code = (k // LANE) * STEPS + lane % STEPS + 16 * ((lane // STEPS) % 8)
     row_code = jnp.where(lane // GROUP == pl.program_id(0) + first, row_code, -1)
-    col_code = jnp.where(kind == 0, m, m % 16 + 16 * (nfield - 1 + kind))
-    col_code = jnp.where(m < 16 * nfield, col_code, -2)
-    pick = jnp.where(row_code == col_code, 1.0, 0.0).astype(BF16)
+    m = iota((1, LANE), 1)
+    picks = []
+    for kind in range(4):
+        col_code = m if kind == 0 else m % 16 + 16 * (nfield - 1 + kind)
+        col_code = jnp.where(m < 16 * nfield, col_code, -2)
+        picks.append(jnp.where(row_code == col_code, 1.0, 0.0).astype(BF16))
+    pick = jnp.concatenate(picks, axis=1)
     strip_ref[...] = jnp.dot(sources, pick, preferred_element_type=F32)
 
     @pl.when(pl.program_id(0) == 0)
@@ -679,12 +660,14 @@
 
 def spread(piece):
     size = lax.axis_size("lat")
-    other = lax.ppermute(piece, "lat", [(i, i ^ 1) for i in range(size)])
-    both = jnp.concatenate([piece, other], axis=0)
-    pieces = [both]
-    for shift in range(1, size // 2):
-        pieces.append(lax.ppermute(both, "lat", [(i, (i + 2 * shift) % size) for i in range(size)]))
-    return pieces
+    held = [piece]
+    for flip in (1, 2, 4):
+        mine = jnp.concatenate(held, axis=0) if len(held) > 1 else held[0]
+        theirs = lax.ppermute(mine, "lat", [(i, i ^ flip) for i in range(size)])
+        held = [mine, theirs]
+        if flip == 2:
+            chips = held
+    return chips + [theirs]
 
 
 def scattered(parts, start):

time: 169 us -> 170 us (level)
  starting transfers between devices: 50.5 us -> 52.9 us
    ppermute x1, starting transfers between devices: 3.5 us -> 6.5 us  [scattered(): other = lax.ppermute(other, 'lat', [(i, i ^ 1) for i in range(size)])]
    all_to_all x4, waiting for transfers between devices: 8.2 us -> 6.31 us  [exchange(): return lax.all_to_all(array, axis, split_axis=0, concat_axis=0, tiled=True)]
    ppermute x4 -> x3, starting transfers between devices: 6.58 us -> 4.72 us  [spread(): theirs = lax.ppermute(mine, 'lat', [(i, i ^ flip) for i in range(size)])]
    ppermute x4 -> x3, waiting for transfers between devices: 6.21 us -> 6.91 us  [spread(): theirs = lax.ppermute(mine, 'lat', [(i, i ^ flip) for i in range(size)])]
    unnamed x33 -> x29, local copies, waits for them, and re-layouts: 5.74 us -> 5.52 us
  transfers between devices with their start and end apart: 16 -> 15, of which waited for: 6 -> 4; matrix products, arithmetic and copies ran while one was open for 3% -> 3% of each run, Pallas kernels for 40% -> 40%
where the time goes in v3:
time: 170 us; the launch traced here: 168 us
  Pallas kernels  82.1 us (48%)
  starting transfers between devices  52.9 us (31%)
  waiting for transfers between devices  22 us (13%)
  local copies, waits for them, and re-layouts  8.16 us (5%)
  other arithmetic  2.18 us (1%)
    all_to_all x4, starting transfers between devices, exchange(): return lax.all_to_all(array, axis, split_axis=0, concat_axis=0, tiled=True)  30.6 us
    pallas_call x2, Pallas kernels, steps(): pl.pallas_call(kernel, grid=(count,), in_specs=specs, out_specs=fields_sp...  17.7 us
    pallas_call x2, Pallas kernels, scatter_columns(): pl.pallas_call(kernel, grid=(rows // WIDE,), in_specs=specs, out_specs=pl...  17.6 us
    pallas_call x1, Pallas kernels, physics_backward(): pl.pallas_call(kernel, grid=(nblock // WIDE,), in_specs=[pl.BlockSpec(mem...  12.8 us
    pallas_call x1, Pallas kernels, gather_first(): pl.pallas_call(kernel, grid=(nblock // WIDE,), in_specs=[scalars, scalars...  7.77 us
    pallas_call x1, Pallas kernels, gather_columns(): pl.pallas_call(kernel, grid=(nblock // WIDE,), in_specs=[pl.BlockSpec(tab...  7.53 us
    pallas_call x1, Pallas kernels, physics_forward(): pl.pallas_call(kernel, grid=(nblock // WIDE,), in_specs=[pl.BlockSpec(mem...  7.2 us
    ppermute x3, waiting for transfers between devices, spread(): theirs = lax.ppermute(mine, 'lat', [(i, i ^ flip) for i in range(size)])  6.91 us
  transfers between devices with their start and end apart: 15, of which 4 were waited for; matrix products, arithmetic and copies ran while one was open for 3% of the time, Pallas kernels for 40%

profile of v3, /device:TPU:8, one launch (start us, length us, event | category | flops | bytes accessed | tf_op | source)
XLA Modules:
  0.0 168.2 jit_solution(7099345918167295697)
XLA Ops:
  0.6 7.8 %gather_first.1 = (bf16[16,360,128]{2,1,0:T(8,128)(2,1)}, s32[16,128]{1,0:T(8,128)}) custom-call(s32[1,1,16]{2,1,0:T(1,128)} %refs_0_.1, s32[1,1,16]{2,1,0:T(1,128)} %refs_1_.1, s32[16,1,128]{2,1,0:T(1,128)} %bitcast.72, f32[5760,128]{1,0:T(8,128)} %bitcast.45), custom_call_target="tpu_custom_call" | custom-call | flops 3019898880 | bytes 4423680 | tf_op jit(solution)/shard_map/gather_first/pallas_call | solution.py:91
  8.4 8.5 %all-to-all-start = ((bf16[16,360,128]{2,1,0:T(8,128)(2,1)}), bf16[16,360,128]{2,1,0:T(8,128)(2,1)S(1)}, u32[]{:S(2)}, u32[]{:S(2)}) async-start(bf16[16,360,128]{2,1,0:T(8,128)(2,1)} %get-tuple-element.35), calls=%async_computation | async-start | bytes 2949120 | tf_op jit(solution)/shard_map/all_to_all | solution.py:658
  17.2 4.5 %rims.1 = (bf16[4,7,96,128]{3,2,1,0:T(8,128)(2,1)}, bf16[4,7,96,128]{3,2,1,0:T(8,128)(2,1)}) custom-call(f32[4,1440,128]{2,1,0:T(8,128)} %bitcast.46, f32[1440,128]{1,0:T(8,128)} %bitcast.50, f32[1440,128]{1,0:T(8,128)} %bitcast.54, f32[1440,128]{1,0:T(8,128)} %bitcast.58), custom_call_target="tpu_custom_call" | custom-call | tf_op jit(solution)/shard_map/rims/pallas_call | solution.py:569
  21.8 1.6 collective-permute-start.3
  23.4 7.5 %gather_columns.1 = bf16[16,360,128]{2,1,0:T(8,128)(2,1)} custom-call(s32[16,128]{1,0:T(8,128)} %get-tuple-element.41.refs_0_, bf16[5760,128]{1,0:T(8,128)(2,1)} %bitcast.71), custom_call_target="tpu_custom_call" | custom-call | flops 3019898880 | bytes 2949120 | tf_op jit(solution)/shard_map/gather_columns/pallas_call | solution.py:114
  30.9 6.3 %all-to-all-done.refs_1_ = bf16[16,360,128]{2,1,0:T(8,128)(2,1)S(1)} async-done(((bf16[16,360,128]{2,1,0:T(8,128)(2,1)}), bf16[16,360,128]{2,1,0:T(8,128)(2,1)S(1)}, u32[]{:S(2)}, u32[]{:S(2)}) %all-to-all-start) | async-done | bytes 1474592 | tf_op jit(solution)/shard_map/all_to_all | solution.py:658
  37.2 1.1 copy-done.3
  38.3 6.7 %all-to-all-start.2 = ((bf16[16,360,128]{2,1,0:T(8,128)(2,1)}), bf16[16,360,128]{2,1,0:T(8,128)(2,1)}, u32[]{:S(2)}, u32[]{:S(2)}) async-start(bf16[16,360,128]{2,1,0:T(8,128)(2,1)} %gather_columns.1), calls=%async_computation.2 | async-start | bytes 2949120 | tf_op jit(solution)/shard_map/all_to_all | solution.py:658
  45.0 1.3 collective-permute-start.1
  46.3 3.1 %collective-permute-start = (bf16[4,7,96,128]{3,2,1,0:T(8,128)(2,1)}, bf16[4,7,96,128]{3,2,1,0:T(8,128)(2,1)S(1)}, u32[]{:S(2)}, u32[]{:S(2)}) collective-permute-start(bf16[4,7,96,128]{3,2,1,0:T(8,128)(2,1)} %get-tuple-element.39), channel_id=1, source_target_pairs={{0,16},{16,32},{32,48},{48,64},{64,80},{80,96},{96,112},{1,17},{17... | collective-permute-start | bytes 2064392 | tf_op jit(solution)/shard_map/ppermute | solution.py:581
  49.5 3.1 %collective-permute-start.4 = (bf16[256,1280]{1,0:T(8,128)(2,1)S(1)}, bf16[256,1280]{1,0:T(8,128)(2,1)S(1)}, u32[]{:S(2)}, u32[]{:S(2)}) collective-permute-start(bf16[256,1280]{1,0:T(8,128)(2,1)S(1)} %pad_maximum_fusion), channel_id=1, source_target_pairs={{0,64},{16,80},{32,96},{48,112},{64,0},{80,16},{96,32},{112,48},{1... | collective-permute-start | bytes 1966088 | tf_op jit(solution)/shard_map/ppermute | solution.py:666
  53.1 0.9 copy-done
  54.8 6.9 %strips.1 = (bf16[768,128]{1,0:T(8,128)(2,1)}, bf16[768,128]{1,0:T(8,128)(2,1)}) custom-call(f32[4,1440,128]{2,1,0:T(8,128)} %bitcast.47, f32[1440,128]{1,0:T(8,128)} %bitcast.51, f32[1440,128]{1,0:T(8,128)} %bitcast.55, f32[1440,128]{1,0:T(8,128)} %bitcast.59, bf16[4,7,96,128]{3,2,1,0:T(8,128)(2,1)} %copy-done.1, bf16[4,7,96,128]{3,2,1,0:T(8,128)(2,1)} %copy-done), custom_call_target="tpu_custom_call" | custom-call | tf_op jit(solution)/shard_map/strips/pallas_call | solution.py:590
  61.8 6.9 %collective-permute-done.4.refs_4_.refs_7_ = bf16[256,1280]{1,0:T(8,128)(2,1)S(1)} collective-permute-done((bf16[256,1280]{1,0:T(8,128)(2,1)S(1)}, bf16[256,1280]{1,0:T(8,128)(2,1)S(1)}, u32[]{:S(2)}, u32[]{:S(2)}) %collective-permute-start.4) | collective-permute-done | bytes 655392 | tf_op jit(solution)/shard_map/ppermute | solution.py:666
  68.7 0.9 copy-done.13
  69.5 7.2 %physics_forward.1 = (bf16[16,360,128]{2,1,0:T(8,128)(2,1)}, f32[512,2048]{1,0:T(8,128)}, f32[512,2048]{1,0:T(8,128)}) custom-call(s32[2]{0:T(128)} %pad_add_fusion.refs_0_, bf16[16,360,128]{2,1,0:T(8,128)(2,1)} %copy-done.3, bf16[128,1280]{1,0:T(8,128)(2,1)} %copy-done.9, bf16[128,1280]{1,0:T(8,128)(2,1)} %copy-done.8, bf16[256,1280]{1,0:T(8,128)(2,1)} %copy-done.13), custom_call_target="tpu_custom_call" | custom-call | flops 2583691264 | bytes 11337728 | tf_op jit(solution)/shard_map/physics_forward/pallas_call | solution.py:298
  76.7 7.3 %all-to-all-start.1 = ((bf16[16,360,128]{2,1,0:T(8,128)(2,1)}), bf16[16,360,128]{2,1,0:T(8,128)(2,1)S(1)}, u32[]{:S(2)}, u32[]{:S(2)}) async-start(bf16[16,360,128]{2,1,0:T(8,128)(2,1)} %get-tuple-element.47), calls=%async_computation.1 | async-start | bytes 2949120 | tf_op jit(solution)/shard_map/all_to_all | solution.py:658
  84.0 12.8 %physics_backward.1 = (bf16[16,360,128]{2,1,0:T(8,128)(2,1)}, bf16[512,1280]{1,0:T(8,128)(2,1)}) custom-call(s32[2]{0:T(128)} %pad_add_fusion.refs_0_, bf16[16,360,128]{2,1,0:T(8,128)(2,1)} %copy-done.3, bf16[16,360,128]{2,1,0:T(8,128)(2,1)} %all-to-all-done.2.refs_2_, f32[512,2048]{1,0:T(8,128)} %get-tuple-element.53.refs_3_, ...), custom_call_target="tpu_custom_call" | custom-call | flops 5167382528 | bytes 12812288 | tf_op jit(solution)/shard_map/physics_backward/pallas_call | solution.py:321
  96.9 1.1 dynamic-slice_bitcast_fusion
  98.0 6.5 %collective-permute-start.7 = (bf16[4,64,1280]{2,1,0:T(8,128)(2,1)S(1)}, bf16[4,64,1280]{2,1,0:T(8,128)(2,1)}, u32[]{:S(2)}, u32[]{:S(2)}) collective-permute-start(bf16[4,64,1280]{2,1,0:T(8,128)(2,1)S(1)} %dynamic-slice_bitcast_fusion), channel_id=1, source_target_pairs={{0,16},{16,0},{32,48},{48,32},{64,80},{80,64},{96,112},{112,96},{1... | collective-permute-start | bytes 1966088 | tf_op jit(solution)/shard_map/ppermute | solution.py:679
  104.5 2.7 %collective-permute-start.5 = (bf16[768,128]{1,0:T(8,128)(2,1)S(1)}, bf16[768,128]{1,0:T(8,128)(2,1)S(1)}, u32[]{:S(2)}, u32[]{:S(2)}) collective-permute-start(bf16[768,128]{1,0:T(8,128)(2,1)S(1)} %copy-done.4), channel_id=1, source_target_pairs={{1,0},{2,1},{3,2},{4,3},{5,4},{6,5},{7,6},{8,7},{9,8},{10,9},{11,1... | collective-permute-start | bytes 589832 | tf_op jit(solution)/shard_map/ppermute | solution.py:607
  107.2 4.4 %collective-permute-done.5.refs_8_ = bf16[768,128]{1,0:T(8,128)(2,1)S(1)} collective-permute-done((bf16[768,128]{1,0:T(8,128)(2,1)S(1)}, bf16[768,128]{1,0:T(8,128)(2,1)S(1)}, u32[]{:S(2)}, u32[]{:S(2)}) %collective-permute-start.5) | collective-permute-done | bytes 196640 | tf_op jit(solution)/shard_map/ppermute | solution.py:607
  111.6 4.3 %collective-permute-done.6.refs_9_ = bf16[768,128]{1,0:T(8,128)(2,1)S(1)} collective-permute-done((bf16[768,128]{1,0:T(8,128)(2,1)S(1)}, bf16[768,128]{1,0:T(8,128)(2,1)S(1)}, u32[]{:S(2)}, u32[]{:S(2)}) %collective-permute-start.6) | collective-permute-done | bytes 196640 | tf_op jit(solution)/shard_map/ppermute | solution.py:606
  116.6 6.7 %dynamics.2.refs_10_ = f32[4,1440,128]{2,1,0:T(8,128)} custom-call(f32[4,1440,128]{2,1,0:T(8,128)} %bitcast.48, f32[1440,128]{1,0:T(8,128)} %bitcast.52, f32[1440,128]{1,0:T(8,128)} %bitcast.56, f32[1440,128]{1,0:T(8,128)} %bitcast.60, bf16[4,7,96,128]{3,2,1,0:T(8,128)(2,1)} %copy-done.1, bf16[4,7,96,128]{3,2,1,0:T(8,128)(2,1)} %copy-done, ...), custom_call_target="tpu_custom_call" | custom-call | flops 14745600 | bytes 2703360 | tf_op jit(solution)/shard_map/dynamics/pallas_call | solution.py:629
  123.3 1.5 fusion.3
  124.8 1.1 copy-done.2
  125.9 8.0 %all-to-all-start.3 = ((bf16[16,360,128]{2,1,0:T(8,128)(2,1)}), bf16[16,360,128]{2,1,0:T(8,128)(2,1)}, u32[]{:S(2)}, u32[]{:S(2)}) async-start(bf16[16,360,128]{2,1,0:T(8,128)(2,1)} %get-tuple-element.60), calls=%async_computation.3 | async-start | bytes 2949120 | tf_op jit(solution)/shard_map/all_to_all | solution.py:658
  134.0 2.5 %collective-permute-start.10 = (bf16[64,1280]{1,0:T(8,128)(2,1)S(1)}, bf16[64,1280]{1,0:T(8,128)(2,1)S(1)}, u32[]{:S(2)}, u32[]{:S(2)}) collective-permute-start(bf16[64,1280]{1,0:T(8,128)(2,1)S(1)} %get-tuple-element.66), channel_id=1, source_target_pairs={{0,96},{16,112},{32,0},{48,16},{64,32},{80,48},{96,64},{112,80},{1... | collective-permute-start | bytes 491528 | tf_op jit(solution)/shard_map/ppermute | solution.py:688
  136.5 1.5 collective-permute-start.9
  138.0 11.0 %dynamics.3 = f32[4,1440,128]{2,1,0:T(8,128)} custom-call(f32[4,1440,128]{2,1,0:T(8,128)} %bitcast.49, f32[1440,128]{1,0:T(8,128)} %bitcast.53, f32[1440,128]{1,0:T(8,128)} %bitcast.57, f32[1440,128]{1,0:T(8,128)} %bitcast.61, bf16[4,7,96,128]{3,2,1,0:T(8,128)(2,1)} %copy-done.1, bf16[4,7,96,128]{3,2,1,0:T(8,128)(2,1)} %copy-done, ...), custom_call_target="tpu_custom_call", output_to_operand_aliasing={{}: (10, {})} | custom-call | flops 29491200 | bytes 5406720 | tf_op jit(solution)/shard_map/dynamics/pallas_call | solution.py:629
  149.1 9.8 %scatter_columns.2 = f32[5760,128]{1,0:T(8,128)} custom-call(s32[16,128]{1,0:T(8,128)} %get-tuple-element.41.refs_0_, bf16[16,360,128]{2,1,0:T(8,128)(2,1)} %copy-done.2, f32[5760,128]{1,0:T(8,128)} %bitcast.62), custom_call_target="tpu_custom_call" | custom-call | flops 3019898880 | bytes 5898240 | tf_op jit(solution)/shard_map/scatter_columns/pallas_call | solution.py:182
  160.3 7.8 %scatter_columns.3 = bf16[5760,128]{1,0:T(8,128)(2,1)} custom-call(s32[16,128]{1,0:T(8,128)} %get-tuple-element.41.refs_0_, bf16[16,360,128]{2,1,0:T(8,128)(2,1)} %all-to-all-done.3.refs_1_), custom_call_target="tpu_custom_call" | custom-call | flops 3019898880 | bytes 5898240 | tf_op jit(solution)/shard_map/scatter_columns/pallas_call | solution.py:182
  (48 shorter events, 3.9 us)
Async XLA Ops:
  8.4 8.6 %copy-start.10 = (bf16[1,512,64]{1,2,0:T(8,128)(2,1)S(1)}, bf16[1,512,64]{1,2,0:T(8,128)(2,1)}, u32[]{:S(2)}) copy-start(bf16[1,512,64]{1,2,0:T(8,128)(2,1)} %param.20) | copy-start | bytes 196612
  8.4 8.6 %copy-start.11 = (bf16[1,360,64]{1,2,0:T(8,128)(2,1)S(1)}, bf16[1,360,64]{1,2,0:T(8,128)(2,1)}, u32[]{:S(2)}) copy-start(bf16[1,360,64]{1,2,0:T(8,128)(2,1)} %param.19) | copy-start | bytes 138244
  8.4 8.6 %copy-start.12 = (bf16[1,360,64]{1,2,0:T(8,128)(2,1)S(1)}, bf16[1,360,64]{1,2,0:T(8,128)(2,1)}, u32[]{:S(2)}) copy-start(bf16[1,360,64]{1,2,0:T(8,128)(2,1)} %param.21) | copy-start | bytes 138244
  8.4 28.8 %all-to-all-start = ((bf16[16,360,128]{2,1,0:T(8,128)(2,1)}), bf16[16,360,128]{2,1,0:T(8,128)(2,1)S(1)}, u32[]{:S(2)}, u32[]{:S(2)}) async-start(bf16[16,360,128]{2,1,0:T(8,128)(2,1)} %get-tuple-element.35), calls=%async_computation | async-start | bytes 2949120 | tf_op jit(solution)/shard_map/all_to_all | solution.py:658
  17.1 4.6 %collective-permute-start.2 = (bf16[64,1280]{1,0:T(8,128)(2,1)S(1)}, bf16[64,1280]{1,0:T(8,128)(2,1)S(1)}, u32[]{:S(2)}, u32[]{:S(2)}) collective-permute-start(bf16[64,1280]{1,0:T(8,128)(2,1)S(1)} %bitcast.63), channel_id=1, source_target_pairs={{0,16},{16,0},{32,48},{48,32},{64,80},{80,64},{96,112},{112,96},{1... | collective-permute-start | bytes 491528 | tf_op jit(solution)/shard_map/ppermute | solution.py:666
  21.8 9.1 %copy-start.9 = (bf16[128,1280]{1,0:T(8,128)(2,1)}, bf16[128,1280]{1,0:T(8,128)(2,1)S(1)}, u32[]{:S(2)}) copy-start(bf16[128,1280]{1,0:T(8,128)(2,1)S(1)} %constant_dynamic-update-slice_fusion.refs_2_.refs_5_) | copy-start | bytes 983044
  21.8 27.6 %collective-permute-start.3 = (bf16[128,1280]{1,0:T(8,128)(2,1)S(1)}, bf16[128,1280]{1,0:T(8,128)(2,1)S(1)}, u32[]{:S(2)}, u32[]{:S(2)}) collective-permute-start(bf16[128,1280]{1,0:T(8,128)(2,1)S(1)} %constant_dynamic-update-slice_fusion.refs_2_.refs_5_), channel_id=1, source_target_pairs={{0,32},{16,48},{32,0},{48,16},{64,96},{80,112},{96,64},{112,80},{1... | collective-permute-start | bytes 983048 | tf_op jit(solution)/shard_map/ppermute | solution.py:666
  37.2 1.1 copy-start.3
  38.3 38.4 %all-to-all-start.2 = ((bf16[16,360,128]{2,1,0:T(8,128)(2,1)}), bf16[16,360,128]{2,1,0:T(8,128)(2,1)}, u32[]{:S(2)}, u32[]{:S(2)}) async-start(bf16[16,360,128]{2,1,0:T(8,128)(2,1)} %gather_columns.1), calls=%async_computation.2 | async-start | bytes 2949120 | tf_op jit(solution)/shard_map/all_to_all | solution.py:658
  45.0 8.1 %collective-permute-start.1 = (bf16[4,7,96,128]{3,2,1,0:T(8,128)(2,1)}, bf16[4,7,96,128]{3,2,1,0:T(8,128)(2,1)S(1)}, u32[]{:S(2)}, u32[]{:S(2)}) collective-permute-start(bf16[4,7,96,128]{3,2,1,0:T(8,128)(2,1)} %get-tuple-element.40), channel_id=1, source_target_pairs={{16,0},{32,16},{48,32},{64,48},{80,64},{96,80},{112,96},{17,1},{33... | collective-permute-start | bytes 2064392 | tf_op jit(solution)/shard_map/ppermute | solution.py:582
  46.3 6.8 %collective-permute-start = (bf16[4,7,96,128]{3,2,1,0:T(8,128)(2,1)}, bf16[4,7,96,128]{3,2,1,0:T(8,128)(2,1)S(1)}, u32[]{:S(2)}, u32[]{:S(2)}) collective-permute-start(bf16[4,7,96,128]{3,2,1,0:T(8,128)(2,1)} %get-tuple-element.39), channel_id=1, source_target_pairs={{0,16},{16,32},{32,48},{48,64},{64,80},{80,96},{96,112},{1,17},{17... | collective-permute-start | bytes 2064392 | tf_op jit(solution)/shard_map/ppermute | solution.py:581
  49.4 12.3 %copy-start.8 = (bf16[128,1280]{1,0:T(8,128)(2,1)}, bf16[128,1280]{1,0:T(8,128)(2,1)S(1)}, u32[]{:S(2)}) copy-start(bf16[128,1280]{1,0:T(8,128)(2,1)S(1)} %collective-permute-done.3.refs_3_.refs_6_) | copy-start | bytes 983044
  49.5 19.2 %collective-permute-start.4 = (bf16[256,1280]{1,0:T(8,128)(2,1)S(1)}, bf16[256,1280]{1,0:T(8,128)(2,1)S(1)}, u32[]{:S(2)}, u32[]{:S(2)}) collective-permute-start(bf16[256,1280]{1,0:T(8,128)(2,1)S(1)} %pad_maximum_fusion), channel_id=1, source_target_pairs={{0,64},{16,80},{32,96},{48,112},{64,0},{80,16},{96,32},{112,48},{1... | collective-permute-start | bytes 1966088 | tf_op jit(solution)/shard_map/ppermute | solution.py:666
  53.1 0.9 copy-start
  54.0 0.9 copy-start.1
  68.7 0.9 copy-start.13
  76.7 48.0 %all-to-all-start.1 = ((bf16[16,360,128]{2,1,0:T(8,128)(2,1)}), bf16[16,360,128]{2,1,0:T(8,128)(2,1)S(1)}, u32[]{:S(2)}, u32[]{:S(2)}) async-start(bf16[16,360,128]{2,1,0:T(8,128)(2,1)} %get-tuple-element.47), calls=%async_computation.1 | async-start | bytes 2949120 | tf_op jit(solution)/shard_map/all_to_all | solution.py:658
  84.0 20.5 %copy-start.4 = (bf16[768,128]{1,0:T(8,128)(2,1)S(1)}, bf16[768,128]{1,0:T(8,128)(2,1)}, u32[]{:S(2)}) copy-start(bf16[768,128]{1,0:T(8,128)(2,1)} %get-tuple-element.56.refs_6_) | copy-start | bytes 589828
  84.0 23.2 %copy-start.5 = (bf16[768,128]{1,0:T(8,128)(2,1)S(1)}, bf16[768,128]{1,0:T(8,128)(2,1)}, u32[]{:S(2)}) copy-start(bf16[768,128]{1,0:T(8,128)(2,1)} %get-tuple-element.57.refs_7_) | copy-start | bytes 589828
  98.0 25.3 %collective-permute-start.7 = (bf16[4,64,1280]{2,1,0:T(8,128)(2,1)S(1)}, bf16[4,64,1280]{2,1,0:T(8,128)(2,1)}, u32[]{:S(2)}, u32[]{:S(2)}) collective-permute-start(bf16[4,64,1280]{2,1,0:T(8,128)(2,1)S(1)} %dynamic-slice_bitcast_fusion), channel_id=1, source_target_pairs={{0,16},{16,0},{32,48},{48,32},{64,80},{80,64},{96,112},{112,96},{1... | collective-permute-start | bytes 1966088 | tf_op jit(solution)/shard_map/ppermute | solution.py:679
  104.5 7.1 %collective-permute-start.5 = (bf16[768,128]{1,0:T(8,128)(2,1)S(1)}, bf16[768,128]{1,0:T(8,128)(2,1)S(1)}, u32[]{:S(2)}, u32[]{:S(2)}) collective-permute-start(bf16[768,128]{1,0:T(8,128)(2,1)S(1)} %copy-done.4), channel_id=1, source_target_pairs={{1,0},{2,1},{3,2},{4,3},{5,4},{6,5},{7,6},{8,7},{9,8},{10,9},{11,1... | collective-permute-start | bytes 589832 | tf_op jit(solution)/shard_map/ppermute | solution.py:607
  107.2 8.7 %collective-permute-start.6 = (bf16[768,128]{1,0:T(8,128)(2,1)S(1)}, bf16[768,128]{1,0:T(8,128)(2,1)S(1)}, u32[]{:S(2)}, u32[]{:S(2)}) collective-permute-start(bf16[768,128]{1,0:T(8,128)(2,1)S(1)} %copy-done.5), channel_id=1, source_target_pairs={{0,1},{1,2},{2,3},{3,4},{4,5},{5,6},{6,7},{7,8},{8,9},{9,10},{10,1... | collective-permute-start | bytes 589832 | tf_op jit(solution)/shard_map/ppermute | solution.py:606
  111.6 4.3 %copy-start.6 = (bf16[768,128]{1,0:T(8,128)(2,1)}, bf16[768,128]{1,0:T(8,128)(2,1)S(1)}, u32[]{:S(2)}) copy-start(bf16[768,128]{1,0:T(8,128)(2,1)S(1)} %collective-permute-done.5.refs_8_) | copy-start | bytes 589828
  115.9 0.7 copy-start.7
  124.8 1.1 copy-start.2
  125.9 34.5 %all-to-all-start.3 = ((bf16[16,360,128]{2,1,0:T(8,128)(2,1)}), bf16[16,360,128]{2,1,0:T(8,128)(2,1)}, u32[]{:S(2)}, u32[]{:S(2)}) async-start(bf16[16,360,128]{2,1,0:T(8,128)(2,1)} %get-tuple-element.60), calls=%async_computation.3 | async-start | bytes 2949120 | tf_op jit(solution)/shard_map/all_to_all | solution.py:658
  134.0 24.9 %collective-permute-start.10 = (bf16[64,1280]{1,0:T(8,128)(2,1)S(1)}, bf16[64,1280]{1,0:T(8,128)(2,1)S(1)}, u32[]{:S(2)}, u32[]{:S(2)}) collective-permute-start(bf16[64,1280]{1,0:T(8,128)(2,1)S(1)} %get-tuple-element.66), channel_id=1, source_target_pairs={{0,96},{16,112},{32,0},{48,16},{64,32},{80,48},{96,64},{112,80},{1... | collective-permute-start | bytes 491528 | tf_op jit(solution)/shard_map/ppermute | solution.py:688
  136.5 22.4 %collective-permute-start.8 = (bf16[64,1280]{1,0:T(8,128)(2,1)S(1)}, bf16[64,1280]{1,0:T(8,128)(2,1)S(1)}, u32[]{:S(2)}, u32[]{:S(2)}) collective-permute-start(bf16[64,1280]{1,0:T(8,128)(2,1)S(1)} %get-tuple-element.65), channel_id=1, source_target_pairs={{0,32},{16,48},{32,64},{48,80},{64,96},{80,112},{96,0},{112,16},{1... | collective-permute-start | bytes 491528 | tf_op jit(solution)/shard_map/ppermute | solution.py:688
  136.5 22.4 %collective-permute-start.9 = (bf16[64,1280]{1,0:T(8,128)(2,1)S(1)}, bf16[64,1280]{1,0:T(8,128)(2,1)S(1)}, u32[]{:S(2)}, u32[]{:S(2)}) collective-permute-start(bf16[64,1280]{1,0:T(8,128)(2,1)S(1)} %get-tuple-element.67), channel_id=1, source_target_pairs={{0,64},{16,80},{32,96},{48,112},{64,0},{80,16},{96,32},{112,48},{1... | collective-permute-start | bytes 491528 | tf_op jit(solution)/shard_map/ppermute | solution.py:688

commit v4 on v3

--- a/solution.py
+++ b/solution.py
@@ -212,11 +212,14 @@
 
 
 def place_weights(at_ref, piece_refs, w_t_ref, w_ref, parts):
+    chips = len(piece_refs)
     size = piece_refs[0].shape[0] // 2
-    pieces = [ref.at[k : k + size] for ref in piece_refs for k in range(0, ref.shape[0], size)]
-    for n, piece in enumerate(pieces):
-        place = 2 * (at_ref[0] ^ (n // 2)) + (at_ref[1] ^ (n % 2))
-        w_t_ref[pl.ds(pl.multiple_of(place * size, size), size), :] = piece[...]
+    for n, piece in enumerate(piece_refs):
+        chip = (at_ref[0] + (chips - n)) % chips
+        for half in range(2):
+            core = at_ref[1] if half == 0 else 1 - at_ref[1]
+            at = pl.multiple_of((2 * chip + core) * size, size)
+            w_t_ref[pl.ds(at, size), :] = piece[half * size : (half + 1) * size, :]
     row = 0
     for start, stop in parts:
         w_ref[row : row + stop - start, :] = w_t_ref[:, start:stop].T
@@ -279,12 +282,12 @@
 
 def column_specs(shape, pieces):
     _, feat, length = shape
-    span = pieces[0].shape[1]
-    hid = sum(piece.shape[0] for piece in pieces)
+    rows, span = pieces[0].shape
+    hid = rows * len(pieces)
     block = pl.BlockSpec((WIDE, feat, length), lambda i: (i, 0, 0))
     hidden = pl.BlockSpec((hid, WIDE * length), lambda i: (0, i))
-    specs = [pl.BlockSpec(piece.shape, lambda i: (0, 0), pipeline_mode=pl.Buffered(1)) for piece in pieces]
-    return hid, span, block, hidden, specs
+    piece = pl.BlockSpec((rows, span), lambda i: (0, 0), pipeline_mode=pl.Buffered(1))
+    return hid, span, block, hidden, [piece] * len(pieces)
 
 
 def physics_forward(at, x, pieces, cuts):
@@ -440,19 +443,21 @@
     rim_ref[0] = south_ref[...].astype(F32)
     rim_ref[1] = north_ref[...].astype(F32)
 
-    sources = jnp.concatenate([own_e_ref[...], from_e_ref[...], from_w_ref[...], own_w_ref[...]], axis=1)
-    k = iota((4 * LANE, LANE), 0)
-    lane = k % LANE
-    row_code = (k // LANE) * STEPS + lane % STEPS + 16 * ((lane // STEPS) % 8)
-    row_code = jnp.where(lane // GROUP == pl.program_id(0) + first, row_code, -1)
-    m = iota((1, LANE), 1)
-    picks = []
-    for kind in range(4):
-        col_code = m if kind == 0 else m % 16 + 16 * (nfield - 1 + kind)
-        col_code = jnp.where(m < 16 * nfield, col_code, -2)
-        picks.append(jnp.where(row_code == col_code, 1.0, 0.0).astype(BF16))
-    pick = jnp.concatenate(picks, axis=1)
-    strip_ref[...] = jnp.dot(sources, pick, preferred_element_type=F32)
+    @pl.when(pl.program_id(0) % (GROUP // LEVELS) == 0)
+    def _():
+        sources = jnp.concatenate([own_e_ref[...], from_e_ref[...], from_w_ref[...], own_w_ref[...]], axis=1)
+        k = iota((4 * LANE, LANE), 0)
+        lane = k % LANE
+        row_code = (k // LANE) * STEPS + lane % STEPS + 16 * ((lane // STEPS) % 8)
+        row_code = jnp.where(lane // GROUP == pl.program_id(0) // (GROUP // LEVELS) + first, row_code, -1)
+        m = iota((1, LANE), 1)
+        picks = []
+        for kind in range(4):
+            col_code = m if kind == 0 else m % 16 + 16 * (nfield - 1 + kind)
+            col_code = jnp.where(m < 16 * nfield, col_code, -2)
+            picks.append(jnp.where(row_code == col_code, 1.0, 0.0).astype(BF16))
+        pick = jnp.concatenate(picks, axis=1)
+        strip_ref[...] = jnp.dot(sources, pick, preferred_element_type=F32)
 
     @pl.when(pl.program_id(0) == 0)
     def _():
@@ -466,12 +471,14 @@
     lane = iota((part, LANE), 1)
     of_field = [jnp.where(lane // 16 == f, 1.0, 0.0).astype(BF16) for f in range(nfield)]
 
-    def levels(sub, carry):
+    sub = pl.program_id(0) % (GROUP // part)
+
+    def levels():
         def cell(a, t):
             if STEPS <= t < rows + STEPS:
-                return plane(fields_ref, coefs, a, pl.ds(sub * (part * rows) + t - STEPS, part, stride=rows))
+                return plane(fields_ref, coefs, a, pl.ds(t - STEPS, part, stride=rows))
             side, at = (0, t) if t < STEPS else (1, t - rows - STEPS)
-            return rim_ref[side, at, a, pl.ds(sub * part, part), :]
+            return rim_ref[side, at, a]
 
         def strip(kind, t):
             return strip_ref[pl.ds(t * GROUP + sub * part, part), kind * LANE : (kind + 1) * LANE]
@@ -539,10 +546,9 @@
                     if step < STEPS - 1:
                         state_ref[1 - cur, f, at] = value
                     else:
-                        out_ref[f, pl.ds(sub * (part * rows) + u - STEPS, part, stride=rows), :] = value
-        return carry
-
-    lax.fori_loop(0, GROUP // part, levels, 0)
+                        out_ref[f, pl.ds(u - STEPS, part, stride=rows), :] = value
+
+    levels()
 
 
 class Dynamics:
@@ -614,10 +620,11 @@
 
         fields = self.args[0]
         nfield = fields.shape[0]
-        chunk = GROUP * self.rows
-        fields_spec = pl.BlockSpec((nfield, chunk, LANE), lambda i: (0, i + first, 0))
-        coef_spec = pl.BlockSpec((chunk, LANE), lambda i: (i + first, 0))
-        rim_spec = pl.BlockSpec((STEPS, self.planes, GROUP, LANE), lambda i: (0, 0, i + first, 0))
+        chunk = LEVELS * self.rows
+        skip = first * (GROUP // LEVELS)
+        fields_spec = pl.BlockSpec((nfield, chunk, LANE), lambda i: (0, i + skip, 0))
+        coef_spec = pl.BlockSpec((chunk, LANE), lambda i: (i + skip, 0))
+        rim_spec = pl.BlockSpec((STEPS, self.planes, LEVELS, LANE), lambda i: (0, 0, i + skip, 0))
         specs = [fields_spec] + [coef_spec] * 3 + [rim_spec] * 2 + [self.strip_spec] * 4
         operands = self.args + rims + after(strips, start)
         aliases = {}
@@ -628,13 +635,13 @@
         cells = (self.rows + 2 * STEPS) * LEVELS
         return pl.pallas_call(
             kernel,
-            grid=(count,),
+            grid=(count * (GROUP // LEVELS),),
             in_specs=specs,
             out_specs=fields_spec,
             out_shape=jax.ShapeDtypeStruct(fields.shape, F32),
             input_output_aliases=aliases,
             scratch_shapes=[
-                pltpu.VMEM((2, STEPS, self.planes, GROUP, LANE), F32),
+                pltpu.VMEM((2, STEPS, self.planes, LEVELS, LANE), F32),
                 pltpu.VMEM((self.strip_rows, 4 * LANE), F32),
                 pltpu.VMEM((2, 5, cells, LANE), F32),
                 pltpu.VMEM((STEPS, nfield, cells, LANE), BF16),
@@ -660,14 +667,12 @@
 
 def spread(piece):
     size = lax.axis_size("lat")
-    held = [piece]
-    for flip in (1, 2, 4):
-        mine = jnp.concatenate(held, axis=0) if len(held) > 1 else held[0]
-        theirs = lax.ppermute(mine, "lat", [(i, i ^ flip) for i in range(size)])
-        held = [mine, theirs]
-        if flip == 2:
-            chips = held
-    return chips + [theirs]
+    other = lax.ppermute(piece, "lat", [(i, i ^ 1) for i in range(size)])
+    both = jnp.concatenate([piece, other], axis=0)
+    pieces = [both]
+    for shift in range(1, size // 2):
+        pieces.append(lax.ppermute(both, "lat", [(i, (i + 2 * shift) % size) for i in range(size)]))
+    return pieces
 
 
 def scattered(parts, start):

time: 170 us -> 167 us (0.982)
  starting transfers between devices: 52.9 us -> 50.5 us
    ppermute x1, starting transfers between devices: 6.5 us -> 3.5 us  [scattered(): other = lax.ppermute(other, 'lat', [(i, i ^ 1) for i in range(size)])]
    all_to_all x4, waiting for transfers between devices: 6.31 us -> 8.2 us  [exchange(): return lax.all_to_all(array, axis, split_axis=0, concat_axis=0, tiled=True)]
    ppermute x3 -> x4, starting transfers between devices: 4.72 us -> 6.58 us  [the longest x3 5.43 us: spread(): lax.ppermute(both, 'lat', [(i, (i + 2 * shift) % size) for i in range(siz...]
    ppermute x3 -> x4, waiting for transfers between devices: 6.91 us -> 6.21 us  [the longest x3 5.19 us: spread(): lax.ppermute(both, 'lat', [(i, (i + 2 * shift) % size) for i in range(siz...]
    unnamed x29 -> x33, local copies, waits for them, and re-layouts: 5.52 us -> 5.74 us
  transfers between devices with their start and end apart: 15 -> 16, of which waited for: 4 -> 6; matrix products, arithmetic and copies ran while one was open for 3% -> 3% of each run, Pallas kernels for 40% -> 40%
where the time goes in v4:
time: 167 us; the launch traced here: 166 us
  Pallas kernels  81.5 us (49%)
  starting transfers between devices  50.5 us (30%)
  waiting for transfers between devices  23.1 us (14%)
  local copies, waits for them, and re-layouts  8.38 us (5%)
  other arithmetic  2.14 us (1%)
    all_to_all x4, starting transfers between devices, exchange(): return lax.all_to_all(array, axis, split_axis=0, concat_axis=0, tiled=True)  30.4 us
    pallas_call x2, Pallas kernels, scatter_columns(): pl.pallas_call(kernel, grid=(rows // WIDE,), in_specs=specs, out_specs=pl...  17.6 us
    pallas_call x2, Pallas kernels, steps(): pl.pallas_call(kernel, grid=(count * (GROUP // LEVELS),), in_specs=specs,...  17 us
    pallas_call x1, Pallas kernels, physics_backward(): pl.pallas_call(kernel, grid=(nblock // WIDE,), in_specs=[pl.BlockSpec(mem...  12.9 us
    all_to_all x4, waiting for transfers between devices, exchange(): return lax.all_to_all(array, axis, split_axis=0, concat_axis=0, tiled=True)  8.2 us
    pallas_call x1, Pallas kernels, gather_first(): pl.pallas_call(kernel, grid=(nblock // WIDE,), in_specs=[scalars, scalars...  7.77 us
    pallas_call x1, Pallas kernels, gather_columns(): pl.pallas_call(kernel, grid=(nblock // WIDE,), in_specs=[pl.BlockSpec(tab...  7.51 us
    pallas_call x1, Pallas kernels, physics_forward(): pl.pallas_call(kernel, grid=(nblock // WIDE,), in_specs=[pl.BlockSpec(mem...  7.22 us
  transfers between devices with their start and end apart: 16, of which 6 were waited for; matrix products, arithmetic and copies ran while one was open for 3% of the time, Pallas kernels for 40%

profile of v4, /device:TPU:8, one launch (start us, length us, event | category | flops | bytes accessed | tf_op | source)
XLA Modules:
  0.0 166.4 jit_solution(15579888926421412983)
XLA Ops:
  0.6 7.8 %gather_first.1 = (bf16[16,360,128]{2,1,0:T(8,128)(2,1)}, s32[16,128]{1,0:T(8,128)}) custom-call(s32[1,1,16]{2,1,0:T(1,128)} %refs_0_.1, s32[1,1,16]{2,1,0:T(1,128)} %refs_1_.1, s32[16,1,128]{2,1,0:T(1,128)} %bitcast.71, f32[5760,128]{1,0:T(8,128)} %bitcast.45), custom_call_target="tpu_custom_call" | custom-call | flops 3019898880 | bytes 4423680 | tf_op jit(solution)/shard_map/gather_first/pallas_call | solution.py:91
  8.4 8.4 %all-to-all-start = ((bf16[16,360,128]{2,1,0:T(8,128)(2,1)}), bf16[16,360,128]{2,1,0:T(8,128)(2,1)S(1)}, u32[]{:S(2)}, u32[]{:S(2)}) async-start(bf16[16,360,128]{2,1,0:T(8,128)(2,1)} %get-tuple-element.35), calls=%async_computation | async-start | bytes 2949120 | tf_op jit(solution)/shard_map/all_to_all | solution.py:665
  16.8 4.5 %rims.1 = (bf16[4,7,96,128]{3,2,1,0:T(8,128)(2,1)}, bf16[4,7,96,128]{3,2,1,0:T(8,128)(2,1)}) custom-call(f32[4,1440,128]{2,1,0:T(8,128)} %bitcast.46, f32[1440,128]{1,0:T(8,128)} %bitcast.50, f32[1440,128]{1,0:T(8,128)} %bitcast.54, f32[1440,128]{1,0:T(8,128)} %bitcast.58), custom_call_target="tpu_custom_call" | custom-call | tf_op jit(solution)/shard_map/rims/pallas_call | solution.py:575
  21.3 7.5 %gather_columns.1 = bf16[16,360,128]{2,1,0:T(8,128)(2,1)} custom-call(s32[16,128]{1,0:T(8,128)} %get-tuple-element.41.refs_0_, bf16[5760,128]{1,0:T(8,128)(2,1)} %bitcast.70), custom_call_target="tpu_custom_call" | custom-call | flops 3019898880 | bytes 2949120 | tf_op jit(solution)/shard_map/gather_columns/pallas_call | solution.py:114
  28.9 8.2 %all-to-all-done.refs_1_ = bf16[16,360,128]{2,1,0:T(8,128)(2,1)S(1)} async-done(((bf16[16,360,128]{2,1,0:T(8,128)(2,1)}), bf16[16,360,128]{2,1,0:T(8,128)(2,1)S(1)}, u32[]{:S(2)}, u32[]{:S(2)}) %all-to-all-start) | async-done | bytes 1474592 | tf_op jit(solution)/shard_map/all_to_all | solution.py:665
  37.1 1.1 copy-done.3
  38.2 6.7 %all-to-all-start.2 = ((bf16[16,360,128]{2,1,0:T(8,128)(2,1)}), bf16[16,360,128]{2,1,0:T(8,128)(2,1)}, u32[]{:S(2)}, u32[]{:S(2)}) async-start(bf16[16,360,128]{2,1,0:T(8,128)(2,1)} %gather_columns.1), calls=%async_computation.2 | async-start | bytes 2949120 | tf_op jit(solution)/shard_map/all_to_all | solution.py:665
  44.9 1.3 collective-permute-start.1
  46.1 3.1 %collective-permute-start = (bf16[4,7,96,128]{3,2,1,0:T(8,128)(2,1)S(1)}, bf16[4,7,96,128]{3,2,1,0:T(8,128)(2,1)S(1)}, u32[]{:S(2)}, u32[]{:S(2)}) collective-permute-start(bf16[4,7,96,128]{3,2,1,0:T(8,128)(2,1)S(1)} %copy-done.12), channel_id=1, source_target_pairs={{0,16},{16,32},{32,48},{48,64},{64,80},{80,96},{96,112},{1,17},{17... | collective-permute-start | bytes 2064392 | tf_op jit(solution)/shard_map/ppermute | solution.py:587
  49.4 1.1 collective-permute-start.2
  50.5 1.0 collective-permute-done.2
  51.6 1.6 collective-permute-start.3
  53.1 2.4 %collective-permute-start.4 = (bf16[128,1280]{1,0:T(8,128)(2,1)S(1)}, bf16[128,1280]{1,0:T(8,128)(2,1)S(1)}, u32[]{:S(2)}, u32[]{:S(2)}) collective-permute-start(bf16[128,1280]{1,0:T(8,128)(2,1)S(1)} %constant_dynamic-update-slice_fusion.refs_2_.refs_5_), channel_id=1, source_target_pairs={{0,64},{16,80},{32,96},{48,112},{64,0},{80,16},{96,32},{112,48},{1... | collective-permute-start | bytes 983048 | tf_op jit(solution)/shard_map/ppermute | solution.py:674
  55.5 1.5 collective-permute-start.5
  59.3 6.9 %strips.1 = (bf16[768,128]{1,0:T(8,128)(2,1)}, bf16[768,128]{1,0:T(8,128)(2,1)}) custom-call(f32[4,1440,128]{2,1,0:T(8,128)} %bitcast.47, f32[1440,128]{1,0:T(8,128)} %bitcast.51, f32[1440,128]{1,0:T(8,128)} %bitcast.55, f32[1440,128]{1,0:T(8,128)} %bitcast.59, bf16[4,7,96,128]{3,2,1,0:T(8,128)(2,1)} %copy-done.1, bf16[4,7,96,128]{3,2,1,0:T(8,128)(2,1)} %copy-done), custom_call_target="tpu_custom_call" | custom-call | tf_op jit(solution)/shard_map/strips/pallas_call | solution.py:596
  66.3 4.9 %collective-permute-done.4.refs_4_.refs_7_ = bf16[128,1280]{1,0:T(8,128)(2,1)S(1)} collective-permute-done((bf16[128,1280]{1,0:T(8,128)(2,1)S(1)}, bf16[128,1280]{1,0:T(8,128)(2,1)S(1)}, u32[]{:S(2)}, u32[]{:S(2)}) %collective-permute-start.4) | collective-permute-done | bytes 327712 | tf_op jit(solution)/shard_map/ppermute | solution.py:674
  72.6 7.2 %physics_forward.1 = (bf16[16,360,128]{2,1,0:T(8,128)(2,1)}, f32[512,2048]{1,0:T(8,128)}, f32[512,2048]{1,0:T(8,128)}) custom-call(s32[2]{0:T(128)} %pad_add_fusion.refs_0_, bf16[16,360,128]{2,1,0:T(8,128)(2,1)} %copy-done.3, bf16[128,1280]{1,0:T(8,128)(2,1)} %copy-done.8, bf16[128,1280]{1,0:T(8,128)(2,1)} %copy-done.13, bf16[128,1280]{1,0:T(8,128)(2,1)} %copy-done.14, ...), custom_call_target="tpu_custom_call" | custom-call | flops 2583691264 | bytes 11337728 | tf_op jit(solution)/shard_map/physics_forward/pallas_call | solution.py:301
  79.8 7.3 %all-to-all-start.1 = ((bf16[16,360,128]{2,1,0:T(8,128)(2,1)}), bf16[16,360,128]{2,1,0:T(8,128)(2,1)S(1)}, u32[]{:S(2)}, u32[]{:S(2)}) async-start(bf16[16,360,128]{2,1,0:T(8,128)(2,1)} %get-tuple-element.47), calls=%async_computation.1 | async-start | bytes 2949120 | tf_op jit(solution)/shard_map/all_to_all | solution.py:665
  87.1 12.9 %physics_backward.1 = (bf16[16,360,128]{2,1,0:T(8,128)(2,1)}, bf16[512,1280]{1,0:T(8,128)(2,1)}) custom-call(s32[2]{0:T(128)} %pad_add_fusion.refs_0_, bf16[16,360,128]{2,1,0:T(8,128)(2,1)} %copy-done.3, bf16[16,360,128]{2,1,0:T(8,128)(2,1)} %all-to-all-done.2.refs_2_, f32[512,2048]{1,0:T(8,128)} %get-tuple-element.53.refs_3_, ...), custom_call_target="tpu_custom_call" | custom-call | flops 5167382528 | bytes 12812288 | tf_op jit(solution)/shard_map/physics_backward/pallas_call | solution.py:324
  100.0 1.1 dynamic-slice_bitcast_fusion
  101.1 3.5 %collective-permute-start.8 = (bf16[4,64,1280]{2,1,0:T(8,128)(2,1)S(1)}, bf16[4,64,1280]{2,1,0:T(8,128)(2,1)}, u32[]{:S(2)}, u32[]{:S(2)}) collective-permute-start(bf16[4,64,1280]{2,1,0:T(8,128)(2,1)S(1)} %dynamic-slice_bitcast_fusion), channel_id=1, source_target_pairs={{0,16},{16,0},{32,48},{48,32},{64,80},{80,64},{96,112},{112,96},{1... | collective-permute-start | bytes 1966088 | tf_op jit(solution)/shard_map/ppermute | solution.py:684
  104.6 2.7 %collective-permute-start.6 = (bf16[768,128]{1,0:T(8,128)(2,1)S(1)}, bf16[768,128]{1,0:T(8,128)(2,1)S(1)}, u32[]{:S(2)}, u32[]{:S(2)}) collective-permute-start(bf16[768,128]{1,0:T(8,128)(2,1)S(1)} %copy-done.4), channel_id=1, source_target_pairs={{1,0},{2,1},{3,2},{4,3},{5,4},{6,5},{7,6},{8,7},{9,8},{10,9},{11,1... | collective-permute-start | bytes 589832 | tf_op jit(solution)/shard_map/ppermute | solution.py:613
  107.3 4.4 %collective-permute-done.6.refs_8_ = bf16[768,128]{1,0:T(8,128)(2,1)S(1)} collective-permute-done((bf16[768,128]{1,0:T(8,128)(2,1)S(1)}, bf16[768,128]{1,0:T(8,128)(2,1)S(1)}, u32[]{:S(2)}, u32[]{:S(2)}) %collective-permute-start.6) | collective-permute-done | bytes 196640 | tf_op jit(solution)/shard_map/ppermute | solution.py:613
  111.7 4.3 %collective-permute-done.7.refs_9_ = bf16[768,128]{1,0:T(8,128)(2,1)S(1)} collective-permute-done((bf16[768,128]{1,0:T(8,128)(2,1)S(1)}, bf16[768,128]{1,0:T(8,128)(2,1)S(1)}, u32[]{:S(2)}, u32[]{:S(2)}) %collective-permute-start.7) | collective-permute-done | bytes 196640 | tf_op jit(solution)/shard_map/ppermute | solution.py:612
  116.7 6.3 %dynamics.2.refs_10_ = f32[4,1440,128]{2,1,0:T(8,128)} custom-call(f32[4,1440,128]{2,1,0:T(8,128)} %bitcast.48, f32[1440,128]{1,0:T(8,128)} %bitcast.52, f32[1440,128]{1,0:T(8,128)} %bitcast.56, f32[1440,128]{1,0:T(8,128)} %bitcast.60, bf16[4,7,96,128]{3,2,1,0:T(8,128)(2,1)} %copy-done.1, bf16[4,7,96,128]{3,2,1,0:T(8,128)(2,1)} %copy-done, ...), custom_call_target="tpu_custom_call" | custom-call | flops 14745600 | bytes 2703360 | tf_op jit(solution)/shard_map/dynamics/pallas_call | solution.py:636
  123.0 1.5 fusion.3
  124.6 1.1 copy-done.2
  125.7 8.0 %all-to-all-start.3 = ((bf16[16,360,128]{2,1,0:T(8,128)(2,1)}), bf16[16,360,128]{2,1,0:T(8,128)(2,1)}, u32[]{:S(2)}, u32[]{:S(2)}) async-start(bf16[16,360,128]{2,1,0:T(8,128)(2,1)} %get-tuple-element.60), calls=%async_computation.3 | async-start | bytes 2949120 | tf_op jit(solution)/shard_map/all_to_all | solution.py:665
  134.7 2.0 %collective-permute-start.9 = (bf16[64,1280]{1,0:T(8,128)(2,1)S(1)}, bf16[64,1280]{1,0:T(8,128)(2,1)S(1)}, u32[]{:S(2)}, u32[]{:S(2)}) collective-permute-start(bf16[64,1280]{1,0:T(8,128)(2,1)S(1)} %get-tuple-element.65), channel_id=1, source_target_pairs={{0,32},{16,48},{32,64},{48,80},{64,96},{80,112},{96,0},{112,16},{1... | collective-permute-start | bytes 491528 | tf_op jit(solution)/shard_map/ppermute | solution.py:693
  136.7 10.6 %dynamics.3 = f32[4,1440,128]{2,1,0:T(8,128)} custom-call(f32[4,1440,128]{2,1,0:T(8,128)} %bitcast.49, f32[1440,128]{1,0:T(8,128)} %bitcast.53, f32[1440,128]{1,0:T(8,128)} %bitcast.57, f32[1440,128]{1,0:T(8,128)} %bitcast.61, bf16[4,7,96,128]{3,2,1,0:T(8,128)(2,1)} %copy-done.1, bf16[4,7,96,128]{3,2,1,0:T(8,128)(2,1)} %copy-done, ...), custom_call_target="tpu_custom_call", output_to_operand_aliasing={{}: (10, {})} | custom-call | flops 29491200 | bytes 5406720 | tf_op jit(solution)/shard_map/dynamics/pallas_call | solution.py:636
  147.3 9.8 %scatter_columns.2 = f32[5760,128]{1,0:T(8,128)} custom-call(s32[16,128]{1,0:T(8,128)} %get-tuple-element.41.refs_0_, bf16[16,360,128]{2,1,0:T(8,128)(2,1)} %copy-done.2, f32[5760,128]{1,0:T(8,128)} %bitcast.62), custom_call_target="tpu_custom_call" | custom-call | flops 3019898880 | bytes 5898240 | tf_op jit(solution)/shard_map/scatter_columns/pallas_call | solution.py:182
  158.6 7.8 %scatter_columns.3 = bf16[5760,128]{1,0:T(8,128)(2,1)} custom-call(s32[16,128]{1,0:T(8,128)} %get-tuple-element.41.refs_0_, bf16[16,360,128]{2,1,0:T(8,128)(2,1)} %all-to-all-done.3.refs_1_), custom_call_target="tpu_custom_call" | custom-call | flops 3019898880 | bytes 5898240 | tf_op jit(solution)/shard_map/scatter_columns/pallas_call | solution.py:182
  (53 shorter events, 7.0 us)
Async XLA Ops:
  8.4 28.6 %all-to-all-start = ((bf16[16,360,128]{2,1,0:T(8,128)(2,1)}), bf16[16,360,128]{2,1,0:T(8,128)(2,1)S(1)}, u32[]{:S(2)}, u32[]{:S(2)}) async-start(bf16[16,360,128]{2,1,0:T(8,128)(2,1)} %get-tuple-element.35), calls=%async_computation | async-start | bytes 2949120 | tf_op jit(solution)/shard_map/all_to_all | solution.py:665
  28.9 17.3 %copy-start.12 = (bf16[4,7,96,128]{3,2,1,0:T(8,128)(2,1)S(1)}, bf16[4,7,96,128]{3,2,1,0:T(8,128)(2,1)}, u32[]{:S(2)}) copy-start(bf16[4,7,96,128]{3,2,1,0:T(8,128)(2,1)} %get-tuple-element.39) | copy-start | bytes 2064388
  28.9 20.4 %copy-start.9 = (bf16[1,512,64]{1,2,0:T(8,128)(2,1)S(1)}, bf16[1,512,64]{1,2,0:T(8,128)(2,1)}, u32[]{:S(2)}) copy-start(bf16[1,512,64]{1,2,0:T(8,128)(2,1)} %param.20) | copy-start | bytes 196612
  28.9 20.4 %copy-start.10 = (bf16[1,360,64]{1,2,0:T(8,128)(2,1)S(1)}, bf16[1,360,64]{1,2,0:T(8,128)(2,1)}, u32[]{:S(2)}) copy-start(bf16[1,360,64]{1,2,0:T(8,128)(2,1)} %param.19) | copy-start | bytes 138244
  28.9 20.4 %copy-start.11 = (bf16[1,360,64]{1,2,0:T(8,128)(2,1)S(1)}, bf16[1,360,64]{1,2,0:T(8,128)(2,1)}, u32[]{:S(2)}) copy-start(bf16[1,360,64]{1,2,0:T(8,128)(2,1)} %param.21) | copy-start | bytes 138244
  37.1 1.1 copy-start.3
  38.2 41.6 %all-to-all-start.2 = ((bf16[16,360,128]{2,1,0:T(8,128)(2,1)}), bf16[16,360,128]{2,1,0:T(8,128)(2,1)}, u32[]{:S(2)}, u32[]{:S(2)}) async-start(bf16[16,360,128]{2,1,0:T(8,128)(2,1)} %gather_columns.1), calls=%async_computation.2 | async-start | bytes 2949120 | tf_op jit(solution)/shard_map/all_to_all | solution.py:665
  44.9 12.7 %collective-permute-start.1 = (bf16[4,7,96,128]{3,2,1,0:T(8,128)(2,1)}, bf16[4,7,96,128]{3,2,1,0:T(8,128)(2,1)S(1)}, u32[]{:S(2)}, u32[]{:S(2)}) collective-permute-start(bf16[4,7,96,128]{3,2,1,0:T(8,128)(2,1)} %get-tuple-element.40), channel_id=1, source_target_pairs={{16,0},{32,16},{48,32},{64,48},{80,64},{96,80},{112,96},{17,1},{33... | collective-permute-start | bytes 2064392 | tf_op jit(solution)/shard_map/ppermute | solution.py:588
  46.1 11.4 %collective-permute-start = (bf16[4,7,96,128]{3,2,1,0:T(8,128)(2,1)S(1)}, bf16[4,7,96,128]{3,2,1,0:T(8,128)(2,1)S(1)}, u32[]{:S(2)}, u32[]{:S(2)}) collective-permute-start(bf16[4,7,96,128]{3,2,1,0:T(8,128)(2,1)S(1)} %copy-done.12), channel_id=1, source_target_pairs={{0,16},{16,32},{32,48},{48,64},{64,80},{80,96},{96,112},{1,17},{17... | collective-permute-start | bytes 2064392 | tf_op jit(solution)/shard_map/ppermute | solution.py:587
  49.4 2.2 %collective-permute-start.2 = (bf16[64,1280]{1,0:T(8,128)(2,1)S(1)}, bf16[64,1280]{1,0:T(8,128)(2,1)S(1)}, u32[]{:S(2)}, u32[]{:S(2)}) collective-permute-start(bf16[64,1280]{1,0:T(8,128)(2,1)S(1)} %bitcast.65), channel_id=1, source_target_pairs={{0,16},{16,0},{32,48},{48,32},{64,80},{80,64},{96,112},{112,96},{1... | collective-permute-start | bytes 491528 | tf_op jit(solution)/shard_map/ppermute | solution.py:670
  51.6 19.9 %copy-start.8 = (bf16[128,1280]{1,0:T(8,128)(2,1)}, bf16[128,1280]{1,0:T(8,128)(2,1)S(1)}, u32[]{:S(2)}) copy-start(bf16[128,1280]{1,0:T(8,128)(2,1)S(1)} %constant_dynamic-update-slice_fusion.refs_2_.refs_5_) | copy-start | bytes 983044
  51.6 14.7 %collective-permute-start.3 = (bf16[128,1280]{1,0:T(8,128)(2,1)S(1)}, bf16[128,1280]{1,0:T(8,128)(2,1)S(1)}, u32[]{:S(2)}, u32[]{:S(2)}) collective-permute-start(bf16[128,1280]{1,0:T(8,128)(2,1)S(1)} %constant_dynamic-update-slice_fusion.refs_2_.refs_5_), channel_id=1, source_target_pairs={{0,32},{16,48},{32,64},{48,80},{64,96},{80,112},{96,0},{112,16},{1... | collective-permute-start | bytes 983048 | tf_op jit(solution)/shard_map/ppermute | solution.py:674
  53.1 18.0 %collective-permute-start.4 = (bf16[128,1280]{1,0:T(8,128)(2,1)S(1)}, bf16[128,1280]{1,0:T(8,128)(2,1)S(1)}, u32[]{:S(2)}, u32[]{:S(2)}) collective-permute-start(bf16[128,1280]{1,0:T(8,128)(2,1)S(1)} %constant_dynamic-update-slice_fusion.refs_2_.refs_5_), channel_id=1, source_target_pairs={{0,64},{16,80},{32,96},{48,112},{64,0},{80,16},{96,32},{112,48},{1... | collective-permute-start | bytes 983048 | tf_op jit(solution)/shard_map/ppermute | solution.py:674
  55.5 15.9 %collective-permute-start.5 = (bf16[128,1280]{1,0:T(8,128)(2,1)S(1)}, bf16[128,1280]{1,0:T(8,128)(2,1)S(1)}, u32[]{:S(2)}, u32[]{:S(2)}) collective-permute-start(bf16[128,1280]{1,0:T(8,128)(2,1)S(1)} %constant_dynamic-update-slice_fusion.refs_2_.refs_5_), channel_id=1, source_target_pairs={{0,96},{16,112},{32,0},{48,16},{64,32},{80,48},{96,64},{112,80},{1... | collective-permute-start | bytes 983048 | tf_op jit(solution)/shard_map/ppermute | solution.py:674
  57.6 0.9 copy-start
  58.5 0.9 copy-start.1
  66.2 5.2 %copy-start.13 = (bf16[128,1280]{1,0:T(8,128)(2,1)}, bf16[128,1280]{1,0:T(8,128)(2,1)S(1)}, u32[]{:S(2)}) copy-start(bf16[128,1280]{1,0:T(8,128)(2,1)S(1)} %collective-permute-done.3.refs_3_.refs_6_) | copy-start | bytes 983044
  71.1 0.7 copy-start.14
  71.8 0.7 copy-start.15
  79.8 44.8 %all-to-all-start.1 = ((bf16[16,360,128]{2,1,0:T(8,128)(2,1)}), bf16[16,360,128]{2,1,0:T(8,128)(2,1)S(1)}, u32[]{:S(2)}, u32[]{:S(2)}) async-start(bf16[16,360,128]{2,1,0:T(8,128)(2,1)} %get-tuple-element.47), calls=%async_computation.1 | async-start | bytes 2949120 | tf_op jit(solution)/shard_map/all_to_all | solution.py:665
  87.0 17.6 %copy-start.4 = (bf16[768,128]{1,0:T(8,128)(2,1)S(1)}, bf16[768,128]{1,0:T(8,128)(2,1)}, u32[]{:S(2)}) copy-start(bf16[768,128]{1,0:T(8,128)(2,1)} %get-tuple-element.56.refs_6_) | copy-start | bytes 589828
  87.1 20.2 %copy-start.5 = (bf16[768,128]{1,0:T(8,128)(2,1)S(1)}, bf16[768,128]{1,0:T(8,128)(2,1)}, u32[]{:S(2)}) copy-start(bf16[768,128]{1,0:T(8,128)(2,1)} %get-tuple-element.57.refs_7_) | copy-start | bytes 589828
  101.1 21.9 %collective-permute-start.8 = (bf16[4,64,1280]{2,1,0:T(8,128)(2,1)S(1)}, bf16[4,64,1280]{2,1,0:T(8,128)(2,1)}, u32[]{:S(2)}, u32[]{:S(2)}) collective-permute-start(bf16[4,64,1280]{2,1,0:T(8,128)(2,1)S(1)} %dynamic-slice_bitcast_fusion), channel_id=1, source_target_pairs={{0,16},{16,0},{32,48},{48,32},{64,80},{80,64},{96,112},{112,96},{1... | collective-permute-start | bytes 1966088 | tf_op jit(solution)/shard_map/ppermute | solution.py:684
  104.6 7.1 %collective-permute-start.6 = (bf16[768,128]{1,0:T(8,128)(2,1)S(1)}, bf16[768,128]{1,0:T(8,128)(2,1)S(1)}, u32[]{:S(2)}, u32[]{:S(2)}) collective-permute-start(bf16[768,128]{1,0:T(8,128)(2,1)S(1)} %copy-done.4), channel_id=1, source_target_pairs={{1,0},{2,1},{3,2},{4,3},{5,4},{6,5},{7,6},{8,7},{9,8},{10,9},{11,1... | collective-permute-start | bytes 589832 | tf_op jit(solution)/shard_map/ppermute | solution.py:613
  107.3 8.7 %collective-permute-start.7 = (bf16[768,128]{1,0:T(8,128)(2,1)S(1)}, bf16[768,128]{1,0:T(8,128)(2,1)S(1)}, u32[]{:S(2)}, u32[]{:S(2)}) collective-permute-start(bf16[768,128]{1,0:T(8,128)(2,1)S(1)} %copy-done.5), channel_id=1, source_target_pairs={{0,1},{1,2},{2,3},{3,4},{4,5},{5,6},{6,7},{7,8},{8,9},{9,10},{10,1... | collective-permute-start | bytes 589832 | tf_op jit(solution)/shard_map/ppermute | solution.py:612
  111.7 4.3 %copy-start.6 = (bf16[768,128]{1,0:T(8,128)(2,1)}, bf16[768,128]{1,0:T(8,128)(2,1)S(1)}, u32[]{:S(2)}) copy-start(bf16[768,128]{1,0:T(8,128)(2,1)S(1)} %collective-permute-done.6.refs_8_) | copy-start | bytes 589828
  116.0 0.7 copy-start.7
  124.5 1.1 copy-start.2
  125.7 32.9 %all-to-all-start.3 = ((bf16[16,360,128]{2,1,0:T(8,128)(2,1)}), bf16[16,360,128]{2,1,0:T(8,128)(2,1)}, u32[]{:S(2)}, u32[]{:S(2)}) async-start(bf16[16,360,128]{2,1,0:T(8,128)(2,1)} %get-tuple-element.60), calls=%async_computation.3 | async-start | bytes 2949120 | tf_op jit(solution)/shard_map/all_to_all | solution.py:665
  133.7 23.4 %collective-permute-start.10 = (bf16[64,1280]{1,0:T(8,128)(2,1)S(1)}, bf16[64,1280]{1,0:T(8,128)(2,1)S(1)}, u32[]{:S(2)}, u32[]{:S(2)}) collective-permute-start(bf16[64,1280]{1,0:T(8,128)(2,1)S(1)} %get-tuple-element.67), channel_id=1, source_target_pairs={{0,64},{16,80},{32,96},{48,112},{64,0},{80,16},{96,32},{112,48},{1... | collective-permute-start | bytes 491528 | tf_op jit(solution)/shard_map/ppermute | solution.py:693
  134.7 22.5 %collective-permute-start.11 = (bf16[64,1280]{1,0:T(8,128)(2,1)S(1)}, bf16[64,1280]{1,0:T(8,128)(2,1)S(1)}, u32[]{:S(2)}, u32[]{:S(2)}) collective-permute-start(bf16[64,1280]{1,0:T(8,128)(2,1)S(1)} %get-tuple-element.66), channel_id=1, source_target_pairs={{0,96},{16,112},{32,0},{48,16},{64,32},{80,48},{96,64},{112,80},{1... | collective-permute-start | bytes 491528 | tf_op jit(solution)/shard_map/ppermute | solution.py:693
  134.7 22.5 %collective-permute-start.9 = (bf16[64,1280]{1,0:T(8,128)(2,1)S(1)}, bf16[64,1280]{1,0:T(8,128)(2,1)S(1)}, u32[]{:S(2)}, u32[]{:S(2)}) collective-permute-start(bf16[64,1280]{1,0:T(8,128)(2,1)S(1)} %get-tuple-element.65), channel_id=1, source_target_pairs={{0,32},{16,48},{32,64},{48,80},{64,96},{80,112},{96,0},{112,16},{1... | collective-permute-start | bytes 491528 | tf_op jit(solution)/shard_map/ppermute | solution.py:693

commit v5 on v4

--- a/solution.py
+++ b/solution.py
@@ -8,6 +8,7 @@
 
 STEPS = 4
 LANE = 128
+SPAN = 8
 WIDE = 4
 GROUP = 32
 LEVELS = 16
@@ -26,11 +27,11 @@
 
 def gather_blocks(table_ref, mat_ref, out_ref):
     ncol = mat_ref.shape[1]
-    first = pl.program_id(0) * WIDE
+    first = pl.program_id(0) * SPAN
     column = iota((ncol, LANE), 0)
-    hot = [jnp.where(column == table_ref[pl.ds(first + b, 1), :], 1.0, 0.0).astype(BF16) for b in range(WIDE)]
+    hot = [jnp.where(column == table_ref[pl.ds(first + b, 1), :], 1.0, 0.0).astype(BF16) for b in range(SPAN)]
     got = jnp.dot(mat_ref[...], jnp.concatenate(hot, axis=1), preferred_element_type=F32).astype(BF16)
-    for b in range(WIDE):
+    for b in range(SPAN):
         out_ref[b] = got[:, b * LANE : (b + 1) * LANE]
 
 
@@ -69,7 +70,7 @@
 
 def gather_parts(source, nblock, feat, rows):
     once = pl.BlockSpec(source.shape, lambda i: (0, 0), pipeline_mode=pl.Buffered(1))
-    out = pl.BlockSpec((WIDE, feat, LANE), lambda i: (i, 0, 0))
+    out = pl.BlockSpec((SPAN, feat, LANE), lambda i: (i, 0, 0))
     shape = jax.ShapeDtypeStruct((nblock, feat, LANE), BF16)
     cost = pl.CostEstimate(
         flops=2 * feat * rows * LANE * nblock * LANE,
@@ -90,7 +91,7 @@
     scalars = pl.BlockSpec(memory_space=pltpu.SMEM)
     return pl.pallas_call(
         kernel,
-        grid=(nblock // WIDE,),
+        grid=(nblock // SPAN,),
         in_specs=[scalars, scalars, pl.BlockSpec(cols.shape, lambda i: (0, 0, 0)), pl.BlockSpec(memory_space=pl.ANY)],
         out_specs=[out, pl.BlockSpec(table.shape, lambda i: (0, 0))],
         out_shape=[shape, table],
@@ -113,7 +114,7 @@
 
     return pl.pallas_call(
         kernel,
-        grid=(nblock // WIDE,),
+        grid=(nblock // SPAN,),
         in_specs=[pl.BlockSpec(table.shape, lambda i: (0, 0)), once],
         out_specs=out,
         out_shape=shape,
@@ -136,22 +137,22 @@
             where_ref[b * LANE : (b + 1) * LANE, :] = column.astype(jnp.int32)
 
     where = where_ref[...]
-    lane = iota(where.shape, 1) + pl.program_id(0) * (WIDE * LANE)
-    hot = [jnp.where(where == lane + r * LANE, 1.0, 0.0).astype(BF16) for r in range(WIDE)]
+    lane = iota(where.shape, 1) + pl.program_id(0) * (SPAN * LANE)
+    hot = [jnp.where(where == lane + r * LANE, 1.0, 0.0).astype(BF16) for r in range(SPAN)]
     return jnp.dot(mat_ref[...], jnp.concatenate(hot, axis=1), preferred_element_type=F32)
 
 
 def scatter_add_kernel(table_ref, blocks_ref, base_ref, out_ref, mat_ref, where_ref, *, rows):
     got = scatter_rows(table_ref, blocks_ref, mat_ref, where_ref)
-    for r in range(WIDE):
-        at = pl.ds(pl.program_id(0) * WIDE + r, mat_ref.shape[0], stride=rows)
+    for r in range(SPAN):
+        at = pl.ds(pl.program_id(0) * SPAN + r, mat_ref.shape[0], stride=rows)
         out_ref[at, :] = base_ref[at, :] + got[:, r * LANE : (r + 1) * LANE]
 
 
 def scatter_kernel(table_ref, blocks_ref, out_ref, mat_ref, where_ref, full_ref, *, rows):
     got = scatter_rows(table_ref, blocks_ref, mat_ref, where_ref)
-    for r in range(WIDE):
-        at = pl.ds(pl.program_id(0) * WIDE + r, mat_ref.shape[0], stride=rows)
+    for r in range(SPAN):
+        at = pl.ds(pl.program_id(0) * SPAN + r, mat_ref.shape[0], stride=rows)
         full_ref[at, :] = got[:, r * LANE : (r + 1) * LANE]
 
     @pl.when(pl.program_id(0) == pl.num_programs(0) - 1)
@@ -181,7 +182,7 @@
 
     return pl.pallas_call(
         kernel,
-        grid=(rows // WIDE,),
+        grid=(rows // SPAN,),
         in_specs=specs,
         out_specs=pl.BlockSpec(shape, lambda i: (0, 0)),
         out_shape=jax.ShapeDtypeStruct(shape, dtype),

time: 167 us -> 166 us (level)
  transfers between devices with their start and end apart: 16 -> 16, of which waited for: 6 -> 6; matrix products, arithmetic and copies ran while one was open for 3% -> 3% of each run, Pallas kernels for 40% -> 39%
where the time goes in v5:
time: 166 us; the launch traced here: 165 us
  Pallas kernels  80.3 us (48%)
  starting transfers between devices  50.5 us (30%)
  waiting for transfers between devices  23.4 us (14%)
  local copies, waits for them, and re-layouts  8.38 us (5%)
  other arithmetic  2.14 us (1%)
    all_to_all x4, starting transfers between devices, exchange(): return lax.all_to_all(array, axis, split_axis=0, concat_axis=0, tiled=True)  30.4 us
    pallas_call x2, Pallas kernels, steps(): pl.pallas_call(kernel, grid=(count * (GROUP // LEVELS),), in_specs=specs,...  17 us
    pallas_call x2, Pallas kernels, scatter_columns(): pl.pallas_call(kernel, grid=(rows // SPAN,), in_specs=specs, out_specs=pl...  16.9 us
    pallas_call x1, Pallas kernels, physics_backward(): pl.pallas_call(kernel, grid=(nblock // WIDE,), in_specs=[pl.BlockSpec(mem...  12.9 us
    all_to_all x4, waiting for transfers between devices, exchange(): return lax.all_to_all(array, axis, split_axis=0, concat_axis=0, tiled=True)  8.42 us
    pallas_call x1, Pallas kernels, gather_first(): pl.pallas_call(kernel, grid=(nblock // SPAN,), in_specs=[scalars, scalars...  7.53 us
    pallas_call x1, Pallas kernels, gather_columns(): pl.pallas_call(kernel, grid=(nblock // SPAN,), in_specs=[pl.BlockSpec(tab...  7.28 us
    pallas_call x1, Pallas kernels, physics_forward(): pl.pallas_call(kernel, grid=(nblock // WIDE,), in_specs=[pl.BlockSpec(mem...  7.21 us
  transfers between devices with their start and end apart: 16, of which 6 were waited for; matrix products, arithmetic and copies ran while one was open for 3% of the time, Pallas kernels for 39%

profile of v5, /device:TPU:8, one launch (start us, length us, event | category | flops | bytes accessed | tf_op | source)
XLA Modules:
  0.0 165.4 jit_solution(13025645312266876043)
XLA Ops:
  0.6 7.5 %gather_first.1 = (bf16[16,360,128]{2,1,0:T(8,128)(2,1)}, s32[16,128]{1,0:T(8,128)}) custom-call(s32[1,1,16]{2,1,0:T(1,128)} %refs_0_.1, s32[1,1,16]{2,1,0:T(1,128)} %refs_1_.1, s32[16,1,128]{2,1,0:T(1,128)} %bitcast.71, f32[5760,128]{1,0:T(8,128)} %bitcast.45), custom_call_target="tpu_custom_call" | custom-call | flops 3019898880 | bytes 4423680 | tf_op jit(solution)/shard_map/gather_first/pallas_call | solution.py:92
  8.2 8.4 %all-to-all-start = ((bf16[16,360,128]{2,1,0:T(8,128)(2,1)}), bf16[16,360,128]{2,1,0:T(8,128)(2,1)S(1)}, u32[]{:S(2)}, u32[]{:S(2)}) async-start(bf16[16,360,128]{2,1,0:T(8,128)(2,1)} %get-tuple-element.35), calls=%async_computation | async-start | bytes 2949120 | tf_op jit(solution)/shard_map/all_to_all | solution.py:666
  16.6 4.5 %rims.1 = (bf16[4,7,96,128]{3,2,1,0:T(8,128)(2,1)}, bf16[4,7,96,128]{3,2,1,0:T(8,128)(2,1)}) custom-call(f32[4,1440,128]{2,1,0:T(8,128)} %bitcast.46, f32[1440,128]{1,0:T(8,128)} %bitcast.50, f32[1440,128]{1,0:T(8,128)} %bitcast.54, f32[1440,128]{1,0:T(8,128)} %bitcast.58), custom_call_target="tpu_custom_call" | custom-call | tf_op jit(solution)/shard_map/rims/pallas_call | solution.py:576
  21.1 7.3 %gather_columns.1 = bf16[16,360,128]{2,1,0:T(8,128)(2,1)} custom-call(s32[16,128]{1,0:T(8,128)} %get-tuple-element.41.refs_0_, bf16[5760,128]{1,0:T(8,128)(2,1)} %bitcast.70), custom_call_target="tpu_custom_call" | custom-call | flops 3019898880 | bytes 2949120 | tf_op jit(solution)/shard_map/gather_columns/pallas_call | solution.py:115
  28.4 8.4 %all-to-all-done.refs_1_ = bf16[16,360,128]{2,1,0:T(8,128)(2,1)S(1)} async-done(((bf16[16,360,128]{2,1,0:T(8,128)(2,1)}), bf16[16,360,128]{2,1,0:T(8,128)(2,1)S(1)}, u32[]{:S(2)}, u32[]{:S(2)}) %all-to-all-start) | async-done | bytes 1474592 | tf_op jit(solution)/shard_map/all_to_all | solution.py:666
  36.8 1.1 copy-done.3
  37.9 6.7 %all-to-all-start.2 = ((bf16[16,360,128]{2,1,0:T(8,128)(2,1)}), bf16[16,360,128]{2,1,0:T(8,128)(2,1)}, u32[]{:S(2)}, u32[]{:S(2)}) async-start(bf16[16,360,128]{2,1,0:T(8,128)(2,1)} %gather_columns.1), calls=%async_computation.2 | async-start | bytes 2949120 | tf_op jit(solution)/shard_map/all_to_all | solution.py:666
  44.6 1.3 collective-permute-start.1
  45.9 3.1 %collective-permute-start = (bf16[4,7,96,128]{3,2,1,0:T(8,128)(2,1)S(1)}, bf16[4,7,96,128]{3,2,1,0:T(8,128)(2,1)S(1)}, u32[]{:S(2)}, u32[]{:S(2)}) collective-permute-start(bf16[4,7,96,128]{3,2,1,0:T(8,128)(2,1)S(1)} %copy-done.12), channel_id=1, source_target_pairs={{0,16},{16,32},{32,48},{48,64},{64,80},{80,96},{96,112},{1,17},{17... | collective-permute-start | bytes 2064392 | tf_op jit(solution)/shard_map/ppermute | solution.py:588
  49.1 1.1 collective-permute-start.2
  50.3 1.0 collective-permute-done.2
  51.3 1.6 collective-permute-start.3
  52.9 2.4 %collective-permute-start.4 = (bf16[128,1280]{1,0:T(8,128)(2,1)S(1)}, bf16[128,1280]{1,0:T(8,128)(2,1)S(1)}, u32[]{:S(2)}, u32[]{:S(2)}) collective-permute-start(bf16[128,1280]{1,0:T(8,128)(2,1)S(1)} %constant_dynamic-update-slice_fusion.refs_2_.refs_5_), channel_id=1, source_target_pairs={{0,64},{16,80},{32,96},{48,112},{64,0},{80,16},{96,32},{112,48},{1... | collective-permute-start | bytes 983048 | tf_op jit(solution)/shard_map/ppermute | solution.py:675
  55.3 1.5 collective-permute-start.5
  59.1 6.9 %strips.1 = (bf16[768,128]{1,0:T(8,128)(2,1)}, bf16[768,128]{1,0:T(8,128)(2,1)}) custom-call(f32[4,1440,128]{2,1,0:T(8,128)} %bitcast.47, f32[1440,128]{1,0:T(8,128)} %bitcast.51, f32[1440,128]{1,0:T(8,128)} %bitcast.55, f32[1440,128]{1,0:T(8,128)} %bitcast.59, bf16[4,7,96,128]{3,2,1,0:T(8,128)(2,1)} %copy-done.1, bf16[4,7,96,128]{3,2,1,0:T(8,128)(2,1)} %copy-done), custom_call_target="tpu_custom_call" | custom-call | tf_op jit(solution)/shard_map/strips/pallas_call | solution.py:597
  66.0 4.9 %collective-permute-done.4.refs_4_.refs_7_ = bf16[128,1280]{1,0:T(8,128)(2,1)S(1)} collective-permute-done((bf16[128,1280]{1,0:T(8,128)(2,1)S(1)}, bf16[128,1280]{1,0:T(8,128)(2,1)S(1)}, u32[]{:S(2)}, u32[]{:S(2)}) %collective-permute-start.4) | collective-permute-done | bytes 327712 | tf_op jit(solution)/shard_map/ppermute | solution.py:675
  72.3 7.2 %physics_forward.1 = (bf16[16,360,128]{2,1,0:T(8,128)(2,1)}, f32[512,2048]{1,0:T(8,128)}, f32[512,2048]{1,0:T(8,128)}) custom-call(s32[2]{0:T(128)} %pad_add_fusion.refs_0_, bf16[16,360,128]{2,1,0:T(8,128)(2,1)} %copy-done.3, bf16[128,1280]{1,0:T(8,128)(2,1)} %copy-done.8, bf16[128,1280]{1,0:T(8,128)(2,1)} %copy-done.13, bf16[128,1280]{1,0:T(8,128)(2,1)} %copy-done.14, ...), custom_call_target="tpu_custom_call" | custom-call | flops 2583691264 | bytes 11337728 | tf_op jit(solution)/shard_map/physics_forward/pallas_call | solution.py:302
  79.5 7.3 %all-to-all-start.1 = ((bf16[16,360,128]{2,1,0:T(8,128)(2,1)}), bf16[16,360,128]{2,1,0:T(8,128)(2,1)S(1)}, u32[]{:S(2)}, u32[]{:S(2)}) async-start(bf16[16,360,128]{2,1,0:T(8,128)(2,1)} %get-tuple-element.47), calls=%async_computation.1 | async-start | bytes 2949120 | tf_op jit(solution)/shard_map/all_to_all | solution.py:666
  86.8 12.9 %physics_backward.1 = (bf16[16,360,128]{2,1,0:T(8,128)(2,1)}, bf16[512,1280]{1,0:T(8,128)(2,1)}) custom-call(s32[2]{0:T(128)} %pad_add_fusion.refs_0_, bf16[16,360,128]{2,1,0:T(8,128)(2,1)} %copy-done.3, bf16[16,360,128]{2,1,0:T(8,128)(2,1)} %all-to-all-done.2.refs_2_, f32[512,2048]{1,0:T(8,128)} %get-tuple-element.53.refs_3_, ...), custom_call_target="tpu_custom_call" | custom-call | flops 5167382528 | bytes 12812288 | tf_op jit(solution)/shard_map/physics_backward/pallas_call | solution.py:325
  99.7 1.1 dynamic-slice_bitcast_fusion
  100.9 3.5 %collective-permute-start.8 = (bf16[4,64,1280]{2,1,0:T(8,128)(2,1)S(1)}, bf16[4,64,1280]{2,1,0:T(8,128)(2,1)}, u32[]{:S(2)}, u32[]{:S(2)}) collective-permute-start(bf16[4,64,1280]{2,1,0:T(8,128)(2,1)S(1)} %dynamic-slice_bitcast_fusion), channel_id=1, source_target_pairs={{0,16},{16,0},{32,48},{48,32},{64,80},{80,64},{96,112},{112,96},{1... | collective-permute-start | bytes 1966088 | tf_op jit(solution)/shard_map/ppermute | solution.py:685
  104.4 2.7 %collective-permute-start.6 = (bf16[768,128]{1,0:T(8,128)(2,1)S(1)}, bf16[768,128]{1,0:T(8,128)(2,1)S(1)}, u32[]{:S(2)}, u32[]{:S(2)}) collective-permute-start(bf16[768,128]{1,0:T(8,128)(2,1)S(1)} %copy-done.4), channel_id=1, source_target_pairs={{1,0},{2,1},{3,2},{4,3},{5,4},{6,5},{7,6},{8,7},{9,8},{10,9},{11,1... | collective-permute-start | bytes 589832 | tf_op jit(solution)/shard_map/ppermute | solution.py:614
  107.1 4.4 %collective-permute-done.6.refs_8_ = bf16[768,128]{1,0:T(8,128)(2,1)S(1)} collective-permute-done((bf16[768,128]{1,0:T(8,128)(2,1)S(1)}, bf16[768,128]{1,0:T(8,128)(2,1)S(1)}, u32[]{:S(2)}, u32[]{:S(2)}) %collective-permute-start.6) | collective-permute-done | bytes 196640 | tf_op jit(solution)/shard_map/ppermute | solution.py:614
  111.5 4.3 %collective-permute-done.7.refs_9_ = bf16[768,128]{1,0:T(8,128)(2,1)S(1)} collective-permute-done((bf16[768,128]{1,0:T(8,128)(2,1)S(1)}, bf16[768,128]{1,0:T(8,128)(2,1)S(1)}, u32[]{:S(2)}, u32[]{:S(2)}) %collective-permute-start.7) | collective-permute-done | bytes 196640 | tf_op jit(solution)/shard_map/ppermute | solution.py:613
  116.5 6.3 %dynamics.2.refs_10_ = f32[4,1440,128]{2,1,0:T(8,128)} custom-call(f32[4,1440,128]{2,1,0:T(8,128)} %bitcast.48, f32[1440,128]{1,0:T(8,128)} %bitcast.52, f32[1440,128]{1,0:T(8,128)} %bitcast.56, f32[1440,128]{1,0:T(8,128)} %bitcast.60, bf16[4,7,96,128]{3,2,1,0:T(8,128)(2,1)} %copy-done.1, bf16[4,7,96,128]{3,2,1,0:T(8,128)(2,1)} %copy-done, ...), custom_call_target="tpu_custom_call" | custom-call | flops 14745600 | bytes 2703360 | tf_op jit(solution)/shard_map/dynamics/pallas_call | solution.py:637
  122.8 1.5 fusion.3
  124.3 1.1 copy-done.2
  125.4 8.0 %all-to-all-start.3 = ((bf16[16,360,128]{2,1,0:T(8,128)(2,1)}), bf16[16,360,128]{2,1,0:T(8,128)(2,1)}, u32[]{:S(2)}, u32[]{:S(2)}) async-start(bf16[16,360,128]{2,1,0:T(8,128)(2,1)} %get-tuple-element.60), calls=%async_computation.3 | async-start | bytes 2949120 | tf_op jit(solution)/shard_map/all_to_all | solution.py:666
  134.4 2.0 %collective-permute-start.9 = (bf16[64,1280]{1,0:T(8,128)(2,1)S(1)}, bf16[64,1280]{1,0:T(8,128)(2,1)S(1)}, u32[]{:S(2)}, u32[]{:S(2)}) collective-permute-start(bf16[64,1280]{1,0:T(8,128)(2,1)S(1)} %get-tuple-element.65), channel_id=1, source_target_pairs={{0,32},{16,48},{32,64},{48,80},{64,96},{80,112},{96,0},{112,16},{1... | collective-permute-start | bytes 491528 | tf_op jit(solution)/shard_map/ppermute | solution.py:694
  136.4 10.6 %dynamics.3 = f32[4,1440,128]{2,1,0:T(8,128)} custom-call(f32[4,1440,128]{2,1,0:T(8,128)} %bitcast.49, f32[1440,128]{1,0:T(8,128)} %bitcast.53, f32[1440,128]{1,0:T(8,128)} %bitcast.57, f32[1440,128]{1,0:T(8,128)} %bitcast.61, bf16[4,7,96,128]{3,2,1,0:T(8,128)(2,1)} %copy-done.1, bf16[4,7,96,128]{3,2,1,0:T(8,128)(2,1)} %copy-done, ...), custom_call_target="tpu_custom_call", output_to_operand_aliasing={{}: (10, {})} | custom-call | flops 29491200 | bytes 5406720 | tf_op jit(solution)/shard_map/dynamics/pallas_call | solution.py:637
  147.1 9.4 %scatter_columns.2 = f32[5760,128]{1,0:T(8,128)} custom-call(s32[16,128]{1,0:T(8,128)} %get-tuple-element.41.refs_0_, bf16[16,360,128]{2,1,0:T(8,128)(2,1)} %copy-done.2, f32[5760,128]{1,0:T(8,128)} %bitcast.62), custom_call_target="tpu_custom_call" | custom-call | flops 3019898880 | bytes 5898240 | tf_op jit(solution)/shard_map/scatter_columns/pallas_call | solution.py:183
  157.9 7.5 %scatter_columns.3 = bf16[5760,128]{1,0:T(8,128)(2,1)} custom-call(s32[16,128]{1,0:T(8,128)} %get-tuple-element.41.refs_0_, bf16[16,360,128]{2,1,0:T(8,128)(2,1)} %all-to-all-done.3.refs_1_), custom_call_target="tpu_custom_call" | custom-call | flops 3019898880 | bytes 5898240 | tf_op jit(solution)/shard_map/scatter_columns/pallas_call | solution.py:183
  (53 shorter events, 7.0 us)
Async XLA Ops:
  8.2 28.6 %all-to-all-start = ((bf16[16,360,128]{2,1,0:T(8,128)(2,1)}), bf16[16,360,128]{2,1,0:T(8,128)(2,1)S(1)}, u32[]{:S(2)}, u32[]{:S(2)}) async-start(bf16[16,360,128]{2,1,0:T(8,128)(2,1)} %get-tuple-element.35), calls=%async_computation | async-start | bytes 2949120 | tf_op jit(solution)/shard_map/all_to_all | solution.py:666
  28.4 17.5 %copy-start.12 = (bf16[4,7,96,128]{3,2,1,0:T(8,128)(2,1)S(1)}, bf16[4,7,96,128]{3,2,1,0:T(8,128)(2,1)}, u32[]{:S(2)}) copy-start(bf16[4,7,96,128]{3,2,1,0:T(8,128)(2,1)} %get-tuple-element.39) | copy-start | bytes 2064388
  28.4 20.6 %copy-start.9 = (bf16[1,512,64]{1,2,0:T(8,128)(2,1)S(1)}, bf16[1,512,64]{1,2,0:T(8,128)(2,1)}, u32[]{:S(2)}) copy-start(bf16[1,512,64]{1,2,0:T(8,128)(2,1)} %param.20) | copy-start | bytes 196612
  28.4 20.6 %copy-start.10 = (bf16[1,360,64]{1,2,0:T(8,128)(2,1)S(1)}, bf16[1,360,64]{1,2,0:T(8,128)(2,1)}, u32[]{:S(2)}) copy-start(bf16[1,360,64]{1,2,0:T(8,128)(2,1)} %param.19) | copy-start | bytes 138244
  28.4 20.6 %copy-start.11 = (bf16[1,360,64]{1,2,0:T(8,128)(2,1)S(1)}, bf16[1,360,64]{1,2,0:T(8,128)(2,1)}, u32[]{:S(2)}) copy-start(bf16[1,360,64]{1,2,0:T(8,128)(2,1)} %param.21) | copy-start | bytes 138244
  36.8 1.1 copy-start.3
  37.9 41.6 %all-to-all-start.2 = ((bf16[16,360,128]{2,1,0:T(8,128)(2,1)}), bf16[16,360,128]{2,1,0:T(8,128)(2,1)}, u32[]{:S(2)}, u32[]{:S(2)}) async-start(bf16[16,360,128]{2,1,0:T(8,128)(2,1)} %gather_columns.1), calls=%async_computation.2 | async-start | bytes 2949120 | tf_op jit(solution)/shard_map/all_to_all | solution.py:666
  44.6 12.7 %collective-permute-start.1 = (bf16[4,7,96,128]{3,2,1,0:T(8,128)(2,1)}, bf16[4,7,96,128]{3,2,1,0:T(8,128)(2,1)S(1)}, u32[]{:S(2)}, u32[]{:S(2)}) collective-permute-start(bf16[4,7,96,128]{3,2,1,0:T(8,128)(2,1)} %get-tuple-element.40), channel_id=1, source_target_pairs={{16,0},{32,16},{48,32},{64,48},{80,64},{96,80},{112,96},{17,1},{33... | collective-permute-start | bytes 2064392 | tf_op jit(solution)/shard_map/ppermute | solution.py:589
  45.9 11.5 %collective-permute-start = (bf16[4,7,96,128]{3,2,1,0:T(8,128)(2,1)S(1)}, bf16[4,7,96,128]{3,2,1,0:T(8,128)(2,1)S(1)}, u32[]{:S(2)}, u32[]{:S(2)}) collective-permute-start(bf16[4,7,96,128]{3,2,1,0:T(8,128)(2,1)S(1)} %copy-done.12), channel_id=1, source_target_pairs={{0,16},{16,32},{32,48},{48,64},{64,80},{80,96},{96,112},{1,17},{17... | collective-permute-start | bytes 2064392 | tf_op jit(solution)/shard_map/ppermute | solution.py:588
  49.1 2.2 %collective-permute-start.2 = (bf16[64,1280]{1,0:T(8,128)(2,1)S(1)}, bf16[64,1280]{1,0:T(8,128)(2,1)S(1)}, u32[]{:S(2)}, u32[]{:S(2)}) collective-permute-start(bf16[64,1280]{1,0:T(8,128)(2,1)S(1)} %bitcast.65), channel_id=1, source_target_pairs={{0,16},{16,0},{32,48},{48,32},{64,80},{80,64},{96,112},{112,96},{1... | collective-permute-start | bytes 491528 | tf_op jit(solution)/shard_map/ppermute | solution.py:671
  51.3 19.9 %copy-start.8 = (bf16[128,1280]{1,0:T(8,128)(2,1)}, bf16[128,1280]{1,0:T(8,128)(2,1)S(1)}, u32[]{:S(2)}) copy-start(bf16[128,1280]{1,0:T(8,128)(2,1)S(1)} %constant_dynamic-update-slice_fusion.refs_2_.refs_5_) | copy-start | bytes 983044
  51.3 14.7 %collective-permute-start.3 = (bf16[128,1280]{1,0:T(8,128)(2,1)S(1)}, bf16[128,1280]{1,0:T(8,128)(2,1)S(1)}, u32[]{:S(2)}, u32[]{:S(2)}) collective-permute-start(bf16[128,1280]{1,0:T(8,128)(2,1)S(1)} %constant_dynamic-update-slice_fusion.refs_2_.refs_5_), channel_id=1, source_target_pairs={{0,32},{16,48},{32,64},{48,80},{64,96},{80,112},{96,0},{112,16},{1... | collective-permute-start | bytes 983048 | tf_op jit(solution)/shard_map/ppermute | solution.py:675
  52.9 18.0 %collective-permute-start.4 = (bf16[128,1280]{1,0:T(8,128)(2,1)S(1)}, bf16[128,1280]{1,0:T(8,128)(2,1)S(1)}, u32[]{:S(2)}, u32[]{:S(2)}) collective-permute-start(bf16[128,1280]{1,0:T(8,128)(2,1)S(1)} %constant_dynamic-update-slice_fusion.refs_2_.refs_5_), channel_id=1, source_target_pairs={{0,64},{16,80},{32,96},{48,112},{64,0},{80,16},{96,32},{112,48},{1... | collective-permute-start | bytes 983048 | tf_op jit(solution)/shard_map/ppermute | solution.py:675
  55.3 15.9 %collective-permute-start.5 = (bf16[128,1280]{1,0:T(8,128)(2,1)S(1)}, bf16[128,1280]{1,0:T(8,128)(2,1)S(1)}, u32[]{:S(2)}, u32[]{:S(2)}) collective-permute-start(bf16[128,1280]{1,0:T(8,128)(2,1)S(1)} %constant_dynamic-update-slice_fusion.refs_2_.refs_5_), channel_id=1, source_target_pairs={{0,96},{16,112},{32,0},{48,16},{64,32},{80,48},{96,64},{112,80},{1... | collective-permute-start | bytes 983048 | tf_op jit(solution)/shard_map/ppermute | solution.py:675
  57.4 0.9 copy-start
  58.2 0.9 copy-start.1
  66.0 5.2 %copy-start.13 = (bf16[128,1280]{1,0:T(8,128)(2,1)}, bf16[128,1280]{1,0:T(8,128)(2,1)S(1)}, u32[]{:S(2)}) copy-start(bf16[128,1280]{1,0:T(8,128)(2,1)S(1)} %collective-permute-done.3.refs_3_.refs_6_) | copy-start | bytes 983044
  70.9 0.7 copy-start.14
  71.6 0.7 copy-start.15
  79.5 44.8 %all-to-all-start.1 = ((bf16[16,360,128]{2,1,0:T(8,128)(2,1)}), bf16[16,360,128]{2,1,0:T(8,128)(2,1)S(1)}, u32[]{:S(2)}, u32[]{:S(2)}) async-start(bf16[16,360,128]{2,1,0:T(8,128)(2,1)} %get-tuple-element.47), calls=%async_computation.1 | async-start | bytes 2949120 | tf_op jit(solution)/shard_map/all_to_all | solution.py:666
  86.8 17.6 %copy-start.4 = (bf16[768,128]{1,0:T(8,128)(2,1)S(1)}, bf16[768,128]{1,0:T(8,128)(2,1)}, u32[]{:S(2)}) copy-start(bf16[768,128]{1,0:T(8,128)(2,1)} %get-tuple-element.56.refs_6_) | copy-start | bytes 589828
  86.8 20.3 %copy-start.5 = (bf16[768,128]{1,0:T(8,128)(2,1)S(1)}, bf16[768,128]{1,0:T(8,128)(2,1)}, u32[]{:S(2)}) copy-start(bf16[768,128]{1,0:T(8,128)(2,1)} %get-tuple-element.57.refs_7_) | copy-start | bytes 589828
  100.9 21.9 %collective-permute-start.8 = (bf16[4,64,1280]{2,1,0:T(8,128)(2,1)S(1)}, bf16[4,64,1280]{2,1,0:T(8,128)(2,1)}, u32[]{:S(2)}, u32[]{:S(2)}) collective-permute-start(bf16[4,64,1280]{2,1,0:T(8,128)(2,1)S(1)} %dynamic-slice_bitcast_fusion), channel_id=1, source_target_pairs={{0,16},{16,0},{32,48},{48,32},{64,80},{80,64},{96,112},{112,96},{1... | collective-permute-start | bytes 1966088 | tf_op jit(solution)/shard_map/ppermute | solution.py:685
  104.4 7.1 %collective-permute-start.6 = (bf16[768,128]{1,0:T(8,128)(2,1)S(1)}, bf16[768,128]{1,0:T(8,128)(2,1)S(1)}, u32[]{:S(2)}, u32[]{:S(2)}) collective-permute-start(bf16[768,128]{1,0:T(8,128)(2,1)S(1)} %copy-done.4), channel_id=1, source_target_pairs={{1,0},{2,1},{3,2},{4,3},{5,4},{6,5},{7,6},{8,7},{9,8},{10,9},{11,1... | collective-permute-start | bytes 589832 | tf_op jit(solution)/shard_map/ppermute | solution.py:614
  107.1 8.7 %collective-permute-start.7 = (bf16[768,128]{1,0:T(8,128)(2,1)S(1)}, bf16[768,128]{1,0:T(8,128)(2,1)S(1)}, u32[]{:S(2)}, u32[]{:S(2)}) collective-permute-start(bf16[768,128]{1,0:T(8,128)(2,1)S(1)} %copy-done.5), channel_id=1, source_target_pairs={{0,1},{1,2},{2,3},{3,4},{4,5},{5,6},{6,7},{7,8},{8,9},{9,10},{10,1... | collective-permute-start | bytes 589832 | tf_op jit(solution)/shard_map/ppermute | solution.py:613
  111.5 4.3 %copy-start.6 = (bf16[768,128]{1,0:T(8,128)(2,1)}, bf16[768,128]{1,0:T(8,128)(2,1)S(1)}, u32[]{:S(2)}) copy-start(bf16[768,128]{1,0:T(8,128)(2,1)S(1)} %collective-permute-done.6.refs_8_) | copy-start | bytes 589828
  115.8 0.7 copy-start.7
  124.3 1.1 copy-start.2
  125.4 32.5 %all-to-all-start.3 = ((bf16[16,360,128]{2,1,0:T(8,128)(2,1)}), bf16[16,360,128]{2,1,0:T(8,128)(2,1)}, u32[]{:S(2)}, u32[]{:S(2)}) async-start(bf16[16,360,128]{2,1,0:T(8,128)(2,1)} %get-tuple-element.60), calls=%async_computation.3 | async-start | bytes 2949120 | tf_op jit(solution)/shard_map/all_to_all | solution.py:666
  133.5 23.0 %collective-permute-start.10 = (bf16[64,1280]{1,0:T(8,128)(2,1)S(1)}, bf16[64,1280]{1,0:T(8,128)(2,1)S(1)}, u32[]{:S(2)}, u32[]{:S(2)}) collective-permute-start(bf16[64,1280]{1,0:T(8,128)(2,1)S(1)} %get-tuple-element.67), channel_id=1, source_target_pairs={{0,64},{16,80},{32,96},{48,112},{64,0},{80,16},{96,32},{112,48},{1... | collective-permute-start | bytes 491528 | tf_op jit(solution)/shard_map/ppermute | solution.py:694
  134.4 22.1 %collective-permute-start.11 = (bf16[64,1280]{1,0:T(8,128)(2,1)S(1)}, bf16[64,1280]{1,0:T(8,128)(2,1)S(1)}, u32[]{:S(2)}, u32[]{:S(2)}) collective-permute-start(bf16[64,1280]{1,0:T(8,128)(2,1)S(1)} %get-tuple-element.66), channel_id=1, source_target_pairs={{0,96},{16,112},{32,0},{48,16},{64,32},{80,48},{96,64},{112,80},{1... | collective-permute-start | bytes 491528 | tf_op jit(solution)/shard_map/ppermute | solution.py:694
  134.4 22.0 %collective-permute-start.9 = (bf16[64,1280]{1,0:T(8,128)(2,1)S(1)}, bf16[64,1280]{1,0:T(8,128)(2,1)S(1)}, u32[]{:S(2)}, u32[]{:S(2)}) collective-permute-start(bf16[64,1280]{1,0:T(8,128)(2,1)S(1)} %get-tuple-element.65), channel_id=1, source_target_pairs={{0,32},{16,48},{32,64},{48,80},{64,96},{80,112},{96,0},{112,16},{1... | collective-permute-start | bytes 491528 | tf_op jit(solution)/shard_map/ppermute | solution.py:694
